TPU v7x, 32 devices: a whole 2x2x4 slice. The times are simulated.
32 devices in a mesh: dp: 8 (over y, x, core), expert: 4 (over z).
Axes of the slice: x: 2, y: 2, z: 4, core: 2. Of those that a mesh axis runs over, the one named last changes fastest.
Arguments:
- tokens: bfloat16 [8192, 1536], P(('dp', 'expert')), may hold values from -6 to 6
- attn_gain: bfloat16 [1536], P('dp'), may hold values from 0.5 to 1.5
- q_weight: bfloat16 [1536, 1536], P('dp'), may hold values from -0.15625 to 0.15625
- key_matrix: bfloat16 [1536, 512], P('dp'), may hold values from -0.15625 to 0.15625
- value_matrix: bfloat16 [1536, 512], P('dp'), may hold values from -0.15625 to 0.15625
- o_weight: bfloat16 [1536, 1536], P('dp'), may hold values from -0.75 to 0.75
- ffn_gain: bfloat16 [1536], P('dp'), may hold values from 0.5 to 1.5
- router_weight: bfloat16 [1536, 20], P('dp'), may hold values from -0.078125 to 0.078125
- expert_gate: bfloat16 [20, 1536, 512], P('expert', 'dp'), may hold values from -0.15625 to 0.15625
- expert_up: bfloat16 [20, 1536, 512], P('expert', 'dp'), may hold values from -0.15625 to 0.15625
- expert_down: bfloat16 [20, 512, 1536], P('expert', 'dp'), may hold values from -1 to 1
- routes: int32 [8192, 8], P(('dp', 'expert')), may hold values from 0 to 19, all different within a row; in each aligned block of 256 rows (0 to 255, 256 to 511, ...) at most 128 rows name the same one
- starts: int32 [8, 2], P('dp'), may hold values from 0 to 768, as said below
- cotangent: bfloat16 [8192, 1536], P(('dp', 'expert')), may hold values from -6 to 6
Outputs:
- output: bfloat16 [8192, 1536], P(('dp', 'expert'))
- input_grad: bfloat16 [8192, 1536], P(('dp', 'expert'))
- attn_gain_grad: float32 [1536], P('dp')
- q_grad: float32 [1536, 1536], P('dp')
- k_grad: float32 [1536, 512], P('dp')
- v_grad: float32 [1536, 512], P('dp')
- o_grad: float32 [1536, 1536], P('dp')
- ffn_gain_grad: float32 [1536], P('dp')
- router_grad: float32 [1536, 20], P('dp')
- gate_grad: float32 [20, 1536, 512], P('expert', 'dp')
- up_grad: float32 [20, 1536, 512], P('expert', 'dp')
- down_grad: float32 [20, 512, 1536], P('expert', 'dp')
Inputs may be any that keep to these rules, and one draw needn't show every extreme that they name: `routes`: among the 256 tokens of one device no expert is named by more than 128 tokens, and in every draw some device has an expert named by exactly 128. `starts`: piece k of a sequence lies within positions k * 512 to (k + 1) * 512 - 1.
All inputs are finite; a program needn't handle non-finite values.
Results may differ from a plain program's by a relative error of at most 0.025.
Values may be sent and summed in bfloat16 or wider, within the bound.
A program may use at most 256 MiB of HBM per device.

v0:
```python
import jax
import jax.numpy as jnp
from jax import lax
from jax.sharding import PartitionSpec as P

MODEL_WIDTH = 1536
QUERY_HEADS = 24
KEY_VALUE_HEADS = 8
HEAD_SIZE = 64
TOPK = 8
PIECE_LEN = 256


EPSILON = 1e-05
THETA = 10000.0


def rms_parts(value_rows, gain):
    inverse = lax.rsqrt(jnp.mean(value_rows * value_rows, axis=-1, keepdims=True) + EPSILON)
    return (value_rows * inverse * gain, inverse)


def rms_back(grad_norm, value_rows, inverse, gain):
    scaled = grad_norm * gain
    grad_gain = jnp.sum(grad_norm * value_rows * inverse, axis=0)
    grad_values = inverse * scaled - value_rows * inverse**3 * jnp.mean(
        scaled * value_rows, axis=-1, keepdims=True
    )
    return (grad_values, grad_gain)


def inner_product(left, right):
    return jnp.dot(left, right, preferred_element_type=jnp.float32)


def contract(left, right):
    return jnp.einsum("ta,tb->ab", left, right, preferred_element_type=jnp.float32)


def compared_with(left, right):
    return jnp.einsum("tb,ab->ta", left, right, preferred_element_type=jnp.float32)


def rotary_tables(positions):
    half_size = HEAD_SIZE // 2
    freqs = THETA ** (-(jnp.arange(half_size, dtype=jnp.float32) * 2.0 / HEAD_SIZE))
    angles = positions.astype(jnp.float32)[:, None] * freqs[None, :]
    return (jnp.cos(angles)[:, None, :], jnp.sin(angles)[:, None, :])


def rotate_halves_fn(value_rows, cosine_table, sine_values):
    half_size = value_rows.shape[-1] // 2
    first = value_rows[..., :half_size]
    second = value_rows[..., half_size:]
    return jnp.concatenate(
        [first * cosine_table - second * sine_values, second * cosine_table + first * sine_values],
        axis=-1,
    )


def piece_index(positions, starts_row):
    inside = (positions[:, None] >= starts_row[None, :]) & (
        positions[:, None] < starts_row[None, :] + PIECE_LEN
    )
    labels = jnp.arange(1, starts_row.shape[0] + 1, dtype=jnp.int32)[None, :]
    return jnp.sum(jnp.where(inside, labels, 0), axis=-1)


def visible(query_pos, query_piece, key_pos, key_piece):
    causal = key_pos[None, :] <= query_pos[:, None]
    shared = (query_piece[:, None] == key_piece[None, :]) & (query_piece[:, None] > 0)
    return causal | shared


def softmax_rows(scores):
    powers = jnp.exp(scores - jnp.max(scores, axis=-1, keepdims=True))
    return powers / jnp.sum(powers, axis=-1, keepdims=True)


def slot_table(route_rows, expert_total, capacity):
    flat_routes = route_rows.reshape(-1)
    picked = (flat_routes[:, None] == jnp.arange(expert_total, dtype=jnp.int32)[None, :]).astype(
        jnp.int32
    )
    ranks = jnp.sum(jnp.cumsum(picked, axis=0) * picked, axis=-1) - 1
    return flat_routes * capacity + ranks


def per_device(
    tokens,
    attn_gain,
    q_weight,
    key_matrix,
    value_matrix,
    o_weight,
    ffn_gain,
    router_weight,
    expert_gate,
    expert_up,
    expert_down,
    routes,
    starts,
    cotangent,
):
    groups = lax.axis_size("expert")
    member = lax.axis_index("expert")
    row_total = tokens.shape[0]
    sequence_length = row_total * groups
    query_per_key = QUERY_HEADS // KEY_VALUE_HEADS
    score_scale = HEAD_SIZE ** (-0.5)
    local_experts = expert_gate.shape[0]
    expert_total = local_experts * groups
    capacity = row_total * TOPK * 5 // (4 * expert_total)
    gain_one, w_query, key_weight, value_weight, output_weight, gain_two, w_router = (
        lax.all_gather(attn_gain, "dp", axis=0, tiled=True),
        lax.all_gather(q_weight, "dp", axis=0, tiled=True),
        lax.all_gather(key_matrix, "dp", axis=0, tiled=True),
        lax.all_gather(value_matrix, "dp", axis=0, tiled=True),
        lax.all_gather(o_weight, "dp", axis=0, tiled=True),
        lax.all_gather(ffn_gain, "dp", axis=0, tiled=True),
        lax.all_gather(router_weight, "dp", axis=0, tiled=True),
    )
    full_gate, full_up, full_down = (
        lax.all_gather(expert_gate, "dp", axis=1, tiled=True),
        lax.all_gather(expert_up, "dp", axis=1, tiled=True),
        lax.all_gather(expert_down, "dp", axis=1, tiled=True),
    )
    gain_one = gain_one.astype(jnp.float32)
    gain_two = gain_two.astype(jnp.float32)
    inputs = tokens.astype(jnp.float32)
    normed, inverse_one = rms_parts(inputs, gain_one)
    first_norm = normed.astype(jnp.bfloat16)
    query_pos = member * row_total + jnp.arange(row_total, dtype=jnp.int32)
    cosine_table, sine_values = rotary_tables(query_pos)
    query_rows = rotate_halves_fn(
        inner_product(first_norm, w_query).reshape(row_total, QUERY_HEADS, HEAD_SIZE),
        cosine_table,
        sine_values,
    )
    query_rows = query_rows.astype(jnp.bfloat16).reshape(
        row_total, KEY_VALUE_HEADS, query_per_key, HEAD_SIZE
    )
    rotated_keys = rotate_halves_fn(
        inner_product(first_norm, key_weight).reshape(row_total, KEY_VALUE_HEADS, HEAD_SIZE),
        cosine_table,
        sine_values,
    )
    rotated_keys = rotated_keys.astype(jnp.bfloat16).reshape(row_total, KEY_VALUE_HEADS * HEAD_SIZE)
    values_local = inner_product(first_norm, value_weight).astype(jnp.bfloat16)
    every_key, every_value = (
        lax.all_gather(rotated_keys, "expert", axis=0, tiled=True),
        lax.all_gather(values_local, "expert", axis=0, tiled=True),
    )
    block_span = min(512, sequence_length)
    block_total = sequence_length // block_span
    key_pos = jnp.arange(sequence_length, dtype=jnp.int32)
    starts_row = starts[0]
    query_piece = piece_index(query_pos, starts_row)
    key_piece = piece_index(key_pos, starts_row)
    block_group = (
        every_key.reshape(block_total, block_span, KEY_VALUE_HEADS, HEAD_SIZE),
        every_value.reshape(block_total, block_span, KEY_VALUE_HEADS, HEAD_SIZE),
        key_pos.reshape(block_total, block_span),
        key_piece.reshape(block_total, block_span),
    )

    def scores_of(key_block, pos_block, piece_block):
        raw_scores = jnp.einsum(
            "qgrd,kgd->grqk", query_rows, key_block, preferred_element_type=jnp.float32
        )
        allowed = visible(query_pos, query_piece, pos_block, piece_block)
        return (raw_scores * score_scale, allowed)

    def attend(carried, block_items):
        running_max, running_sum, accumulated = carried
        key_block, value_block, pos_block, piece_block = block_items
        scores, allowed = scores_of(key_block, pos_block, piece_block)
        scores = jnp.where(allowed, scores, -1e30)
        new_max = jnp.maximum(running_max, jnp.max(scores, axis=-1))
        weight = jnp.where(allowed, jnp.exp(scores - new_max[..., None]), 0.0)
        rescale = jnp.exp(running_max - new_max)
        running_sum = running_sum * rescale + jnp.sum(weight, axis=-1)
        accumulated = accumulated * rescale[..., None] + jnp.einsum(
            "grqk,kgd->grqd",
            weight.astype(jnp.bfloat16),
            value_block,
            preferred_element_type=jnp.float32,
        )
        return ((new_max, running_sum, accumulated), None)

    initial = (
        jnp.full((KEY_VALUE_HEADS, query_per_key, row_total), -1e30, jnp.float32),
        jnp.zeros((KEY_VALUE_HEADS, query_per_key, row_total), jnp.float32),
        jnp.zeros((KEY_VALUE_HEADS, query_per_key, row_total, HEAD_SIZE), jnp.float32),
    )
    (running_max, running_sum, accumulated), unused = lax.scan(attend, initial, block_group)
    attn_out = accumulated / running_sum[..., None]
    log_total = running_max + jnp.log(running_sum)
    attended = (
        attn_out.transpose(2, 0, 1, 3)
        .reshape(row_total, QUERY_HEADS * HEAD_SIZE)
        .astype(jnp.bfloat16)
    )
    hidden = inputs + inner_product(attended, output_weight)
    normed_two, inverse_two = rms_parts(hidden, gain_two)
    norm_two = normed_two.astype(jnp.bfloat16)
    logits = inner_product(norm_two, w_router)
    picked = (
        routes[:, :, None] == jnp.arange(expert_total, dtype=jnp.int32)[None, None, :]
    ).astype(jnp.float32)
    gates = softmax_rows(jnp.sum(picked * logits[:, None, :], axis=-1))
    slots = slot_table(routes, expert_total, capacity)
    pair_total = row_total * TOPK
    source_of = (
        jnp.zeros((expert_total * capacity,), jnp.int32)
        .at[slots]
        .set(jnp.arange(1, pair_total + 1, dtype=jnp.int32))
    )
    filled = (source_of > 0)[:, None]
    pair_index = jnp.maximum(source_of - 1, 0)
    buffer = jnp.where(filled, norm_two[pair_index // TOPK], jnp.zeros((), jnp.bfloat16))
    buffer = buffer.reshape(groups, local_experts, capacity, MODEL_WIDTH)
    received = lax.all_to_all(buffer, "expert", split_axis=0, concat_axis=0, tiled=True)
    gate_part = jnp.einsum(
        "pecd,edf->pecf", received, full_gate, preferred_element_type=jnp.float32
    )
    up_part = jnp.einsum("pecd,edf->pecf", received, full_up, preferred_element_type=jnp.float32)
    active = (gate_part * jax.nn.sigmoid(gate_part) * up_part).astype(jnp.bfloat16)
    result = jnp.einsum(
        "pecf,efd->pecd", active, full_down, preferred_element_type=jnp.float32
    ).astype(jnp.bfloat16)
    returned = lax.all_to_all(result, "expert", split_axis=0, concat_axis=0, tiled=True)
    pair_values = returned.reshape(expert_total * capacity, MODEL_WIDTH)[slots].reshape(
        row_total, TOPK, MODEL_WIDTH
    )
    mixture = jnp.einsum("tk,tkd->td", gates, pair_values.astype(jnp.float32))
    output = (hidden + mixture).astype(jnp.bfloat16)
    grad_out = cotangent.astype(jnp.float32)
    grad_gates = jnp.einsum("td,tkd->tk", grad_out, pair_values.astype(jnp.float32))
    grad_pairs = (
        (gates[:, :, None] * grad_out[:, None, :])
        .astype(jnp.bfloat16)
        .reshape(pair_total, MODEL_WIDTH)
    )
    grad_buffer = jnp.where(filled, grad_pairs[pair_index], jnp.zeros((), jnp.bfloat16))
    grad_received = lax.all_to_all(
        grad_buffer.reshape(groups, local_experts, capacity, MODEL_WIDTH),
        "expert",
        split_axis=0,
        concat_axis=0,
        tiled=True,
    )
    back_gate, back_up, back_down = (full_gate, full_up, full_down)
    gate_part = jnp.einsum(
        "pecd,edf->pecf", received, back_gate, preferred_element_type=jnp.float32
    )
    up_part = jnp.einsum("pecd,edf->pecf", received, back_up, preferred_element_type=jnp.float32)
    sigma = jax.nn.sigmoid(gate_part)
    active = (gate_part * sigma * up_part).astype(jnp.bfloat16)
    grad_active = jnp.einsum(
        "pecd,efd->pecf", grad_received, back_down, preferred_element_type=jnp.float32
    )
    grad_down = jnp.einsum(
        "pecf,pecd->efd", active, grad_received, preferred_element_type=jnp.float32
    )
    grad_gate_part = (grad_active * up_part * sigma * (1.0 + gate_part * (1.0 - sigma))).astype(
        jnp.bfloat16
    )
    grad_up_part = (grad_active * gate_part * sigma).astype(jnp.bfloat16)
    grad_gate_w = jnp.einsum(
        "pecd,pecf->edf", received, grad_gate_part, preferred_element_type=jnp.float32
    )
    grad_up_w = jnp.einsum(
        "pecd,pecf->edf", received, grad_up_part, preferred_element_type=jnp.float32
    )
    grad_rows = (
        jnp.einsum("pecf,edf->pecd", grad_gate_part, back_gate, preferred_element_type=jnp.float32)
        + jnp.einsum("pecf,edf->pecd", grad_up_part, back_up, preferred_element_type=jnp.float32)
    ).astype(jnp.bfloat16)
    grad_back = lax.all_to_all(grad_rows, "expert", split_axis=0, concat_axis=0, tiled=True)
    gate_grad, up_grad, down_grad = (
        lax.psum_scatter(
            grad_gate_w.astype(jnp.bfloat16), "dp", scatter_dimension=1, tiled=True
        ).astype(jnp.float32),
        lax.psum_scatter(
            grad_up_w.astype(jnp.bfloat16), "dp", scatter_dimension=1, tiled=True
        ).astype(jnp.float32),
        lax.psum_scatter(
            grad_down.astype(jnp.bfloat16), "dp", scatter_dimension=1, tiled=True
        ).astype(jnp.float32),
    )
    grad_pair_rows = grad_back.reshape(expert_total * capacity, MODEL_WIDTH)[slots].reshape(
        row_total, TOPK, MODEL_WIDTH
    )
    grad_norm_two = jnp.sum(grad_pair_rows.astype(jnp.float32), axis=1)
    grad_chosen = gates * (grad_gates - jnp.sum(gates * grad_gates, axis=-1, keepdims=True))
    grad_logits = jnp.sum(picked * grad_chosen[:, :, None], axis=1).astype(jnp.bfloat16)
    grad_router = contract(norm_two, grad_logits)
    grad_norm_two = grad_norm_two + compared_with(grad_logits, w_router)
    grad_hidden_norm, grad_gain_two = rms_back(grad_norm_two, hidden, inverse_two, gain_two)
    grad_hidden = grad_out + grad_hidden_norm
    projection_gradient = grad_hidden.astype(jnp.bfloat16)
    grad_out_w = contract(attended, projection_gradient)
    grad_att = (
        compared_with(projection_gradient, output_weight)
        .astype(jnp.bfloat16)
        .reshape(row_total, KEY_VALUE_HEADS, query_per_key, HEAD_SIZE)
    )
    delta = jnp.einsum("qgrd,grqd->grq", grad_att.astype(jnp.float32), attn_out)

    def attention_backward(grad_query, block_items):
        key_block, value_block, pos_block, piece_block = block_items
        scores, allowed = scores_of(key_block, pos_block, piece_block)
        probs = jnp.where(allowed, jnp.exp(scores - log_total[..., None]), 0.0)
        grad_probs = jnp.einsum(
            "qgrd,kgd->grqk", grad_att, value_block, preferred_element_type=jnp.float32
        )
        grad_raw = (probs * (grad_probs - delta[..., None]) * score_scale).astype(jnp.bfloat16)
        grad_query = grad_query + jnp.einsum(
            "grqk,kgd->qgrd", grad_raw, key_block, preferred_element_type=jnp.float32
        )
        grad_key = jnp.einsum(
            "grqk,qgrd->kgd", grad_raw, query_rows, preferred_element_type=jnp.float32
        )
        grad_value = jnp.einsum(
            "grqk,qgrd->kgd",
            probs.astype(jnp.bfloat16),
            grad_att,
            preferred_element_type=jnp.float32,
        )
        return (grad_query, (grad_key, grad_value))

    grad_query, (key_factors, value_factors) = lax.scan(
        attention_backward,
        jnp.zeros((row_total, KEY_VALUE_HEADS, query_per_key, HEAD_SIZE), jnp.float32),
        block_group,
    )
    key_gradient, grad_values = (
        lax.psum_scatter(
            key_factors.reshape(sequence_length, KEY_VALUE_HEADS * HEAD_SIZE).astype(jnp.bfloat16),
            "expert",
            scatter_dimension=0,
            tiled=True,
        ).astype(jnp.float32),
        lax.psum_scatter(
            value_factors.reshape(sequence_length, KEY_VALUE_HEADS * HEAD_SIZE).astype(
                jnp.bfloat16
            ),
            "expert",
            scatter_dimension=0,
            tiled=True,
        ).astype(jnp.float32),
    )
    grad_query_b = (
        rotate_halves_fn(
            grad_query.reshape(row_total, QUERY_HEADS, HEAD_SIZE), cosine_table, -sine_values
        )
        .astype(jnp.bfloat16)
        .reshape(row_total, QUERY_HEADS * HEAD_SIZE)
    )
    grad_key_b = (
        rotate_halves_fn(
            key_gradient.reshape(row_total, KEY_VALUE_HEADS, HEAD_SIZE), cosine_table, -sine_values
        )
        .astype(jnp.bfloat16)
        .reshape(row_total, KEY_VALUE_HEADS * HEAD_SIZE)
    )
    grad_value_b = grad_values.astype(jnp.bfloat16)
    grad_norm_one = (
        compared_with(grad_query_b, w_query)
        + compared_with(grad_key_b, key_weight)
        + compared_with(grad_value_b, value_weight)
    )
    grad_query_w = contract(first_norm, grad_query_b)
    grad_key_w = contract(first_norm, grad_key_b)
    grad_value_w = contract(first_norm, grad_value_b)
    grad_inputs_norm, grad_gain_one = rms_back(grad_norm_one, inputs, inverse_one, gain_one)
    input_grad = (grad_hidden + grad_inputs_norm).astype(jnp.bfloat16)
    shares = (
        lax.psum_scatter(
            grad_gain_one.astype(jnp.bfloat16), "dp", scatter_dimension=0, tiled=True
        ).astype(jnp.float32),
        lax.psum_scatter(
            grad_query_w.astype(jnp.bfloat16), "dp", scatter_dimension=0, tiled=True
        ).astype(jnp.float32),
        lax.psum_scatter(
            grad_key_w.astype(jnp.bfloat16), "dp", scatter_dimension=0, tiled=True
        ).astype(jnp.float32),
        lax.psum_scatter(
            grad_value_w.astype(jnp.bfloat16), "dp", scatter_dimension=0, tiled=True
        ).astype(jnp.float32),
        lax.psum_scatter(
            grad_out_w.astype(jnp.bfloat16), "dp", scatter_dimension=0, tiled=True
        ).astype(jnp.float32),
        lax.psum_scatter(
            grad_gain_two.astype(jnp.bfloat16), "dp", scatter_dimension=0, tiled=True
        ).astype(jnp.float32),
        lax.psum_scatter(
            grad_router.astype(jnp.bfloat16), "dp", scatter_dimension=0, tiled=True
        ).astype(jnp.float32),
    )
    attn_gain_grad, q_grad, k_grad, v_grad, o_grad, ffn_gain_grad, router_grad = (
        lax.psum(shares[0].astype(jnp.bfloat16), "expert").astype(jnp.float32),
        lax.psum(shares[1].astype(jnp.bfloat16), "expert").astype(jnp.float32),
        lax.psum(shares[2].astype(jnp.bfloat16), "expert").astype(jnp.float32),
        lax.psum(shares[3].astype(jnp.bfloat16), "expert").astype(jnp.float32),
        lax.psum(shares[4].astype(jnp.bfloat16), "expert").astype(jnp.float32),
        lax.psum(shares[5].astype(jnp.bfloat16), "expert").astype(jnp.float32),
        lax.psum(shares[6].astype(jnp.bfloat16), "expert").astype(jnp.float32),
    )
    return (
        output,
        input_grad,
        attn_gain_grad,
        q_grad,
        k_grad,
        v_grad,
        o_grad,
        ffn_gain_grad,
        router_grad,
        gate_grad,
        up_grad,
        down_grad,
    )


def solution(mesh):
    placed = (
        P(("dp", "expert"), None),
        P("dp"),
        P("dp", None),
        P("dp", None),
        P("dp", None),
        P("dp", None),
        P("dp"),
        P("dp", None),
        P("expert", "dp", None),
        P("expert", "dp", None),
        P("expert", "dp", None),
        P(("dp", "expert"), None),
        P("dp", None),
        P(("dp", "expert"), None),
    )
    return jax.shard_map(
        per_device,
        mesh=mesh,
        in_specs=placed,
        out_specs=(
            P(("dp", "expert"), None),
            P(("dp", "expert"), None),
            P("dp"),
            P("dp", None),
            P("dp", None),
            P("dp", None),
            P("dp", None),
            P("dp"),
            P("dp", None),
            P("expert", "dp", None),
            P("expert", "dp", None),
            P("expert", "dp", None),
        ),
        check_vma=False,
    )
```

profile of v0, /device:TPU:0, one launch (start us, length us, event | category | flops | bytes accessed | tf_op | source)
XLA Modules:
  0.0 1784.8 jit_solution(5276867636887240389)
XLA Ops:
  12.5 15.4 all-reduce.5
  41.8 24.3 %all-gather.17.cloned.1.call-done = bf16[1536,512]{1,0:T(8,128)(2,1)} async-done(((bf16[192,512]{1,0:T(8,128)(2,1)}), bf16[1536,512]{1,0:T(8,128)(2,1)}) %all-gather.17.cloned.1.call-update) | async-done | bytes 1572880 | tf_op jit(solution)/shard_map/all_gather | solution.py:118
  102.5 24.2 %all-gather.19.cloned.1.call-done = bf16[1024,512]{1,0:T(8,128)(2,1)} async-done(((bf16[256,512]{1,0:T(8,128)(2,1)}), bf16[1024,512]{1,0:T(8,128)(2,1)}) %all-gather.19.cloned.1.call-update) | async-done | bytes 1048592 | tf_op jit(solution)/shard_map/all_gather | solution.py:152
  133.9 32.9 %all-gather.15.cloned.1.call-done = bf16[1536,1536]{1,0:T(8,128)(2,1)} async-done(((bf16[192,1536]{1,0:T(8,128)(2,1)}), bf16[1536,1536]{1,0:T(8,128)(2,1)}) %all-gather.15.cloned.1.call-update) | async-done | bytes 4718608 | tf_op jit(solution)/shard_map/all_gather | solution.py:116
  171.6 41.6 %while.30 = (s32[]{:T(128)}, f32[8,3,256]{2,1,0:T(4,128)S(1)}, f32[8,3,256]{2,1,0:T(4,128)S(1)}, f32[8,3,256,64]{2,3,1,0:T(8,128)}, s32[2,512]{1,0:T(2,128)S(1)}...) while((s32[]{:T(128)}, f32[8,3,256]{2,1,0:T(4,128)S(1)}, ...), condition=%wide.region_6.7_spmd.clone, body=%wide.region_3.6_spmd.clone.sunk | while | flops 847936000 | bytes 93996208 | solution.py:196
  245.5 16.1 all-gather.23.cloned.1.call-done
  261.7 155.7 %all-to-all-done = bf16[4,5,128,1536]{3,2,1,0:T(8,128)(2,1)} async-done(((bf16[4,5,128,1536]{3,2,1,0:T(8,128)(2,1)}), bf16[4,5,128,1536]{3,2,1,0:T(8,128)(2,1)}, u32[]{:S(2)}, u32[]{:S(2)}) %all-to-all-start) | async-done | bytes 7864352 | tf_op jit(solution)/shard_map/all_to_all | solution.py:223
  417.4 12.1 fusion.60
  429.4 13.9 fusion.83
  476.7 161.8 %all-to-all-done.1 = bf16[4,5,128,1536]{3,2,1,0:T(8,128)(2,1)} async-done(((bf16[4,5,128,1536]{3,2,1,0:T(8,128)(2,1)}), bf16[4,5,128,1536]{3,2,1,0:T(8,128)(2,1)}, u32[]{:S(2)}, u32[]{:S(2)}) %all-to-all-start.1) | async-done | bytes 7864352 | tf_op jit(solution)/shard_map/all_to_all | solution.py:232
  638.5 17.6 gather_fusion.1
  666.6 20.0 %gather_fusion.2 = bf16[2560,1536]{1,0:T(8,128)(2,1)} fusion(bf16[2048,1536]{1,0:T(8,128)(2,1)} %fusion.52, s32[3072]{0:T(1024)S(1)} %copy-done.44), kind=kCustom, calls=%fused_computation.2 | custom fusion | bytes 15738880 | tf_op jit(solution)/shard_map/gather | solution.py:245
  690.5 175.4 %all_to_all.20 = bf16[4,5,128,1536]{3,2,1,0:T(8,128)(2,1)} all-to-all(bf16[4,5,128,1536]{3,2,1,0:T(8,128)(2,1)S(1)} %broadcast_select_fusion), channel_id=1, replica_groups=mesh['dp'=8,'expert'=4] {'expert'}, dimensions={0} | all-to-all | bytes 15728640 | tf_op jit(solution)/shard_map/all_to_all | solution.py:246
  865.9 12.3 fusion.80
  878.2 14.7 fusion.54
  892.9 11.9 fusion.53
  923.1 165.4 %all-to-all-done.3 = bf16[4,5,128,1536]{3,2,1,0:T(8,128)(2,1)} async-done(((bf16[4,5,128,1536]{3,2,1,0:T(8,128)(2,1)}), bf16[4,5,128,1536]{3,2,1,0:T(8,128)(2,1)}, u32[]{:S(2)}, u32[]{:S(2)}) %all-to-all-start.3) | async-done | bytes 7864352 | tf_op jit(solution)/shard_map/all_to_all | solution.py:280
  1088.4 17.8 gather_fusion.3
  1122.0 62.3 %while.31 = (s32[]{:T(128)}, f32[256,8,3,64]{0,3,2,1:T(8,128)}, bf16[2,512,8,64]{1,3,2,0:T(8,128)(2,1)}, bf16[2,512,8,64]{1,3,2,0:T(8,128)(2,1)}, bf16[2,512,8,6...) while((s32[]{:T(128)}, f32[256,8,3,64]{0,3,2,1:T(8,128)}, ...), condition=%wide.region_20.21_spmd.clone, body=%wide.region_19.20_spmd.clone.sunk | while | flops 2049180160 | bytes 167749872 | solution.py:333
  1191.9 21.7 %reduce-scatter.13.cloned.1.call-done = bf16[256,512]{0,1:T(8,128)(2,1)} async-done(((bf16[1024,512]{0,1:T(8,128)(2,1)}), bf16[256,512]{0,1:T(8,128)(2,1)}) %reduce-scatter.13.cloned.1.call-update) | async-done | bytes 262160 | tf_op jit(solution)/shard_map/reduce_scatter | solution.py:339
  1216.6 25.7 %reduce-scatter.15.cloned.1.call-done = bf16[256,512]{0,1:T(8,128)(2,1)} async-done(((bf16[1024,512]{0,1:T(8,128)(2,1)}), bf16[256,512]{0,1:T(8,128)(2,1)}) %reduce-scatter.15.cloned.1.call-update) | async-done | bytes 262160 | tf_op jit(solution)/shard_map/reduce_scatter | solution.py:345
  1278.7 11.4 bitcast_convert_fusion.1
  1291.8 29.0 %reduce-scatter.19.cloned.1.call-done = bf16[192,512]{1,0:T(8,128)(2,1)} async-done(((bf16[1536,512]{1,0:T(8,128)(2,1)}), bf16[192,512]{1,0:T(8,128)(2,1)}) %reduce-scatter.19.cloned.1.call-update) | async-done | bytes 196624 | tf_op jit(solution)/shard_map/reduce_scatter | solution.py:386
  1320.7 42.2 %reduce-scatter.21.cloned.1.call-done = bf16[192,512]{1,0:T(8,128)(2,1)} async-done(((bf16[1536,512]{1,0:T(8,128)(2,1)}), bf16[192,512]{1,0:T(8,128)(2,1)}) %reduce-scatter.21.cloned.1.call-update) | async-done | bytes 196624 | tf_op jit(solution)/shard_map/reduce_scatter | solution.py:389
  1362.9 57.2 %reduce-scatter.23.cloned.1.call-done = bf16[192,1536]{1,0:T(8,128)(2,1)} async-done(((bf16[1536,1536]{1,0:T(8,128)(2,1)}), bf16[192,1536]{1,0:T(8,128)(2,1)}) %reduce-scatter.23.cloned.1.call-update) | async-done | bytes 589840 | tf_op jit(solution)/shard_map/reduce_scatter | solution.py:392
  1420.1 57.6 %reduce-scatter.17.cloned.1.call-done = bf16[192,1536]{1,0:T(8,128)(2,1)} async-done(((bf16[1536,1536]{1,0:T(8,128)(2,1)}), bf16[192,1536]{1,0:T(8,128)(2,1)}) %reduce-scatter.17.cloned.1.call-update) | async-done | bytes 589840 | tf_op jit(solution)/shard_map/reduce_scatter | solution.py:383
  1482.7 67.8 %reduce-scatter.29.cloned.1.call-done = bf16[5,64,1536]{2,1,0:T(8,128)(2,1)} async-done(((bf16[5,512,1536]{2,1,0:T(8,128)(2,1)}), bf16[5,64,1536]{2,1,0:T(8,128)(2,1)}) %reduce-scatter.29.cloned.1.call-update) | async-done | bytes 983056 | tf_op jit(solution)/shard_map/reduce_scatter | solution.py:288
  1553.2 70.4 %reduce-scatter.25.cloned.1.call-done = bf16[5,192,512]{2,1,0:T(8,128)(2,1)} async-done(((bf16[5,1536,512]{2,1,0:T(8,128)(2,1)}), bf16[5,192,512]{2,1,0:T(8,128)(2,1)}) %reduce-scatter.25.cloned.1.call-update) | async-done | bytes 983056 | tf_op jit(solution)/shard_map/reduce_scatter | solution.py:282
  1626.3 70.2 %reduce-scatter.27.cloned.1.call-done = bf16[5,192,512]{2,1,0:T(8,128)(2,1)} async-done(((bf16[5,1536,512]{2,1,0:T(8,128)(2,1)}), bf16[5,192,512]{2,1,0:T(8,128)(2,1)}) %reduce-scatter.27.cloned.1.call-update) | async-done | bytes 983056 | tf_op jit(solution)/shard_map/reduce_scatter | solution.py:285
  1705.3 13.7 all-reduce.4
  1719.2 19.5 %all-reduce.6 = (bf16[192]{0:T(256)(128)(2,1)S(1)}, bf16[192]{0:T(256)(128)(2,1)S(1)}, bf16[192,20]{0,1:T(8,128)(2,1)S(1)}) all-reduce(bf16[192]{0:T(256)(128)(2,1)S(1)} %dynamic-slice.3, bf16[192]{0:T(256)(128)(2,1)S(1)} %dynamic-slice.5, bf16[192,20]{0,1:T(8,128)(2,1)S(1)} %copy.167), channel_id=1, replica_groups=mesh['dp'=8,'expert'=4] {'expert'}, use_global_device_ids=true, to_apply=%region_26.27 | all-reduce | flops 4224 | bytes 16896 | tf_op jit(solution)/shard_map/psum | solution.py:403
  1743.3 26.6 %all-reduce.10.cloned.1.call-done = (bf16[192,1536]{1,0:T(8,128)(2,1)}, bf16[192,512]{1,0:T(8,128)(2,1)}, bf16[192,512]{1,0:T(8,128)(2,1)}, bf16[192,1536]{1,0:T(8,128)(2,1)}) async-done(((bf16[192,1536]{1,0:T(8,128)(2,1)}, bf16[192,512]{1,0:T(8,128)(2,1)}, bf16[192,512]{1,0:T(8,128)(2,1)}, bf16[192,1536]{1,0:T(8,128)(2,1)}), (bf16[192,1536]{1,0:T(8,128)(2,1)}, bf16[192,512]{1,0:T(8,128)(2,1)}, ...) | async-done | bytes 1572880 | tf_op jit(solution)/shard_map/psum | solution.py:404
  (341 shorter events, 362.9 us)
Async XLA Ops:
  7.2 58.9 %copy-start.10 = (bf16[256,1536]{1,0:T(8,128)(2,1)S(1)}, bf16[256,1536]{1,0:T(8,128)(2,1)}, u32[]{:S(2)}) copy-start(bf16[256,1536]{1,0:T(8,128)(2,1)} %param.18) | copy-start | bytes 2359300
  7.2 31.2 %all-gather.11.cloned.1.call-start = ((), (), s32[]{:S(2)}) async-start(), calls=%async_computation.14 | async-start | bytes 1769472 | tf_op jit(solution)/shard_map/all_gather | solution.py:117
  7.9 58.1 %all-gather.17.cloned.1.call-start = ((), (), s32[]{:S(2)}) async-start(), calls=%async_computation.17 | async-start | bytes 1769472 | tf_op jit(solution)/shard_map/all_gather | solution.py:118
  8.7 89.7 %all-gather.13.cloned.1.call-start = ((), (), s32[]{:S(2)}) async-start(), calls=%async_computation.15 | async-start | bytes 1310720 | tf_op jit(solution)/shard_map/all_gather | solution.py:151
  27.9 138.9 %copy-start.29 = (f32[1536]{0:T(1024)}, f32[1536]{0:T(1024)S(1)}, u32[]{:S(2)}) copy-start(f32[1536]{0:T(1024)S(1)} %convert_element_type.209) | copy-start | bytes 18436
  29.9 137.0 %copy-start.42 = (f32[256]{0:T(256)}, f32[256]{0:T(256)S(1)}, u32[]{:S(2)}) copy-start(f32[256]{0:T(256)S(1)} %get-tuple-element.431) | copy-start | bytes 3076
  30.7 140.5 %copy-start.27 = (f32[256,32]{0,1:T(8,128)}, f32[256,32]{0,1:T(8,128)S(1)}, u32[]{:S(2)}) copy-start(f32[256,32]{0,1:T(8,128)S(1)} %get-tuple-element.429) | copy-start | bytes 98308
  41.7 85.0 %all-gather.19.cloned.1.call-start = ((), (), s32[]{:S(2)}) async-start(), calls=%async_computation.18 | async-start | bytes 1310720 | tf_op jit(solution)/shard_map/all_gather | solution.py:152
  68.8 98.1 %all-gather.15.cloned.1.call-start = ((), (), s32[]{:S(2)}) async-start(), calls=%async_computation.16 | async-start | bytes 5308416 | tf_op jit(solution)/shard_map/all_gather | solution.py:116
  69.4 146.1 %all-gather.21.cloned.1.call-start = ((), (), s32[]{:S(2)}) async-start(), calls=%async_computation.19 | async-start | bytes 5308416 | tf_op jit(solution)/shard_map/all_gather | solution.py:119
  70.0 191.7 %all-gather.23.cloned.1.call-start = ((), (), s32[]{:S(2)}) async-start(), calls=%async_computation.20 | async-start | bytes 8847360 | tf_op jit(solution)/shard_map/all_gather | solution.py:124
  70.7 358.7 %all-gather.25.cloned.1.call-start = ((), (), s32[]{:S(2)}) async-start(), calls=%async_computation.21 | async-start | bytes 8847360 | tf_op jit(solution)/shard_map/all_gather | solution.py:125
  72.0 148.8 %copy-start.38 = (f32[1536]{0:T(1024)}, f32[1536]{0:T(1024)S(1)}, u32[]{:S(2)}) copy-start(f32[1536]{0:T(1024)S(1)} %convert_element_type.217) | copy-start | bytes 18436
  221.5 254.8 %copy-start = (bf16[256,1536]{1,0:T(8,128)(2,1)}, bf16[256,1536]{1,0:T(8,128)(2,1)S(1)}, u32[]{:S(2)}) copy-start(bf16[256,1536]{1,0:T(8,128)(2,1)S(1)} %multiply_convert_fusion) | copy-start | bytes 2359300
  239.3 178.1 %all-to-all-start = ((bf16[4,5,128,1536]{3,2,1,0:T(8,128)(2,1)}), bf16[4,5,128,1536]{3,2,1,0:T(8,128)(2,1)}, u32[]{:S(2)}, u32[]{:S(2)}) async-start(bf16[4,5,128,1536]{3,2,1,0:T(8,128)(2,1)} %broadcast_select_fusion.1), calls=%async_computation | async-start | bytes 15728640 | tf_op jit(solution)/shard_map/all_to_all | solution.py:223
  244.8 198.5 %all-gather.27.cloned.1.call-start = ((), (), s32[]{:S(2)}) async-start(), calls=%async_computation.22 | async-start | bytes 8847360 | tf_op jit(solution)/shard_map/all_gather | solution.py:126
  461.0 177.5 %all-to-all-start.1 = ((bf16[4,5,128,1536]{3,2,1,0:T(8,128)(2,1)}), bf16[4,5,128,1536]{3,2,1,0:T(8,128)(2,1)}, u32[]{:S(2)}, u32[]{:S(2)}) async-start(bf16[4,5,128,1536]{3,2,1,0:T(8,128)(2,1)} %copy.120), calls=%async_computation.1 | async-start | bytes 15728640 | tf_op jit(solution)/shard_map/all_to_all | solution.py:232
  911.8 176.6 %all-to-all-start.3 = ((bf16[4,5,128,1536]{3,2,1,0:T(8,128)(2,1)}), bf16[4,5,128,1536]{3,2,1,0:T(8,128)(2,1)}, u32[]{:S(2)}, u32[]{:S(2)}) async-start(bf16[4,5,128,1536]{3,2,1,0:T(8,128)(2,1)} %copy.123), calls=%async_computation.3 | async-start | bytes 15728640 | tf_op jit(solution)/shard_map/all_to_all | solution.py:280
  917.5 296.0 %reduce-scatter.13.cloned.1.call-start = ((), (), s32[]{:S(2)}) async-start(), calls=%async_computation.23 | async-start | bytes 1310720 | tf_op jit(solution)/shard_map/reduce_scatter | solution.py:339
  1188.0 54.3 %reduce-scatter.15.cloned.1.call-start = ((), (), s32[]{:S(2)}) async-start(), calls=%async_computation.24 | async-start | bytes 1310720 | tf_op jit(solution)/shard_map/reduce_scatter | solution.py:345
  1190.4 100.5 %reduce-scatter.31.cloned.1.call-start = ((), (), s32[]{:S(2)}) async-start(), calls=%async_computation.32 | async-start | bytes 442368
  1191.6 129.1 %reduce-scatter.19.cloned.1.call-start = ((), (), s32[]{:S(2)}) async-start(), calls=%async_computation.26 | async-start | bytes 1769472 | tf_op jit(solution)/shard_map/reduce_scatter | solution.py:386
  1216.6 146.4 %reduce-scatter.21.cloned.1.call-start = ((), (), s32[]{:S(2)}) async-start(), calls=%async_computation.27 | async-start | bytes 1769472 | tf_op jit(solution)/shard_map/reduce_scatter | solution.py:389
  1245.2 175.0 %reduce-scatter.23.cloned.1.call-start = ((), (), s32[]{:S(2)}) async-start(), calls=%async_computation.28 | async-start | bytes 5308416 | tf_op jit(solution)/shard_map/reduce_scatter | solution.py:392
  1250.2 227.6 %reduce-scatter.17.cloned.1.call-start = ((), (), s32[]{:S(2)}) async-start(), calls=%async_computation.25 | async-start | bytes 5308416 | tf_op jit(solution)/shard_map/reduce_scatter | solution.py:383
  1255.5 295.0 %reduce-scatter.29.cloned.1.call-start = ((), (), s32[]{:S(2)}) async-start(), calls=%async_computation.31 | async-start | bytes 8847360 | tf_op jit(solution)/shard_map/reduce_scatter | solution.py:288
  1267.0 356.6 %reduce-scatter.25.cloned.1.call-start = ((), (), s32[]{:S(2)}) async-start(), calls=%async_computation.29 | async-start | bytes 8847360 | tf_op jit(solution)/shard_map/reduce_scatter | solution.py:282
  1278.6 417.8 %reduce-scatter.27.cloned.1.call-start = ((), (), s32[]{:S(2)}) async-start(), calls=%async_computation.30 | async-start | bytes 8847360 | tf_op jit(solution)/shard_map/reduce_scatter | solution.py:285
  1290.1 479.7 %all-reduce.10.cloned.1.call-start = ((), (), s32[]{:S(2)}) async-start(), calls=%async_computation.33 | async-start | bytes 3145728 | tf_op jit(solution)/shard_map/psum | solution.py:404
  1553.2 148.6 %copy-start.25 = (bf16[256,512]{0,1:T(8,128)(2,1)S(1)}, bf16[256,512]{0,1:T(8,128)(2,1)}, u32[]{:S(2)}) copy-start(bf16[256,512]{0,1:T(8,128)(2,1)} %reduce-scatter.15.cloned.1.call-done) | copy-start | bytes 786436
  1699.2 41.3 %copy-start.17 = (f32[256,1536]{1,0:T(8,128)S(1)}, f32[256,1536]{1,0:T(8,128)}, u32[]{:S(2)}) copy-start(f32[256,1536]{1,0:T(8,128)} %copy-done.16) | copy-start | bytes 4718596
  1699.2 41.3 %copy-start.52 = (f32[256]{0:T(256)S(1)}, f32[256]{0:T(256)}, u32[]{:S(2)}) copy-start(f32[256]{0:T(256)} %get-tuple-element.430) | copy-start | bytes 3076
  (52 other events, 499.7 us)
Sparse Core Ops, SparseCore 0:
  9.9 28.4 all-gather.10
  40.3 25.6 all-gather.16
  68.2 30.1 all-gather.12
  100.4 26.2 all-gather.18
  128.4 38.3 all-gather.14
  168.6 38.9 all-gather.20
  209.5 52.1 all-gather.22
  263.6 52.1 all-gather.24
  317.7 52.1 all-gather.26
  1188.1 25.3 reduce-scatter.12
  1216.5 25.7 reduce-scatter.14
  1245.8 32.5 reduce-scatter.30
  1282.2 38.4 reduce-scatter.18
  1324.5 38.4 reduce-scatter.20
  1366.2 53.8 reduce-scatter.22
  1423.8 53.8 reduce-scatter.16
  1481.0 69.4 reduce-scatter.28
  1554.2 69.3 reduce-scatter.24
  1627.0 69.4 reduce-scatter.26
  1699.1 70.7 all-reduce.9
where the time goes:
time: 1790 us; the launch traced here: 1780 us
  waiting for transfers between devices  1070 us (60%)
  matrix products  238 us (13%)
  blocking collectives  233 us (13%)
  local copies, waits for them, and re-layouts  128 us (7%)
  other arithmetic  77.3 us (4%)
  starting transfers between devices  18.1 us (1%)
    all_to_all x1, blocking collectives, per_device(): lax.all_to_all(grad_buffer.reshape(groups, local_experts, capacity, MODEL...  175 us
    all_to_all x1, waiting for transfers between devices, per_device(): lax.all_to_all(grad_rows, 'expert', split_axis=0, concat_axis=0, tiled=True)  165 us
    all_to_all x1, waiting for transfers between devices, per_device(): lax.all_to_all(result, 'expert', split_axis=0, concat_axis=0, tiled=True)  162 us
    all_to_all x1, waiting for transfers between devices, per_device(): lax.all_to_all(buffer, 'expert', split_axis=0, concat_axis=0, tiled=True)  156 us
    reduce_scatter x1, waiting for transfers between devices, per_device(): lax.psum_scatter(grad_gate_w.astype(jnp.bfloat16), 'dp', scatter_dimensio...  70.4 us
    reduce_scatter x1, waiting for transfers between devices, per_device(): lax.psum_scatter(grad_up_w.astype(jnp.bfloat16), 'dp', scatter_dimension=...  70.2 us
    reduce_scatter x1, waiting for transfers between devices, per_device(): lax.psum_scatter(grad_down.astype(jnp.bfloat16), 'dp', scatter_dimension=...  67.8 us
    reduce_scatter x1, waiting for transfers between devices, per_device(): lax.psum_scatter(grad_query_w.astype(jnp.bfloat16), 'dp', scatter_dimensi...  57.6 us
  transfers between devices with their start and end apart: 23, of which 19 were waited for; matrix products, arithmetic and copies ran while one was open for 12% of the time, Pallas kernels for 0%

commit v1 on v0

v1 whole, which is shorter than its diff:
```python
import functools

import jax
import jax.numpy as jnp
from jax import lax
from jax.experimental import pallas as pl
from jax.experimental.pallas import tpu as pltpu
from jax.sharding import PartitionSpec as P

MODEL_WIDTH = 1536
QUERY_HEADS = 24
KEY_VALUE_HEADS = 8
HEAD_SIZE = 64
TOPK = 8
PIECE_LEN = 256
EPSILON = 1e-05
THETA = 10000.0
BF16 = jnp.bfloat16
F32 = jnp.float32


def dot(left, right, dims=((1,), (0,))):
    return lax.dot_general(left, right, (dims, ((), ())), preferred_element_type=F32)


def dot_t(left, right):
    return dot(left, right, ((1,), (1,)))


def tdot(left, right):
    return dot(left, right, ((0,), (0,)))


DMA = pltpu.SemaphoreType.DMA
MESH = pl.DeviceIdType.MESH


def barrier_all(n, me):
    barrier = pltpu.get_barrier_semaphore()
    for d in range(n):

        @pl.when(d != me)
        def _():
            pl.semaphore_signal(barrier, inc=1, device_id={"expert": d}, device_id_type=MESH)

    pl.semaphore_wait(barrier, n - 1)


def remote(src, dst, send, recv, target):
    return pltpu.make_async_remote_copy(
        src_ref=src, dst_ref=dst, send_sem=send, recv_sem=recv,
        device_id={"expert": target}, device_id_type=MESH,
    )


class ChainGather:
    def __init__(self, n, me, slots, send, recv):
        self.n, self.me, self.slots, self.send, self.recv = n, me, slots, send, recv

    def copy(self, way, s, block, target):
        ref = self.slots.at[block]
        return remote(ref, ref, self.send.at[way, s], self.recv.at[way, s], target)

    def right(self, s):
        return self.copy(0, s, self.me - s, self.me + 1)

    def left(self, s):
        return self.copy(1, s, self.me + s, self.me - 1)

    def arrived(self, s):
        n, me = self.n, self.me

        @pl.when(me - 1 - s >= 0)
        def _():
            self.copy(0, s, me - 1 - s, me).wait_recv()

        @pl.when(me + 1 + s < n)
        def _():
            self.copy(1, s, me + 1 + s, me).wait_recv()

    def step(self, s):
        n, me = self.n, self.me
        if s >= 1:
            self.arrived(s - 1)

        @pl.when((me - s >= 0) & (me + 1 < n))
        def _():
            self.right(s).start()

        @pl.when((me + s < n) & (me > 0))
        def _():
            self.left(s).start()

    def finish(self):
        n, me = self.n, self.me
        self.arrived(n - 2)
        for s in range(n - 1):

            @pl.when((me - s >= 0) & (me + 1 < n))
            def _():
                self.right(s).wait_send()

            @pl.when((me + s < n) & (me > 0))
            def _():
                self.left(s).wait_send()


class Exchange:
    def __init__(self, n, me, source, slots, send, recv):
        self.n, self.me, self.source, self.slots = n, me, source, slots
        self.send, self.recv = send, recv

    def start(self, d):
        me = self.me

        @pl.when(d != me)
        def _():
            remote(
                self.source.at[d], self.slots.at[me], self.send.at[d], self.recv.at[me], d
            ).start()

    def finish(self):
        me = self.me
        for d in range(self.n):

            @pl.when(d != me)
            def _():
                desc = remote(
                    self.source.at[d], self.slots.at[d], self.send.at[d], self.recv.at[d], d
                )
                desc.wait_send()
                desc.wait_recv()


def chain_sems(n):
    return [pltpu.SemaphoreType.DMA((2, n - 1)), pltpu.SemaphoreType.DMA((2, n - 1))]


def direct_sems(n):
    return [pltpu.SemaphoreType.DMA((n,)), pltpu.SemaphoreType.DMA((n,))]


def call(kernel, outs, scratch, ident, name, flops, mib, args, far=()):
    vmem = pl.BlockSpec(memory_space=pltpu.VMEM)
    smem, anywhere = pl.BlockSpec(memory_space=pltpu.SMEM), pl.BlockSpec(memory_space=pl.ANY)
    nbytes = sum(a.size * a.dtype.itemsize for a in args)
    return pl.pallas_call(
        kernel,
        in_specs=[
            anywhere if j in far else smem if a.dtype == jnp.int32 else vmem
            for j, a in enumerate(args)
        ],
        out_specs=[vmem] * len(outs),
        out_shape=outs,
        scratch_shapes=scratch,
        compiler_params=pltpu.CompilerParams(
            collective_id=ident, has_side_effects=True, vmem_limit_bytes=mib * 1024 * 1024
        ),
        cost_estimate=pl.CostEstimate(flops=flops, transcendentals=0, bytes_accessed=nbytes),
        name=name,
    )(*args)


def gather_kernel(n, tokens_ref, chosen_ref, all_ref, every_ref, source, s0, r0, s1, r1):
    me = lax.axis_index("expert")
    barrier_all(n, me)
    all_ref[me] = tokens_ref[...]
    chain = ChainGather(n, me, all_ref, s0, r0)
    chain.step(0)
    every_ref[me] = chosen_ref[...]
    for d in range(n):
        source[d] = chosen_ref[...]
    small = Exchange(n, me, source, every_ref, s1, r1)
    for d in range(n):
        small.start(d)
    for s in range(1, n - 1):
        chain.step(s)
    chain.finish()
    small.finish()


def gather_tokens(n, tokens, chosen):
    rows, width = tokens.shape
    return call(
        functools.partial(gather_kernel, n),
        [
            jax.ShapeDtypeStruct((n, rows, width), BF16),
            jax.ShapeDtypeStruct((n,) + chosen.shape, F32),
        ],
        [pltpu.VMEM((n,) + chosen.shape, F32)] + chain_sems(n) + direct_sems(n),
        1, "gather_tokens", 10**6, 16, (tokens, chosen),
    )


def turn(x, cosine, sine):
    half = HEAD_SIZE // 2
    tiles = []
    for c in range(0, x.shape[1], 128):
        tile = x[:, c : c + 128]
        lane = lax.broadcasted_iota(jnp.int32, tile.shape, 1) % HEAD_SIZE
        other = jnp.where(lane < half, pltpu.roll(tile, 128 - half, 1), pltpu.roll(tile, half, 1))
        tiles.append(tile * cosine + other * sine)
    return jnp.concatenate(tiles, axis=1)


def bias_rows(starts_ref, q_pos, k_pos):
    seen = k_pos <= q_pos
    for k in range(starts_ref.shape[1]):
        a = starts_ref[0, k]
        q_in = (q_pos >= a) & (q_pos < a + PIECE_LEN)
        k_in = (k_pos >= a) & (k_pos < a + PIECE_LEN)
        seen = seen | (q_in & k_in)
    return jnp.where(seen, 0.0, -1e30)


def reach_of(block, rows, length, pieces):
    span = length // pieces
    return min(length, -(-((block + 1) * rows) // span) * span)


def attend_kernel(
    n, kv_local, tokens_ref, packed_ref, cos_ref, sin_ref, starts_ref, cot_ref,
    norm_ref, q_ref, k_ref, v_ref, lse_ref, out_ref, att_ref, cots_ref, small_ref,
    w_s, send_att, load, s0, r0, s1, r1,
):
    me = lax.axis_index("expert")
    per_key, length, tile = q_ref.shape
    rows = length // n
    q_cols, k_cols = per_key * tile, tile
    width, wide = w_s.shape
    weights = pltpu.make_async_copy(packed_ref.at[:, pl.ds(width, wide)], w_s, load)
    weights.start()
    barrier_all(n, me)
    cots_ref[me] = cot_ref[...]
    chain = ChainGather(n, me, cots_ref, s0, r0)
    chain.step(0)
    swap = Exchange(n, me, send_att, att_ref, s1, r1)
    pieces = starts_ref.shape[1]
    weights.wait()
    small = w_s[:, wide - 128 :].astype(F32).T
    small_ref[...] = small[: small_ref.shape[0], :]
    gain = small[:1, :]
    lane = lax.broadcasted_iota(jnp.int32, (rows, tile), 1)
    lane_w = lax.broadcasted_iota(jnp.int32, (rows, 128), 1)
    for i in range(n):
        part = slice(i * rows, (i + 1) * rows)
        x = tokens_ref[i].astype(F32)
        inverse = lax.rsqrt(jnp.mean(x * x, axis=1, keepdims=True) + EPSILON)
        norm = (x * inverse * gain).astype(BF16)
        norm_ref[i] = norm
        qkv = dot(norm, w_s[:, : wide - 128])
        qk = turn(qkv[:, : q_cols + k_cols], cos_ref[part, :], sin_ref[part, :]).astype(BF16)
        v_ref[part, :] = qkv[:, q_cols + k_cols : q_cols + 2 * k_cols].astype(BF16)
        k_ref[part, :] = qk[:, q_cols:]
        q = (qk[:, :q_cols].astype(F32) * HEAD_SIZE ** (-0.5)).astype(BF16)
        for t in range(per_key):
            for g in range(kv_local):
                at = (g * per_key + t) * HEAD_SIZE
                q_ref[t, part, g * HEAD_SIZE : (g + 1) * HEAD_SIZE] = q[:, at : at + HEAD_SIZE]
    if n > 2:
        chain.step(1)
    for i in range(n):
        reach = reach_of(i, rows, length, pieces)
        part = slice(i * rows, (i + 1) * rows)
        q_pos = lax.broadcasted_iota(jnp.int32, (rows, reach), 0) + i * rows
        k_pos = lax.broadcasted_iota(jnp.int32, (rows, reach), 1)
        bias = bias_rows(starts_ref, q_pos, k_pos)
        keys, values = k_ref[:reach, :], v_ref[:reach, :]
        k_lane = lax.broadcasted_iota(jnp.int32, (reach, tile), 1)

        def head(t, logs):
            q = q_ref[t, part, :]
            total = jnp.zeros((rows, tile), F32)
            for g in range(kv_local):
                mine = lane // HEAD_SIZE == g
                scores = dot_t(jnp.where(mine, q, jnp.zeros_like(q)), keys) + bias
                top = jnp.max(scores, axis=1, keepdims=True)
                powers = jnp.exp(scores - top)
                norm = jnp.sum(powers, axis=1, keepdims=True)
                value = jnp.where(k_lane // HEAD_SIZE == g, values, jnp.zeros_like(values))
                total = total + dot(powers.astype(BF16), value) * (1.0 / norm)
                logs = jnp.where(lane_w == t * kv_local + g, top + jnp.log(norm), logs)
            out_ref[t, part, :] = total
            return logs

        logs = lax.fori_loop(0, per_key, head, jnp.zeros((rows, 128), F32))
        lse_ref[:, part] = logs.T[: lse_ref.shape[0], :]
        for t in range(per_key):
            for g in range(kv_local):
                at = (g * per_key + t) * HEAD_SIZE
                send_att[i, :, at : at + HEAD_SIZE] = out_ref[
                    t, part, g * HEAD_SIZE : (g + 1) * HEAD_SIZE
                ].astype(BF16)
        swap.start(i)
        if i + 2 < n - 1:
            chain.step(i + 2)
    att_ref[me] = send_att[me]
    chain.finish()
    swap.finish()


def attend(n, kv_local, tokens_all, packed, cosine, sine, starts, cot):
    rows, width = cot.shape
    length = n * rows
    tile = kv_local * HEAD_SIZE
    per_key = QUERY_HEADS // KEY_VALUE_HEADS
    q_cols = per_key * tile
    wide = packed.shape[1] - width
    sds = jax.ShapeDtypeStruct
    lse_rows = -(-per_key * kv_local // 8) * 8
    return call(
        functools.partial(attend_kernel, n, kv_local),
        [
            sds((n, rows, width), BF16),
            sds((per_key, length, tile), BF16),
            sds((length, tile), BF16),
            sds((length, tile), BF16),
            sds((lse_rows, length), F32),
            sds((per_key, length, tile), F32),
            sds((n, rows, q_cols), BF16),
            sds((n, rows, width), BF16),
            sds((8 + 8 * n, width), F32),
        ],
        [pltpu.VMEM((width, wide), BF16), pltpu.VMEM((n, rows, q_cols), BF16), DMA]
        + chain_sems(n)
        + direct_sems(n),
        2, "attend", 5 * 10**9, 44, (tokens_all, packed, cosine, sine, starts, cot), (1,),
    )


def mix_kernel(
    n, tokens_ref, att_ref, packed_ref, small_ref, hidden_ref, norms_ref, own_ref, w_s, load, s0, r0
):
    me = lax.axis_index("expert")
    q_cols = att_ref.shape[2]
    width = w_s.shape[0]
    weights = pltpu.make_async_copy(packed_ref.at[:, pl.ds(0, width)], w_s, load)
    weights.start()
    hidden = tokens_ref[...].astype(F32)
    weights.wait()
    for s in range(n):
        hidden = hidden + dot(att_ref[s], w_s[s * q_cols : (s + 1) * q_cols, :])
    hidden_ref[...] = hidden
    inverse = lax.rsqrt(jnp.mean(hidden * hidden, axis=1, keepdims=True) + EPSILON)
    norm = (hidden * inverse * small_ref[1:2, :]).astype(BF16)
    own_ref[...] = norm
    barrier_all(n, me)
    norms_ref[me] = norm
    chain = ChainGather(n, me, norms_ref, s0, r0)
    for s in range(n - 1):
        chain.step(s)
    chain.finish()


def mix(n, tokens, att, packed, small):
    rows, width = tokens.shape
    sds = jax.ShapeDtypeStruct
    return call(
        functools.partial(mix_kernel, n),
        [sds((rows, width), F32), sds((n, rows, width), BF16), sds((rows, width), BF16)],
        [pltpu.VMEM((width, width), BF16), DMA] + chain_sems(n),
        3, "mix", 2 * 10**9, 32, (tokens, att, packed, small), (2,),
    )


class ChainReduce:
    def __init__(self, n, me, parts, from_left, from_right, send, recv):
        self.n, self.me, self.parts = n, me, parts
        self.slots, self.send, self.recv = (from_left, from_right), send, recv

    def copy(self, way, s, d, source):
        target = self.me + 1 if way == 0 else self.me - 1
        return remote(
            source.at[d], self.slots[way].at[d], self.send.at[way, s], self.recv.at[way, s], target
        )

    def step(self, s):
        n, me = self.n, self.me
        for way in (0, 1):
            d = n - 1 - s if way == 0 else s
            onward = me < d if way == 0 else me > d
            first = me == 0 if way == 0 else me == n - 1
            slot = self.slots[way]

            @pl.when(onward & first)
            def _():
                if s > 0:
                    self.copy(way, s - 1, d, self.parts).wait_send()
                self.copy(way, s, d, self.parts).start()

            @pl.when(onward & jnp.logical_not(first))
            def _():
                self.copy(way, s, d, slot).wait_recv()
                slot[d] = (slot[d].astype(F32) + self.parts[d].astype(F32)).astype(BF16)
                if s > 0:
                    self.copy(way, s - 1, d, slot).wait_send()
                self.copy(way, s, d, slot).start()

    def finish(self, total):
        n, me = self.n, self.me
        total[...] = self.parts[me].astype(F32)
        for way in (0, 1):
            last = n - 1 - me if way == 0 else me
            slot = self.slots[way]

            @pl.when(me > 0 if way == 0 else me < n - 1)
            def _():
                self.copy(way, last, me, slot).wait_recv()
                total[...] += slot[me].astype(F32)

            @pl.when(me < n - 1 if way == 0 else me > 0)
            def _():
                self.copy(way, last - 1, me, slot).wait_send()


def rms_back(grad, rows, gain):
    inverse = lax.rsqrt(jnp.mean(rows * rows, axis=1, keepdims=True) + EPSILON)
    scaled = grad * gain
    grad_gain = jnp.sum(grad * rows * inverse, axis=0, keepdims=True)
    mean = jnp.mean(scaled * rows, axis=1, keepdims=True)
    return inverse * scaled - rows * (inverse * inverse * inverse * mean), grad_gain


def softmax_chosen(logits, chosen):
    top = jnp.max(jnp.where(chosen > 0.0, logits, -1e30), axis=0, keepdims=True)
    powers = jnp.where(chosen > 0.0, jnp.exp(jnp.where(chosen > 0.0, logits - top, 0.0)), 0.0)
    return powers / jnp.sum(powers, axis=0, keepdims=True)


def return_kernel(
    n, parts_ref, gg_ref, chosen_ref, small_ref, hidden_ref, norm_ref, cot_ref, att_ref, packed_ref,
    grad_ref, ga_ref, o_ref, extra_ref,
    w_s, from_left, from_right, total, gg_s, send_ga, load, s0, r0, s1, r1, s2, r2,
):
    me = lax.axis_index("expert")
    width = w_s.shape[0]
    q_cols = ga_ref.shape[2]
    weights = pltpu.make_async_copy(packed_ref.at[:, pl.ds(0, width)], w_s, load)
    weights.start()
    barrier_all(n, me)
    chain = ChainReduce(n, me, parts_ref, from_left, from_right, s0, r0)
    chain.step(0)
    gates_swap = Exchange(n, me, gg_ref, gg_s, s1, r1)
    for d in range(n):
        gates_swap.start(d)
    gg_s[me] = gg_ref[me]
    router = small_ref[8:, :].astype(BF16)
    gates = softmax_chosen(dot_t(router, norm_ref[...]), chosen_ref[...])
    gates_swap.finish()
    grad_gates = gg_s[...].reshape(gates.shape)
    middle = jnp.sum(gates * grad_gates, axis=0, keepdims=True)
    grad_logits = (gates * (grad_gates - middle)).astype(BF16)
    extra_ref[8:, :] = dot(grad_logits, norm_ref[...])
    for s in range(1, n - 1):
        chain.step(s)
    chain.finish(total)
    grad_norm = total[...] + tdot(grad_logits, router)
    grad, grad_gain = rms_back(grad_norm, hidden_ref[...], small_ref[1:2, :])
    row = lax.broadcasted_iota(jnp.int32, (8, width), 0)
    extra_ref[:8, :] = jnp.where(row == 1, grad_gain, 0.0)
    grad = cot_ref[...].astype(F32) + grad
    grad_ref[...] = grad
    proj = grad.astype(BF16)
    weights.wait()
    swap = Exchange(n, me, send_ga, ga_ref, s2, r2)
    for d in range(n):
        send_ga[d] = dot_t(proj, w_s[d * q_cols : (d + 1) * q_cols, :]).astype(BF16)
        swap.start(d)
    ga_ref[me] = send_ga[me]
    for d in range(n):
        o_ref[d * q_cols : (d + 1) * q_cols, :] = tdot(att_ref[d], proj).astype(BF16)
    swap.finish()


def give_back(n, parts, gg, chosen, small, hidden, norm, cot, att, packed):
    rows, width = cot.shape
    q_cols = att.shape[2]
    sds, vm = jax.ShapeDtypeStruct, pltpu.VMEM
    return call(
        functools.partial(return_kernel, n),
        [
            sds((rows, width), F32), sds(att.shape, BF16), sds((width, width), BF16),
            sds(small.shape, F32),
        ],
        [
            vm((width, width), BF16), vm((n, rows, width), BF16), vm((n, rows, width), BF16),
            vm((rows, width), F32), vm(gg.shape, F32), vm((n, rows, q_cols), BF16), DMA,
        ]
        + chain_sems(n) + direct_sems(n) + direct_sems(n),
        4, "give_back", 4 * 10**9, 48,
        (parts, gg, chosen, small, hidden, norm, cot, att, packed), (8,),
    )


def attend_back_kernel(
    n, kv_local, q_ref, k_ref, v_ref, lse_ref, out_ref, ga_ref, starts_ref, cos_ref, sin_ref,
    norm_ref, packed_ref, tokens_ref, small_ref, grad_ref, hidden_ref, y_ref, extra_ref,
    output_ref, input_ref, dw_ref,
    w_s, gq_s, gk_s, gv_s, gqkv_s, ga_s, parts_s, y_left, y_right, b_left, b_right, total, load,
    s0, r0, s1, r1,
):
    me = lax.axis_index("expert")
    per_key, length, tile = q_ref.shape
    rows = length // n
    q_cols, k_cols = per_key * tile, tile
    width, wide = w_s.shape
    used = q_cols + 2 * k_cols
    scale = HEAD_SIZE ** (-0.5)
    pieces = starts_ref.shape[1]
    weights = pltpu.make_async_copy(packed_ref.at[:, pl.ds(width, wide)], w_s, load)
    weights.start()
    barrier_all(n, me)
    y_chain = ChainReduce(n, me, y_ref, y_left, y_right, s0, r0)
    y_chain.step(0)
    gk_s[...] = jnp.zeros_like(gk_s)
    gv_s[...] = jnp.zeros_like(gv_s)
    lane = lax.broadcasted_iota(jnp.int32, (rows, tile), 1)
    lane_w = lax.broadcasted_iota(jnp.int32, (rows, 128), 1)
    for i in range(n):
        reach = reach_of(i, rows, length, pieces)
        part = slice(i * rows, (i + 1) * rows)
        deltas = jnp.zeros((rows, 128), F32)
        for t in range(per_key):
            for g in range(kv_local):
                at = (g * per_key + t) * HEAD_SIZE
                ga_s[t, :, g * HEAD_SIZE : (g + 1) * HEAD_SIZE] = ga_ref[i, :, at : at + HEAD_SIZE]
            product = ga_s[t].astype(F32) * out_ref[t, part, :]
            for g in range(kv_local):
                own = jnp.where(lane // HEAD_SIZE == g, product, 0.0)
                deltas = jnp.where(
                    lane_w == t * kv_local + g, jnp.sum(own, axis=1, keepdims=True), deltas
                )
        delta_s = deltas.T
        k_pos = lax.broadcasted_iota(jnp.int32, (reach, rows), 0)
        q_pos = lax.broadcasted_iota(jnp.int32, (reach, rows), 1) + i * rows
        bias = bias_rows(starts_ref, q_pos, k_pos)
        keys, values = k_ref[:reach, :], v_ref[:reach, :]
        k_lane = lax.broadcasted_iota(jnp.int32, (reach, tile), 1)
        for t in range(per_key):
            q, ga = q_ref[t, part, :], ga_s[t]
            grad_q = jnp.zeros((rows, tile), F32)
            for g in range(kv_local):
                h = t * kv_local + g
                mine = lane // HEAD_SIZE == g
                q_g = jnp.where(mine, q, jnp.zeros_like(q))
                ga_g = jnp.where(mine, ga, jnp.zeros_like(ga))
                scores = dot_t(keys, q_g) + bias
                probs = jnp.exp(scores - lse_ref[h : h + 1, part])
                grad_probs = dot_t(values, ga_g)
                grad_raw = (probs * (grad_probs - delta_s[h : h + 1, :])).astype(BF16)
                gk_s[:reach, :] += dot(grad_raw, q_g)
                gv_s[:reach, :] += dot(probs.astype(BF16), ga_g)
                key = jnp.where(k_lane // HEAD_SIZE == g, keys, jnp.zeros_like(keys))
                grad_q = grad_q + tdot(grad_raw, key)
            for g in range(kv_local):
                at = (g * per_key + t) * HEAD_SIZE
                gq_s[part, at : at + HEAD_SIZE] = (
                    grad_q[:, g * HEAD_SIZE : (g + 1) * HEAD_SIZE] * scale
                )
        if i + 1 < n - 1:
            y_chain.step(i + 1)
    gq_s[:, q_cols:] = gk_s[...]
    weights.wait()
    if used < gqkv_s.shape[1]:
        gqkv_s[...] = jnp.zeros_like(gqkv_s)
    for i in range(n):
        part = slice(i * rows, (i + 1) * rows)
        qk = turn(gq_s[part, :], cos_ref[part, :], -sin_ref[part, :]).astype(BF16)
        gqkv_s[part, : q_cols + k_cols] = qk
        gqkv_s[part, q_cols + k_cols : used] = gv_s[part, :].astype(BF16)
        parts_s[i] = dot_t(gqkv_s[part, :], w_s[:, : wide - 128]).astype(BF16)
    chain = ChainReduce(n, me, parts_s, b_left, b_right, s1, r1)
    chain.step(0)
    y_chain.finish(total)
    output_ref[...] = (hidden_ref[...] + total[...]).astype(BF16)
    norms = norm_ref[...].reshape(length, width)
    dw_ref[:, : wide - 128] = tdot(norms, gqkv_s[...]).astype(BF16)
    for s in range(1, n - 1):
        chain.step(s)
    chain.finish(total)
    grad, grad_gain = rms_back(total[...], tokens_ref[...].astype(F32), small_ref[:1, :])
    input_ref[...] = (grad_ref[...] + grad).astype(BF16)
    extra = extra_ref[...]
    row = lax.broadcasted_iota(jnp.int32, extra.shape, 0)
    extra = jnp.where(row == 0, grad_gain, extra)
    extra = jnp.concatenate([extra, jnp.zeros((128 - extra.shape[0], width), F32)], axis=0)
    dw_ref[:, wide - 128 :] = extra.T.astype(BF16)


def attend_back(n, kv_local, saved, ga, starts, cosine, sine, norms, packed, tokens, small, grad, hidden, y, extra):
    q, k, v, lse, out = saved
    rows, width = tokens.shape
    per_key, length, tile = q.shape
    wide = packed.shape[1] - width
    sds, vm = jax.ShapeDtypeStruct, pltpu.VMEM
    qk = (per_key + 1) * tile
    block = vm((n, rows, width), BF16)
    return call(
        functools.partial(attend_back_kernel, n, kv_local),
        [sds((rows, width), BF16), sds((rows, width), BF16), sds((width, wide), BF16)],
        [
            vm((width, wide), BF16), vm((length, qk), F32), vm((length, tile), F32),
            vm((length, tile), F32), vm((length, wide - 128), BF16), vm((per_key, rows, tile), BF16),
            block, block, block, block, block, vm((rows, width), F32), DMA,
        ]
        + chain_sems(n) + chain_sems(n),
        5, "attend_back", 10 * 10**9, 58,
        (q, k, v, lse, out, ga, starts, cosine, sine, norms, packed, tokens, small, grad, hidden, y, extra),
        (10,),
    )


def expert_kernel(
    member_ref, chosen_ref, small_ref, n2_ref, cot_ref, wg_ref, wu_ref, wd_ref,
    dw_ref, y_ref, gx_ref, gg_ref,
    xe, ge, gr, act_s, ggp_s, gup_s, pick_s, gated_s, grows_s, gate_s, rank_s,
):
    e, phase = pl.program_id(0), pl.program_id(1)
    groups, rows, width = n2_ref.shape
    cap = xe.shape[0] // groups
    ff = act_s.shape[1]
    shards = wg_ref.shape[0]
    depth = ff // shards
    blocks = width // ff

    def whole(ref):
        return ref[...].reshape(width, ff)

    def down(j):
        return wd_ref[:, 0, j * depth:(j + 1) * depth, :].reshape(ff, ff)

    @pl.when((phase == 0) & (e == 0))
    def _():
        before = lax.broadcasted_iota(jnp.int32, (rows, rows), 0)
        upto = jnp.where(before <= lax.broadcasted_iota(jnp.int32, (rows, rows), 1), 1.0, 0.0)
        router = small_ref[8:, :].astype(BF16)
        for s in range(groups):
            chosen = chosen_ref[s]
            gate_s[s] = softmax_chosen(dot_t(router, n2_ref[s]), chosen)
            count = dot(chosen.astype(BF16), upto.astype(BF16))
            rank_s[s] = jnp.where(chosen > 0.0, count - 1.0, -1.0).astype(jnp.int32)
        gg_ref[...] = jnp.zeros_like(gg_ref)

    @pl.when(phase == 0)
    def _():
        mine = member_ref[0] * gg_ref.shape[1] + e
        picks, cols = [], []
        slot = lax.broadcasted_iota(jnp.int32, (cap, rows), 0)
        for s in range(groups):
            pick = slot == rank_s[s, pl.ds(mine, 1), :]
            picks.append(pick)
            hot = jnp.where(pick, 1.0, 0.0).astype(BF16)
            pick_s[s, pl.ds(pl.multiple_of(e * cap, cap), cap), :] = hot
            col = jnp.sum(jnp.where(pick, gate_s[s, pl.ds(mine, 1), :], 0.0), axis=1, keepdims=True)
            cols.append(col)
            part = slice(s * cap, (s + 1) * cap)
            xe[part, :] = dot(hot, n2_ref[s]).astype(BF16)
            g = dot(hot, cot_ref[s])
            ge[part, :] = g.astype(BF16)
            gr[part, :] = (col * g).astype(BF16)
        x = xe[...]
        gp = dot(x, whole(wg_ref))
        up = dot(x, whole(wu_ref))
        sigma = jax.nn.sigmoid(gp)
        silu = gp * sigma
        act = (silu * up).astype(BF16)
        act_s[...] = act
        grad_act = jnp.zeros_like(gp)
        gate_sums = [jnp.zeros((cap, 1), F32) for _ in range(groups)]
        for j in range(blocks):
            lanes = slice(j * ff, (j + 1) * ff)
            w = down(j)
            res = dot(act, w).astype(BF16).astype(F32)
            grad_act = grad_act + dot_t(gr[:, lanes], w)
            for s in range(groups):
                part = slice(s * cap, (s + 1) * cap)
                r = res[part, :]
                gated_s[s, pl.ds(pl.multiple_of(e * cap, cap), cap), lanes] = (cols[s] * r).astype(BF16)
                gate_sums[s] = gate_sums[s] + jnp.sum(ge[part, lanes].astype(F32) * r, axis=1, keepdims=True)
        for s in range(groups):
            gg_ref[s, pl.ds(e, 1), :] = jnp.sum(jnp.where(picks[s], gate_sums[s], 0.0), axis=0, keepdims=True)
        ggp = (grad_act * up * sigma * (1.0 + gp * (1.0 - sigma))).astype(BF16)
        ggp_s[...] = ggp
        gup_s[...] = (grad_act * silu).astype(BF16)
        dw_ref[...] = tdot(xe[...], ggp).astype(BF16).reshape(dw_ref.shape)

    @pl.when(phase == 1)
    def _():
        dw_ref[...] = tdot(xe[...], gup_s[...]).astype(BF16).reshape(dw_ref.shape)
        grows = (dot_t(ggp_s[...], whole(wg_ref)) + dot_t(gup_s[...], whole(wu_ref))).astype(BF16)
        for s in range(groups):
            grows_s[s, pl.ds(pl.multiple_of(e * cap, cap), cap), :] = grows[s * cap:(s + 1) * cap, :]

    @pl.when(phase == 2)
    def _():
        for j in range(blocks):
            lanes = slice(j * ff, (j + 1) * ff)
            dw_ref[:, 0, j * depth:(j + 1) * depth, :] = tdot(act_s[...], gr[:, lanes]).astype(BF16).reshape(shards, depth, ff)

    @pl.when((phase == 2) & (e == pl.num_programs(0) - 1))
    def _():
        for s in range(groups):
            y_ref[s] = tdot(pick_s[s], gated_s[s]).astype(BF16)
            gx_ref[s] = tdot(pick_s[s], grows_s[s]).astype(BF16)


def experts(member, chosen, small, n2, cot, w):
    groups, rows, width = n2.shape
    shards, local, depth, ff = w.shape
    local = local // 3
    cap = rows * TOPK * 5 // (4 * local * groups)
    tall = groups * cap
    padded = chosen.shape[1] // groups
    once = pl.Buffered(1)

    def const(shape):
        return pl.BlockSpec(shape, lambda e, p: (0,) * len(shape), pipeline_mode=once)

    def weight(k):
        return pl.BlockSpec((shards, 1, depth, ff), lambda e, p: (0, k * local + e, 0, 0))

    sds, vm = jax.ShapeDtypeStruct, pltpu.VMEM
    return pl.pallas_call(
        expert_kernel,
        grid=(local, 3),
        in_specs=[
            pl.BlockSpec(memory_space=pltpu.SMEM), const(chosen.shape), const(small.shape),
            const(n2.shape), const(n2.shape), weight(0), weight(1), weight(2),
        ],
        out_specs=[
            pl.BlockSpec((shards, 1, depth, ff), lambda e, p: (0, p * local + e, 0, 0)),
            const(n2.shape), const(n2.shape), const((groups, padded, rows)),
        ],
        out_shape=[
            sds(w.shape, BF16), sds(n2.shape, BF16), sds(n2.shape, BF16),
            sds((groups, padded, rows), F32),
        ],
        scratch_shapes=[
            vm((tall, width), BF16), vm((tall, width), BF16), vm((tall, width), BF16),
            vm((tall, ff), BF16), vm((tall, ff), BF16), vm((tall, ff), BF16),
            vm((groups, local * cap, rows), BF16), vm((groups, local * cap, width), BF16),
            vm((groups, local * cap, width), BF16), vm(chosen.shape, F32),
            vm(chosen.shape, jnp.int32),
        ],
        compiler_params=pltpu.CompilerParams(
            vmem_limit_bytes=60 * 1024 * 1024, dimension_semantics=("arbitrary", "arbitrary")
        ),
        cost_estimate=pl.CostEstimate(
            flops=40 * 10**9, transcendentals=0, bytes_accessed=60 * 10**6
        ),
        name="experts",
    )(member, chosen, small, n2, cot, w, w, w)


def per_device(
    tokens, attn_gain, q_weight, key_matrix, value_matrix, o_weight, ffn_gain, router_weight,
    expert_gate, expert_up, expert_down, routes, starts, cotangent,
):
    n = lax.axis_size("expert")
    member = lax.axis_index("expert")
    rows, width = tokens.shape
    length = rows * n
    kv_local = KEY_VALUE_HEADS // n
    q_cols = QUERY_HEADS // n * HEAD_SIZE
    k_cols = kv_local * HEAD_SIZE
    local, shard, ff = expert_gate.shape
    depth = expert_down.shape[1]
    blocks = width // ff
    padded = -(-local // 8) * 8

    wq = lax.dynamic_slice_in_dim(q_weight, member * q_cols, q_cols, 1)
    wk = lax.dynamic_slice_in_dim(key_matrix, member * k_cols, k_cols, 1)
    wv = lax.dynamic_slice_in_dim(value_matrix, member * k_cols, k_cols, 1)
    wide = width // 2
    used = q_cols + 2 * k_cols
    router = jnp.pad(
        router_weight.reshape(shard, n, local), ((0, 0), (0, 0), (0, padded - local))
    ).reshape(shard, n * padded)
    gains = jnp.stack([attn_gain, ffn_gain], axis=1)
    gap = jnp.zeros((shard, wide - 128 - used), BF16)
    packed = jnp.concatenate(
        [
            o_weight, wq, wk, wv, gap, jnp.pad(gains, ((0, 0), (0, 6))), router,
            jnp.zeros((shard, 120 - n * padded), BF16),
        ],
        axis=1,
    )
    packed = lax.all_gather(packed, "dp").reshape(width, -1)
    down_rows = expert_down.reshape(local, depth, blocks, ff).transpose(0, 2, 1, 3)
    stacked = jnp.concatenate(
        [expert_gate, expert_up, down_rows.reshape(local, shard, ff)], axis=0
    )
    experts_w = lax.all_gather(stacked, "dp")

    hot = routes[:, :, None] == jnp.arange(n * local, dtype=jnp.int32)
    chosen = jnp.any(hot, axis=1).astype(F32).T.reshape(n, local, rows)
    chosen = jnp.pad(chosen, ((0, 0), (0, padded - local), (0, 0))).reshape(n * padded, rows)
    half = HEAD_SIZE // 2
    freqs = THETA ** (-(jnp.arange(half, dtype=F32) * 2.0 / HEAD_SIZE))
    angles = jnp.arange(length, dtype=jnp.int32).astype(F32)[:, None] * freqs[None, :]
    cosine, sine = jnp.cos(angles), jnp.sin(angles)
    cosine = jnp.concatenate([cosine, cosine, cosine, cosine], axis=1)
    sine = jnp.concatenate([-sine, sine, -sine, sine], axis=1)

    tokens_all, chosen_all = gather_tokens(n, tokens, chosen)
    norms, q, k, v, lse, out, att, cots, small = attend(
        n, kv_local, tokens_all, packed, cosine, sine, starts, cotangent
    )
    hidden, twos, two = mix(n, tokens, att, packed, small)
    grad_experts, y, back, gg = experts(
        member.astype(jnp.int32)[None], chosen_all, small, twos, cots, experts_w
    )
    expert_grads = lax.psum_scatter(grad_experts, "dp", scatter_dimension=0).astype(F32)
    gate_grad, up_grad = expert_grads[:local], expert_grads[local : 2 * local]
    down_grad = expert_grads[2 * local :].reshape(local, blocks, depth, ff)
    down_grad = down_grad.transpose(0, 2, 1, 3).reshape(local, depth, width)
    grad_hidden, ga, grad_o, extra = give_back(
        n, back, gg, chosen, small, hidden, two, cotangent, att, packed
    )
    grad_o = lax.psum_scatter(grad_o.reshape(-1, shard, width), "dp", scatter_dimension=0)
    output, input_grad, grad_w = attend_back(
        n, kv_local, (q, k, v, lse, out), ga, starts, cosine, sine, norms, packed, tokens, small,
        grad_hidden, hidden, y, extra,
    )
    grad_w = lax.psum_scatter(grad_w.reshape(-1, shard, wide), "dp", scatter_dimension=0)
    o_grad = lax.psum(grad_o, "expert").astype(F32)
    shares = lax.all_gather(grad_w, "expert").astype(F32)
    q_grad = shares[:, :, :q_cols].transpose(1, 0, 2).reshape(shard, -1)
    k_grad = shares[:, :, q_cols : q_cols + k_cols].transpose(1, 0, 2).reshape(shard, -1)
    v_grad = shares[:, :, q_cols + k_cols : used].transpose(1, 0, 2).reshape(shard, -1)
    rest = jnp.sum(shares[:, :, wide - 128 :], axis=0)
    router_grad = rest[:, 8 : 8 + n * padded].reshape(shard, n, padded)[:, :, :local]
    return (
        output, input_grad, rest[:, 0], q_grad, k_grad, v_grad, o_grad, rest[:, 1],
        router_grad.reshape(shard, n * local), gate_grad, up_grad, down_grad,
    )


def solution(mesh):
    rows, split, expert = P(("dp", "expert"), None), P("dp", None), P("expert", "dp", None)
    return jax.shard_map(
        per_device,
        mesh=mesh,
        in_specs=(
            rows, P("dp"), split, split, split, split, P("dp"), split,
            expert, expert, expert, rows, split, rows,
        ),
        out_specs=(
            rows, rows, P("dp"), split, split, split, split, P("dp"), split,
            expert, expert, expert,
        ),
        check_vma=False,
    )
```

time: 1790 us -> 872 us (0.49)
  waiting for transfers between devices: 1070 us -> 320 us
  Pallas kernels: 0 us -> 484 us
  matrix products: 238 us -> 0 us
  blocking collectives: 233 us -> 0 us
  local copies, waits for them, and re-layouts: 128 us -> 36 us
  other arithmetic: 77.3 us -> 12.7 us
    pallas_call x0 -> x6, Pallas kernels: none -> 484 us  [the longest x5 413 us: call(): pl.pallas_call(kernel, in_specs=[anywhere if j in far else smem if a.dtyp...]
    all_to_all x3 -> x0, waiting for transfers between devices: 483 us -> none  [the longest x1 165 us: per_device(): lax.all_to_all(grad_rows, 'expert', split_axis=0, concat_axis=0, tiled=True)]
    dot_general x40 -> x0, matrix products: 238 us -> none  [the longest x4 16.8 us: scores_of(): jnp.einsum('qgrd,kgd->grqk', query_rows, key_block, preferred_element_typ...]
    reduce_scatter x9 -> x3, waiting for transfers between devices: 442 us -> 253 us  [the longest x1 150 us: per_device(): lax.psum_scatter(grad_experts, 'dp', scatter_dimension=0).astype(F32)]
    all_to_all x1 -> x0, blocking collectives: 175 us -> none  [per_device(): lax.all_to_all(grad_buffer.reshape(groups, local_experts, capacity, MODEL...]
    all_gather x9 -> x3, waiting for transfers between devices: 116 us -> 31.1 us  [the longest x1 31.1 us: per_device(): shares = lax.all_gather(grad_w, 'expert').astype(F32)]
    gather x4 -> x0, local copies, waits for them, and re-layouts: 65.3 us -> none  [the longest x1 20 us: per_device(): grad_pairs[pair_index]]
    unnamed x2 -> x0, blocking collectives: 29.2 us -> none
  transfers between devices with their start and end apart: 23 -> 7, of which waited for: 19 -> 5; matrix products, arithmetic and copies ran while one was open for 12% -> 2% of each run, Pallas kernels for 0% -> 21%
where the time goes in v1:
time: 872 us; the launch traced here: 868 us
  Pallas kernels  484 us (56%)
  waiting for transfers between devices  320 us (37%)
  local copies, waits for them, and re-layouts  36 us (4%)
  between operations  15 us (2%)
  other arithmetic  12.7 us (1%)
    pallas_call x5, Pallas kernels, call(): pl.pallas_call(kernel, in_specs=[anywhere if j in far else smem if a.dtyp...  413 us
    reduce_scatter x1, waiting for transfers between devices, per_device(): lax.psum_scatter(grad_experts, 'dp', scatter_dimension=0).astype(F32)  150 us
    pallas_call x1, Pallas kernels, experts(): pl.pallas_call(expert_kernel, grid=(local, 3), in_specs=[pl.BlockSpec(mem...  71 us
    reduce_scatter x1, waiting for transfers between devices, per_device(): lax.psum_scatter(grad_o.reshape(-1, shard, width), 'dp', scatter_dimensio...  57.6 us
    reduce_scatter x1, waiting for transfers between devices, per_device(): lax.psum_scatter(grad_w.reshape(-1, shard, wide), 'dp', scatter_dimension=0)  45.2 us
    psum x1, waiting for transfers between devices, per_device(): o_grad = lax.psum(grad_o, 'expert').astype(F32)  34.7 us
    all_gather x1, waiting for transfers between devices, per_device(): shares = lax.all_gather(grad_w, 'expert').astype(F32)  31.1 us
    unnamed x61, local copies, waits for them, and re-layouts  17.9 us
  transfers between devices with their start and end apart: 7, of which 5 were waited for; matrix products, arithmetic and copies ran while one was open for 2% of the time, Pallas kernels for 21%

profile of v1, /device:TPU:0, one launch (start us, length us, event | category | flops | bytes accessed | tf_op | source)
XLA Modules:
  0.0 867.6 jit_solution(4005236839256097699)
XLA Ops:
  10.6 2.0 concatenate.12
  13.6 3.5 pad_maximum_fusion
  18.2 60.0 %gather_tokens.1 = (bf16[4,256,1536]{2,1,0:T(8,128)(2,1)S(1)}, f32[4,32,256]{2,1,0:T(8,128)S(1)}) custom-call(bf16[256,1536]{1,0:T(8,128)(2,1)S(1)} %copy-done.3, f32[32,256]{1,0:T(8,128)S(1)} %convert_bitcast_fusion.chosen_ref), custom_call_target="tpu_custom_call" | custom-call | flops 1000000 | bytes 819200 | tf_op jit(solution)/shard_map/gather_tokens/pallas_call | solution.py:147
  78.3 1.6 copy-done.8
  80.0 1.9 fusion
  81.9 0.9 pad_maximum_fusion.1
  82.8 1.4 copy-done.11
  84.3 68.3 %attend.1 = (bf16[4,256,1536]{2,1,0:T(8,128)(2,1)S(1)}, bf16[3,1024,128]{2,1,0:T(8,128)(2,1)S(1)}, bf16[1024,128]{1,0:T(8,128)(2,1)S(1)}, bf16[1024,128]{1,0:T(8...) custom-call(bf16[4,256,1536]{2,1,0:T(8,128)(2,1)} %copy-done.8, ...), custom_call_target="tpu_custom_call" | custom-call | flops 5000000000 | bytes 12058632 | tf_op jit(solution)/shard_map/attend/pallas_call | solution.py:147
  152.6 1.6 copy-done.19
  154.2 1.1 copy-done.20
  158.2 52.8 %mix.1 = (f32[256,1536]{1,0:T(8,128)S(1)}, bf16[4,256,1536]{2,1,0:T(8,128)(2,1)S(1)}, bf16[256,1536]{1,0:T(8,128)(2,1)S(1)}) custom-call(bf16[256,1536]{1,0:T(8,128)(2,1)S(1)} %copy-done.3, bf16[4,256,384]{2,1,0:T(8,128)(2,1)S(1)} %get-tuple-element.45.att_ref, bf16[1536,2304]{1,0:T(8,128)(2,1)S(1)} %copy-done.2, f32[40,1536]{1,0:T(8,128)S(1)} %get-tuple-element.44.small_ref), custom_call_target="tpu_custom_call" | custom-call | flops 2000000000 | bytes 8896512 | tf_op jit(solution)/shard_map/mix/pallas_call | solution.py:147
  211.1 1.7 copy-done.9
  212.7 1.1 copy-done.10
  213.9 71.0 %experts.1 = (bf16[8,15,192,512]{3,2,1,0:T(8,128)(2,1)}, bf16[4,256,1536]{2,1,0:T(8,128)(2,1)}, bf16[4,256,1536]{2,1,0:T(8,128)(2,1)}, f32[4,8,256]{2,1,0:T(8,128)}) custom-call(s32[1]{0:T(128)} %bitcast.3.member_ref, f32[4,32,256]{2,1,0:T(8,128)} %copy-done.13, f32[40,1536]{1,0:T(8,128)} %copy-done.6, bf16[4,256,1536]{2,1,0:T(8,128)(2,1)} %copy-done.9, ...), custom_call_target="tpu_custom_call" | custom-call | flops 40000000000 | bytes 60000000 | tf_op jit(solution)/shard_map/experts/pallas_call | solution.py:723
  285.7 110.2 %give_back.1 = (f32[256,1536]{1,0:T(8,128)S(1)}, bf16[4,256,384]{2,1,0:T(8,128)(2,1)S(1)}, bf16[1536,1536]{1,0:T(8,128)(2,1)}, f32[40,1536]{1,0:T(8,128)S(1)}) custom-call(bf16[4,256,1536]{2,1,0:T(8,128)(2,1)} %get-tuple-element.48.parts_ref, f32[4,8,256]{2,1,0:T(8,128)S(1)} %copy-done.18, f32[32,256]{1,0:T(8,128)S(1)} %convert_bitcast_fusion.chosen_ref, ...), custom_call_target="tpu_custom_call" | custom-call | flops 4000000000 | bytes 14467072 | tf_op jit(solution)/shard_map/give_back/pallas_call | solution.py:147
  395.9 1.1 copy-done.15
  398.6 121.6 %attend_back.1 = (bf16[256,1536]{1,0:T(8,128)(2,1)}, bf16[256,1536]{1,0:T(8,128)(2,1)}, bf16[1536,768]{1,0:T(8,128)(2,1)}) custom-call(bf16[3,1024,128]{2,1,0:T(8,128)(2,1)} %copy-done.21, bf16[1024,128]{1,0:T(8,128)(2,1)} %copy-done.22, bf16[1024,128]{1,0:T(8,128)(2,1)} %copy-done.23, f32[8,1024]{1,0:T(8,128)} %copy-done.24, f32[3,1024,128]{2,1,0:T(8,128)} %copy-done.20, ...), custom_call_target="tpu_custom_call" | custom-call | flops 10000000000 | bytes 22544392 | tf_op jit(solution)/shard_map/attend_back/pallas_call | solution.py:147
  520.9 45.2 %reduce-scatter.4.cloned.1.call-done = bf16[1,192,768]{2,1,0:T(8,128)(2,1)} async-done(((bf16[8,192,768]{2,1,0:T(8,128)(2,1)}), bf16[1,192,768]{2,1,0:T(8,128)(2,1)}) %reduce-scatter.4.cloned.1.call-update) | async-done | bytes 294928 | tf_op jit(solution)/shard_map/reduce_scatter | solution.py:825
  566.2 57.6 %reduce-scatter.6.cloned.1.call-done = bf16[1,192,1536]{2,1,0:T(8,128)(2,1)} async-done(((bf16[8,192,1536]{2,1,0:T(8,128)(2,1)}), bf16[1,192,1536]{2,1,0:T(8,128)(2,1)}) %reduce-scatter.6.cloned.1.call-update) | async-done | bytes 589840 | tf_op jit(solution)/shard_map/reduce_scatter | solution.py:820
  624.6 31.1 %all-gather.6.cloned.1.call-done = bf16[4,192,768]{2,1,0:T(8,128)(2,1)} async-done(((bf16[1,192,768]{2,1,0:T(8,128)(2,1)}), bf16[4,192,768]{2,1,0:T(8,128)(2,1)}) %all-gather.6.cloned.1.call-update) | async-done | bytes 1179664 | tf_op jit(solution)/shard_map/all_gather | solution.py:827
  655.7 1.5 convert_element_type.44
  657.2 1.2 copy.82
  661.6 34.7 %all-reduce.5.cloned.1.call-done = bf16[192,1536]{1,0:T(8,128)(2,1)} async-done(((bf16[192,1536]{1,0:T(8,128)(2,1)}), bf16[192,1536]{1,0:T(8,128)(2,1)}) %all-reduce.5.cloned.1.call-update) | async-done | bytes 589840 | tf_op jit(solution)/shard_map/psum | solution.py:826
  696.3 2.2 convert_element_type.45
  698.5 149.8 %reduce-scatter.8.cloned.1.call-done = bf16[1,15,192,512]{3,2,1,0:T(8,128)(2,1)} async-done(((bf16[8,15,192,512]{3,2,1,0:T(8,128)(2,1)}), bf16[1,15,192,512]{3,2,1,0:T(8,128)(2,1)}) %reduce-scatter.8.cloned.1.call-update) | async-done | bytes 2949136 | tf_op jit(solution)/shard_map/reduce_scatter | solution.py:813
  848.3 1.5 slice.63
  849.7 1.4 copy.88
  851.1 2.4 reshape.107
  853.5 2.6 convert_element_type.46
  856.2 2.3 slice_bitcast_fusion
  858.5 0.9 copy.94
  859.4 0.9 copy.95
  (93 shorter events, 15.5 us)
Async XLA Ops:
  7.2 2.6 copy-start
  7.2 5.5 copy-start.25
  7.2 75.6 %all-gather.8.cloned.1.call-start = ((), (), s32[]{:S(2)}) async-start(), calls=%async_computation.8 | async-start | bytes 7962624 | tf_op jit(solution)/shard_map/all_gather | solution.py:788
  12.6 201.2 %all-gather.10.cloned.1.call-start = ((), (), s32[]{:S(2)}) async-start(), calls=%async_computation.9 | async-start | bytes 26542080 | tf_op jit(solution)/shard_map/all_gather | solution.py:793
  17.1 1.1 copy-start.3
  17.1 65.7 %copy-start.14 = (s32[1,2]{1,0:T(1,128)S(1)}, s32[1,2]{1,0:T(1,128)}, u32[]{:S(2)}) copy-start(s32[1,2]{1,0:T(1,128)} %starts_ref.3) | copy-start | bytes 28
  17.1 549.0 %reduce-scatter.4.cloned.1.call-start = ((), (), s32[]{:S(2)}) async-start(), calls=%async_computation.3 | async-start | bytes 2654208 | tf_op jit(solution)/shard_map/reduce_scatter | solution.py:825
  78.3 1.6 copy-start.8
  79.9 2.9 copy-start.13
  82.7 69.8 %copy-start.4 = (f32[1024,128]{1,0:T(8,128)}, f32[1024,128]{1,0:T(8,128)S(1)}, u32[]{:S(2)}) copy-start(f32[1024,128]{1,0:T(8,128)S(1)} %get-tuple-element.74.cos_ref) | copy-start | bytes 1572868
  82.8 69.8 %copy-start.5 = (f32[1024,128]{1,0:T(8,128)}, f32[1024,128]{1,0:T(8,128)S(1)}, u32[]{:S(2)}) copy-start(f32[1024,128]{1,0:T(8,128)S(1)} %get-tuple-element.75.sin_ref) | copy-start | bytes 1572868
  82.8 1.5 copy-start.11
  84.3 74.0 %copy-start.2 = (bf16[1536,2304]{1,0:T(8,128)(2,1)S(1)}, bf16[1536,2304]{1,0:T(8,128)(2,1)}, u32[]{:S(2)}) copy-start(bf16[1536,2304]{1,0:T(8,128)(2,1)} %all-gather.8.cloned.1.call-done.packed_ref) | copy-start | bytes 21233668
  152.6 1.6 copy-start.19
  154.2 1.1 copy-start.20
  155.3 0.9 copy-start.21
  156.9 0.7 copy-start.23
  158.2 52.8 %copy-start.6 = (f32[40,1536]{1,0:T(8,128)}, f32[40,1536]{1,0:T(8,128)S(1)}, u32[]{:S(2)}) copy-start(f32[40,1536]{1,0:T(8,128)S(1)} %get-tuple-element.44.small_ref) | copy-start | bytes 737284
  211.1 1.7 copy-start.9
  212.7 1.1 copy-start.10
  213.9 71.0 %copy-start.7 = (f32[40,1536]{1,0:T(8,128)S(1)}, f32[40,1536]{1,0:T(8,128)}, u32[]{:S(2)}) copy-start(f32[40,1536]{1,0:T(8,128)} %copy-done.6) | copy-start | bytes 737284
  213.9 71.0 %copy-start.12 = (bf16[256,1536]{1,0:T(8,128)(2,1)S(1)}, bf16[256,1536]{1,0:T(8,128)(2,1)}, u32[]{:S(2)}) copy-start(bf16[256,1536]{1,0:T(8,128)(2,1)} %cot_ref.3) | copy-start | bytes 2359300
  284.9 0.8 copy-start.18
  395.9 1.1 copy-start.15
  397.0 0.9 copy-start.16
  520.3 103.5 %reduce-scatter.6.cloned.1.call-start = ((), (), s32[]{:S(2)}) async-start(), calls=%async_computation.5 | async-start | bytes 5308416 | tf_op jit(solution)/shard_map/reduce_scatter | solution.py:820
  520.8 134.8 %all-gather.6.cloned.1.call-start = ((), (), s32[]{:S(2)}) async-start(), calls=%async_computation.4 | async-start | bytes 1474560 | tf_op jit(solution)/shard_map/all_gather | solution.py:827
  566.2 130.1 %all-reduce.5.cloned.1.call-start = ((), (), s32[]{:S(2)}) async-start(), calls=%async_computation.6 | async-start | bytes 1179648 | tf_op jit(solution)/shard_map/psum | solution.py:826
  623.8 224.5 %reduce-scatter.8.cloned.1.call-start = ((), (), s32[]{:S(2)}) async-start(), calls=%async_computation.7 | async-start | bytes 26542080 | tf_op jit(solution)/shard_map/reduce_scatter | solution.py:813
  856.2 2.4 copy-start.27
  856.2 3.2 copy-start.26
  856.2 4.1 copy-start.1
  (4 other events, 2.7 us)
Sparse Core Ops, SparseCore 0:
  12.7 51.5 all-gather.7
  66.2 118.6 all-gather.9
  520.4 45.7 reduce-scatter.3
  569.8 53.9 reduce-scatter.5
  625.2 30.4 all-gather.5
  657.9 38.3 all-reduce.4
  699.9 148.2 reduce-scatter.7

commit v2 on v1

--- a/solution.py
+++ b/solution.py
@@ -2,6 +2,7 @@
 
 import jax
 import jax.numpy as jnp
+import numpy as np
 from jax import lax
 from jax.experimental import pallas as pl
 from jax.experimental.pallas import tpu as pltpu
@@ -46,10 +47,33 @@
     pl.semaphore_wait(barrier, n - 1)
 
 
-def remote(src, dst, send, recv, target):
+def barrier_plane(n, me, chips, place):
+    barrier = pltpu.get_barrier_semaphore()
+    core, chip = place % 2, place // 2
+    for d in range(n):
+
+        @pl.when(d != me)
+        def _():
+            pl.semaphore_signal(barrier, inc=1, device_id={"expert": d}, device_id_type=MESH)
+
+    pl.semaphore_signal(
+        barrier, inc=1, device_id={"dp": place + 1 - 2 * core}, device_id_type=MESH
+    )
+    for c in range(chips):
+
+        @pl.when(c != chip)
+        def _():
+            pl.semaphore_signal(
+                barrier, inc=1, device_id={"dp": 2 * c + core}, device_id_type=MESH
+            )
+
+    pl.semaphore_wait(barrier, n - 1 + chips)
+
+
+def remote(src, dst, send, recv, target, axis="expert"):
     return pltpu.make_async_remote_copy(
         src_ref=src, dst_ref=dst, send_sem=send, recv_sem=recv,
-        device_id={"expert": target}, device_id_type=MESH,
+        device_id={axis: target}, device_id_type=MESH,
     )
 
 
@@ -130,6 +154,54 @@
                 )
                 desc.wait_send()
                 desc.wait_recv()
+
+
+class PairReduce:
+    def __init__(self, chips, place, parts, first, sums, second, sems):
+        self.chips, self.core, self.chip = chips, place % 2, place // 2
+        self.partner = place + 1 - 2 * self.core
+        self.parts, self.first, self.sums, self.second = parts, first, sums, second
+        self.sems = sems
+
+    def near(self, c):
+        s, r, _, _ = self.sems
+        source = self.parts.at[2 * c + 1 - self.core]
+        return remote(source, self.first.at[c], s.at[c], r.at[c], self.partner, "dp")
+
+    def across(self, c, slot):
+        _, _, s, r = self.sems
+        return remote(
+            self.sums.at[c], self.second.at[slot], s.at[c], r.at[slot], 2 * c + self.core, "dp"
+        )
+
+    def start(self):
+        for c in range(self.chips):
+            self.near(c).start()
+
+    def middle(self):
+        for c in range(self.chips):
+            self.near(c).wait_recv()
+            mine = self.parts[2 * c + self.core].astype(F32)
+            self.sums[c] = (mine + self.first[c].astype(F32)).astype(BF16)
+
+            @pl.when(c != self.chip)
+            def _():
+                self.across(c, self.chip).start()
+
+    def finish(self, total):
+        total[...] = self.sums[self.chip].astype(F32)
+        for c in range(self.chips):
+            self.near(c).wait_send()
+
+            @pl.when(c != self.chip)
+            def _():
+                self.across(c, self.chip).wait_send()
+                self.across(c, c).wait_recv()
+                total[...] += self.second[c].astype(F32)
+
+
+def pair_sems(chips):
+    return [pltpu.SemaphoreType.DMA((chips,)) for _ in range(4)]
 
 
 def chain_sems(n):
@@ -161,35 +233,23 @@
     )(*args)
 
 
-def gather_kernel(n, tokens_ref, chosen_ref, all_ref, every_ref, source, s0, r0, s1, r1):
+def gather_kernel(n, tokens_ref, all_ref, s0, r0):
     me = lax.axis_index("expert")
     barrier_all(n, me)
     all_ref[me] = tokens_ref[...]
     chain = ChainGather(n, me, all_ref, s0, r0)
-    chain.step(0)
-    every_ref[me] = chosen_ref[...]
-    for d in range(n):
-        source[d] = chosen_ref[...]
-    small = Exchange(n, me, source, every_ref, s1, r1)
-    for d in range(n):
-        small.start(d)
-    for s in range(1, n - 1):
+    for s in range(n - 1):
         chain.step(s)
     chain.finish()
-    small.finish()
-
-
-def gather_tokens(n, tokens, chosen):
+
+
+def gather_tokens(n, tokens):
     rows, width = tokens.shape
     return call(
         functools.partial(gather_kernel, n),
-        [
-            jax.ShapeDtypeStruct((n, rows, width), BF16),
-            jax.ShapeDtypeStruct((n,) + chosen.shape, F32),
-        ],
-        [pltpu.VMEM((n,) + chosen.shape, F32)] + chain_sems(n) + direct_sems(n),
-        1, "gather_tokens", 10**6, 16, (tokens, chosen),
-    )
+        [jax.ShapeDtypeStruct((n, rows, width), BF16)],
+        chain_sems(n), 1, "gather_tokens", 10**6, 16, (tokens,),
+    )[0]
 
 
 def turn(x, cosine, sine):
@@ -220,8 +280,8 @@
 
 def attend_kernel(
     n, kv_local, tokens_ref, packed_ref, cos_ref, sin_ref, starts_ref, cot_ref,
-    norm_ref, q_ref, k_ref, v_ref, lse_ref, out_ref, att_ref, cots_ref, small_ref,
-    w_s, send_att, load, s0, r0, s1, r1,
+    chosen_ref, norm_ref, q_ref, k_ref, v_ref, lse_ref, out_ref, att_ref, cots_ref, small_ref,
+    every_ref, w_s, send_att, send_chosen, load, s0, r0, s1, r1, s2, r2,
 ):
     me = lax.axis_index("expert")
     per_key, length, tile = q_ref.shape
@@ -235,6 +295,11 @@
     chain = ChainGather(n, me, cots_ref, s0, r0)
     chain.step(0)
     swap = Exchange(n, me, send_att, att_ref, s1, r1)
+    choice = Exchange(n, me, send_chosen, every_ref, s2, r2)
+    every_ref[me] = chosen_ref[...]
+    for d in range(n):
+        send_chosen[d] = chosen_ref[...]
+        choice.start(d)
     pieces = starts_ref.shape[1]
     weights.wait()
     small = w_s[:, wide - 128 :].astype(F32).T
@@ -295,11 +360,12 @@
         if i + 2 < n - 1:
             chain.step(i + 2)
     att_ref[me] = send_att[me]
+    choice.finish()
     chain.finish()
     swap.finish()
 
 
-def attend(n, kv_local, tokens_all, packed, cosine, sine, starts, cot):
+def attend(n, kv_local, tokens_all, packed, cosine, sine, starts, cot, chosen):
     rows, width = cot.shape
     length = n * rows
     tile = kv_local * HEAD_SIZE
@@ -319,12 +385,16 @@
             sds((per_key, length, tile), F32),
             sds((n, rows, q_cols), BF16),
             sds((n, rows, width), BF16),
-            sds((8 + 8 * n, width), F32),
+            sds((8 + chosen.shape[0], width), F32),
+            sds((n,) + chosen.shape, F32),
         ],
-        [pltpu.VMEM((width, wide), BF16), pltpu.VMEM((n, rows, q_cols), BF16), DMA]
-        + chain_sems(n)
-        + direct_sems(n),
-        2, "attend", 5 * 10**9, 44, (tokens_all, packed, cosine, sine, starts, cot), (1,),
+        [
+            pltpu.VMEM((width, wide), BF16), pltpu.VMEM((n, rows, q_cols), BF16),
+            pltpu.VMEM((n,) + chosen.shape, F32), DMA,
+        ]
+        + chain_sems(n) + direct_sems(n) + direct_sems(n),
+        2, "attend", 5 * 10**9, 44,
+        (tokens_all, packed, cosine, sine, starts, cot, chosen), (1,),
     )
 
 
@@ -364,53 +434,59 @@
 
 
 class ChainReduce:
-    def __init__(self, n, me, parts, from_left, from_right, send, recv):
+    def __init__(self, n, me, parts, slots, send, recv):
         self.n, self.me, self.parts = n, me, parts
-        self.slots, self.send, self.recv = (from_left, from_right), send, recv
+        self.slots, self.send, self.recv = slots, send, recv
 
     def copy(self, way, s, d, source):
         target = self.me + 1 if way == 0 else self.me - 1
+        slot = d if way == 0 else jnp.where(d == target, self.n, d)
         return remote(
-            source.at[d], self.slots[way].at[d], self.send.at[way, s], self.recv.at[way, s], target
+            source.at[d], self.slots.at[slot], self.send.at[way, s], self.recv.at[way, s], target
         )
 
-    def step(self, s):
-        n, me = self.n, self.me
+    def far(self, way):
+        return self.me if way == 0 else self.n - 1 - self.me
+
+    def step(self, when):
         for way in (0, 1):
-            d = n - 1 - s if way == 0 else s
-            onward = me < d if way == 0 else me > d
-            first = me == 0 if way == 0 else me == n - 1
-            slot = self.slots[way]
-
-            @pl.when(onward & first)
+            far = self.far(way)
+            s = when - far
+            d = self.n - 1 - s if way == 0 else s
+            slots = self.slots
+
+            @pl.when(s >= 0)
             def _():
-                if s > 0:
-                    self.copy(way, s - 1, d, self.parts).wait_send()
-                self.copy(way, s, d, self.parts).start()
-
-            @pl.when(onward & jnp.logical_not(first))
-            def _():
-                self.copy(way, s, d, slot).wait_recv()
-                slot[d] = (slot[d].astype(F32) + self.parts[d].astype(F32)).astype(BF16)
-                if s > 0:
-                    self.copy(way, s - 1, d, slot).wait_send()
-                self.copy(way, s, d, slot).start()
+                @pl.when(far == 0)
+                def _():
+                    self.copy(way, s, d, self.parts).start()
+
+                @pl.when(far > 0)
+                def _():
+                    self.copy(way, s, d, slots).wait_recv()
+                    slots[d] = (slots[d].astype(F32) + self.parts[d].astype(F32)).astype(BF16)
+                    self.copy(way, s, d, slots).start()
+
+            if when > 0:
+
+                @pl.when(s > 0)
+                def _():
+                    self.copy(way, s - 1, d, slots).wait_send()
 
     def finish(self, total):
         n, me = self.n, self.me
         total[...] = self.parts[me].astype(F32)
         for way in (0, 1):
-            last = n - 1 - me if way == 0 else me
-            slot = self.slots[way]
-
-            @pl.when(me > 0 if way == 0 else me < n - 1)
+            far = self.far(way)
+
+            @pl.when(far > 0)
             def _():
-                self.copy(way, last, me, slot).wait_recv()
-                total[...] += slot[me].astype(F32)
-
-            @pl.when(me < n - 1 if way == 0 else me > 0)
+                self.copy(way, n - 1 - far, me, self.slots).wait_recv()
+                total[...] += self.slots[me if way == 0 else n].astype(F32)
+
+            @pl.when(far < n - 1)
             def _():
-                self.copy(way, last - 1, me, slot).wait_send()
+                self.copy(way, n - 2 - far, me, self.slots).wait_send()
 
 
 def rms_back(grad, rows, gain):
@@ -430,7 +506,7 @@
 def return_kernel(
     n, parts_ref, gg_ref, chosen_ref, small_ref, hidden_ref, norm_ref, cot_ref, att_ref, packed_ref,
     grad_ref, ga_ref, o_ref, extra_ref,
-    w_s, from_left, from_right, total, gg_s, send_ga, load, s0, r0, s1, r1, s2, r2,
+    w_s, slots, total, gg_s, send_ga, load, s0, r0, s1, r1, s2, r2,
 ):
     me = lax.axis_index("expert")
     width = w_s.shape[0]
@@ -438,7 +514,7 @@
     weights = pltpu.make_async_copy(packed_ref.at[:, pl.ds(0, width)], w_s, load)
     weights.start()
     barrier_all(n, me)
-    chain = ChainReduce(n, me, parts_ref, from_left, from_right, s0, r0)
+    chain = ChainReduce(n, me, parts_ref, slots, s0, r0)
     chain.step(0)
     gates_swap = Exchange(n, me, gg_ref, gg_s, s1, r1)
     for d in range(n):
@@ -483,7 +559,7 @@
             sds(small.shape, F32),
         ],
         [
-            vm((width, width), BF16), vm((n, rows, width), BF16), vm((n, rows, width), BF16),
+            vm((width, width), BF16), vm((n + 1, rows, width), BF16),
             vm((rows, width), F32), vm(gg.shape, F32), vm((n, rows, q_cols), BF16), DMA,
         ]
         + chain_sems(n) + direct_sems(n) + direct_sems(n),
@@ -493,13 +569,15 @@
 
 
 def attend_back_kernel(
-    n, kv_local, q_ref, k_ref, v_ref, lse_ref, out_ref, ga_ref, starts_ref, cos_ref, sin_ref,
-    norm_ref, packed_ref, tokens_ref, small_ref, grad_ref, hidden_ref, y_ref, extra_ref,
-    output_ref, input_ref, dw_ref,
-    w_s, gq_s, gk_s, gv_s, gqkv_s, ga_s, parts_s, y_left, y_right, b_left, b_right, total, load,
-    s0, r0, s1, r1,
+    n, kv_local, chips, q_ref, k_ref, v_ref, lse_ref, out_ref, ga_ref, starts_ref, cos_ref,
+    sin_ref, norm_ref, packed_ref, tokens_ref, small_ref, grad_ref, extra_ref, o_ref,
+    input_ref, shares_ref, og_ref,
+    w_s, gq_s, gk_s, gv_s, gqkv_s, ga_s, parts_s, b_slots, total, load,
+    o_first, o_sums, o_second, o_total, o_send, o_got, dw_s, w_first, w_sums, w_second, w_total,
+    s1, r1, s2, r2, s3, r3, s4, r4, *sems,
 ):
     me = lax.axis_index("expert")
+    place = lax.axis_index("dp")
     per_key, length, tile = q_ref.shape
     rows = length // n
     q_cols, k_cols = per_key * tile, tile
@@ -509,9 +587,11 @@
     pieces = starts_ref.shape[1]
     weights = pltpu.make_async_copy(packed_ref.at[:, pl.ds(width, wide)], w_s, load)
     weights.start()
-    barrier_all(n, me)
-    y_chain = ChainReduce(n, me, y_ref, y_left, y_right, s0, r0)
-    y_chain.step(0)
+    barrier_plane(n, me, chips, place)
+    o_sum = PairReduce(chips, place, o_ref, o_first, o_sums, o_second, sems[:4])
+    o_sum.start()
+    o_swap = Exchange(n, me, o_send, o_got, s2, r2)
+    o_share = ChainGather(n, me, og_ref, s3, r3)
     gk_s[...] = jnp.zeros_like(gk_s)
     gv_s[...] = jnp.zeros_like(gv_s)
     lane = lax.broadcasted_iota(jnp.int32, (rows, tile), 1)
@@ -557,199 +637,294 @@
                 gq_s[part, at : at + HEAD_SIZE] = (
                     grad_q[:, g * HEAD_SIZE : (g + 1) * HEAD_SIZE] * scale
                 )
-        if i + 1 < n - 1:
-            y_chain.step(i + 1)
+        if i == 0:
+            o_sum.middle()
+        if i == n // 2:
+            o_sum.finish(o_total)
+            piece = width // n
+            for d in range(n):
+                o_send[d] = o_total[:, d * piece : (d + 1) * piece].astype(BF16)
+                o_swap.start(d)
+        if i == n - 1:
+            o_swap.finish()
+            mine = o_send[me].astype(F32)
+            for d in range(n):
+                mine = mine + jnp.where(d == me, 0.0, o_got[d].astype(F32))
+            og_ref[me] = mine.astype(BF16)
+            o_share.step(0)
     gq_s[:, q_cols:] = gk_s[...]
     weights.wait()
     if used < gqkv_s.shape[1]:
         gqkv_s[...] = jnp.zeros_like(gqkv_s)
+    gain = small_ref[:1, :]
+    grad_gain = jnp.zeros_like(gain)
     for i in range(n):
         part = slice(i * rows, (i + 1) * rows)
         qk = turn(gq_s[part, :], cos_ref[part, :], -sin_ref[part, :]).astype(BF16)
         gqkv_s[part, : q_cols + k_cols] = qk
         gqkv_s[part, q_cols + k_cols : used] = gv_s[part, :].astype(BF16)
-        parts_s[i] = dot_t(gqkv_s[part, :], w_s[:, : wide - 128]).astype(BF16)
-    chain = ChainReduce(n, me, parts_s, b_left, b_right, s1, r1)
+        back = dot_t(gqkv_s[part, :], w_s[:, : wide - 128])
+        parts_s[i] = back.astype(BF16)
+        grad_gain = grad_gain + jnp.sum(back * norm_ref[i].astype(F32), axis=0, keepdims=True)
+    chain = ChainReduce(n, me, parts_s, b_slots, s1, r1)
     chain.step(0)
-    y_chain.finish(total)
-    output_ref[...] = (hidden_ref[...] + total[...]).astype(BF16)
     norms = norm_ref[...].reshape(length, width)
-    dw_ref[:, : wide - 128] = tdot(norms, gqkv_s[...]).astype(BF16)
-    for s in range(1, n - 1):
-        chain.step(s)
-    chain.finish(total)
-    grad, grad_gain = rms_back(total[...], tokens_ref[...].astype(F32), small_ref[:1, :])
-    input_ref[...] = (grad_ref[...] + grad).astype(BF16)
+    dw = tdot(norms, gqkv_s[...]).astype(BF16)
+    dw_s[:, :, : wide - 128] = dw.reshape(2 * chips, -1, wide - 128)
     extra = extra_ref[...]
     row = lax.broadcasted_iota(jnp.int32, extra.shape, 0)
-    extra = jnp.where(row == 0, grad_gain, extra)
+    extra = jnp.where(row == 0, grad_gain / gain, extra)
     extra = jnp.concatenate([extra, jnp.zeros((128 - extra.shape[0], width), F32)], axis=0)
-    dw_ref[:, wide - 128 :] = extra.T.astype(BF16)
-
-
-def attend_back(n, kv_local, saved, ga, starts, cosine, sine, norms, packed, tokens, small, grad, hidden, y, extra):
+    dw_s[:, :, wide - 128 :] = extra.T.astype(BF16).reshape(2 * chips, -1, 128)
+    w_sum = PairReduce(chips, place, dw_s, w_first, w_sums, w_second, sems[4:])
+    w_sum.start()
+    for s in range(1, n - 1):
+        o_share.step(s)
+    o_share.finish()
+    w_sum.middle()
+    if n > 2:
+        chain.step(1)
+    w_sum.finish(w_total)
+    shares_ref[me] = w_total[...].astype(BF16)
+    w_share = ChainGather(n, me, shares_ref, s4, r4)
+    w_share.step(0)
+    for s in range(2, n - 1):
+        chain.step(s)
+    for s in range(1, n - 1):
+        w_share.step(s)
+    chain.finish(total)
+    grad, _ = rms_back(total[...], tokens_ref[...].astype(F32), gain)
+    input_ref[...] = (grad_ref[...] + grad).astype(BF16)
+    w_share.finish()
+
+
+def attend_back(
+    n, kv_local, chips, saved, ga, starts, cosine, sine, norms, packed, tokens, small, grad, extra,
+    grad_o,
+):
     q, k, v, lse, out = saved
     rows, width = tokens.shape
     per_key, length, tile = q.shape
     wide = packed.shape[1] - width
     sds, vm = jax.ShapeDtypeStruct, pltpu.VMEM
     qk = (per_key + 1) * tile
-    block = vm((n, rows, width), BF16)
+    shard = width // (2 * chips)
+    across, across_w = vm((chips, shard, width), BF16), vm((chips, shard, wide), BF16)
+    piece = vm((n, shard, width // n), BF16)
     return call(
-        functools.partial(attend_back_kernel, n, kv_local),
-        [sds((rows, width), BF16), sds((rows, width), BF16), sds((width, wide), BF16)],
+        functools.partial(attend_back_kernel, n, kv_local, chips),
+        [
+            sds((rows, width), BF16), sds((n, shard, wide), BF16),
+            sds((n, shard, width // n), BF16),
+        ],
         [
             vm((width, wide), BF16), vm((length, qk), F32), vm((length, tile), F32),
             vm((length, tile), F32), vm((length, wide - 128), BF16), vm((per_key, rows, tile), BF16),
-            block, block, block, block, block, vm((rows, width), F32), DMA,
+            vm((n, rows, width), BF16), vm((n + 1, rows, width), BF16), vm((rows, width), F32), DMA,
+            across, across, across, vm((shard, width), F32), piece, piece,
+            vm((2 * chips, shard, wide), BF16), across_w, across_w, across_w,
+            vm((shard, wide), F32),
         ]
-        + chain_sems(n) + chain_sems(n),
+        + chain_sems(n) + direct_sems(n) + chain_sems(n) + chain_sems(n)
+        + pair_sems(chips) + pair_sems(chips),
         5, "attend_back", 10 * 10**9, 58,
-        (q, k, v, lse, out, ga, starts, cosine, sine, norms, packed, tokens, small, grad, hidden, y, extra),
+        (q, k, v, lse, out, ga, starts, cosine, sine, norms, packed, tokens, small, grad, extra,
+         grad_o.reshape(2 * chips, shard, width)),
         (10,),
     )
 
 
 def expert_kernel(
-    member_ref, chosen_ref, small_ref, n2_ref, cot_ref, wg_ref, wu_ref, wd_ref,
-    dw_ref, y_ref, gx_ref, gg_ref,
-    xe, ge, gr, act_s, ggp_s, gup_s, pick_s, gated_s, grows_s, gate_s, rank_s,
+    n, chosen_ref, small_ref, n2_ref, cot_ref, hidden_ref, wg_ref, wu_ref, wd_ref,
+    dw_ref, gx_ref, gg_ref, output_ref,
+    x_s, g_s, slope_s, silu_s, act_s, gact_s, ggp_s, gup_s, pick_s, mix_s, y_s, y_slots,
+    total, gate_s, rank_s, s0, r0,
 ):
-    e, phase = pl.program_id(0), pl.program_id(1)
-    groups, rows, width = n2_ref.shape
-    cap = xe.shape[0] // groups
-    ff = act_s.shape[1]
+    me = lax.axis_index("expert")
+    _, rows, width = n2_ref.shape
+    local, tall, ff = act_s.shape
+    cap = tall // n
     shards = wg_ref.shape[0]
     depth = ff // shards
     blocks = width // ff
+    at = pl.program_id(0)
+    later = jnp.maximum(at - local, 0)
+    e = jnp.where(at < local, at, later // 3)
+    phase = jnp.where(at < local, -1, later % 3)
+    mine = me * gg_ref.shape[1] + e
+    where = pl.ds(pl.multiple_of(e * cap, cap), cap)
+    chain = ChainReduce(n, me, y_s, y_slots, s0, r0)
 
     def whole(ref):
         return ref[...].reshape(width, ff)
 
     def down(j):
-        return wd_ref[:, 0, j * depth:(j + 1) * depth, :].reshape(ff, ff)
-
-    @pl.when((phase == 0) & (e == 0))
+        return wd_ref[:, 0, j * depth : (j + 1) * depth, :].reshape(ff, ff)
+
+    def gate_column(s, pick):
+        return jnp.sum(jnp.where(pick, gate_s[s, pl.ds(mine, 1), :], 0.0), axis=1, keepdims=True)
+
+    @pl.when(at == 0)
     def _():
+        barrier_all(n, me)
         before = lax.broadcasted_iota(jnp.int32, (rows, rows), 0)
         upto = jnp.where(before <= lax.broadcasted_iota(jnp.int32, (rows, rows), 1), 1.0, 0.0)
         router = small_ref[8:, :].astype(BF16)
-        for s in range(groups):
+        for s in range(n):
             chosen = chosen_ref[s]
             gate_s[s] = softmax_chosen(dot_t(router, n2_ref[s]), chosen)
             count = dot(chosen.astype(BF16), upto.astype(BF16))
             rank_s[s] = jnp.where(chosen > 0.0, count - 1.0, -1.0).astype(jnp.int32)
         gg_ref[...] = jnp.zeros_like(gg_ref)
 
-    @pl.when(phase == 0)
+    @pl.when(phase < 0)
     def _():
-        mine = member_ref[0] * gg_ref.shape[1] + e
-        picks, cols = [], []
         slot = lax.broadcasted_iota(jnp.int32, (cap, rows), 0)
-        for s in range(groups):
+        cols = []
+        for s in range(n):
             pick = slot == rank_s[s, pl.ds(mine, 1), :]
-            picks.append(pick)
             hot = jnp.where(pick, 1.0, 0.0).astype(BF16)
-            pick_s[s, pl.ds(pl.multiple_of(e * cap, cap), cap), :] = hot
-            col = jnp.sum(jnp.where(pick, gate_s[s, pl.ds(mine, 1), :], 0.0), axis=1, keepdims=True)
-            cols.append(col)
-            part = slice(s * cap, (s + 1) * cap)
-            xe[part, :] = dot(hot, n2_ref[s]).astype(BF16)
-            g = dot(hot, cot_ref[s])
-            ge[part, :] = g.astype(BF16)
-            gr[part, :] = (col * g).astype(BF16)
-        x = xe[...]
+            pick_s[s, where, :] = hot
+            cols.append(gate_column(s, pick))
+            x_s[s * cap : (s + 1) * cap, :] = dot(hot, n2_ref[s]).astype(BF16)
+        x = x_s[...]
         gp = dot(x, whole(wg_ref))
         up = dot(x, whole(wu_ref))
         sigma = jax.nn.sigmoid(gp)
         silu = gp * sigma
         act = (silu * up).astype(BF16)
-        act_s[...] = act
-        grad_act = jnp.zeros_like(gp)
-        gate_sums = [jnp.zeros((cap, 1), F32) for _ in range(groups)]
+        act_s[e] = act
+        silu_s[e] = silu.astype(BF16)
+        slope_s[e] = (up * sigma * (1.0 + gp * (1.0 - sigma))).astype(BF16)
         for j in range(blocks):
             lanes = slice(j * ff, (j + 1) * ff)
-            w = down(j)
-            res = dot(act, w).astype(BF16).astype(F32)
-            grad_act = grad_act + dot_t(gr[:, lanes], w)
-            for s in range(groups):
-                part = slice(s * cap, (s + 1) * cap)
-                r = res[part, :]
-                gated_s[s, pl.ds(pl.multiple_of(e * cap, cap), cap), lanes] = (cols[s] * r).astype(BF16)
-                gate_sums[s] = gate_sums[s] + jnp.sum(ge[part, lanes].astype(F32) * r, axis=1, keepdims=True)
-        for s in range(groups):
-            gg_ref[s, pl.ds(e, 1), :] = jnp.sum(jnp.where(picks[s], gate_sums[s], 0.0), axis=0, keepdims=True)
-        ggp = (grad_act * up * sigma * (1.0 + gp * (1.0 - sigma))).astype(BF16)
+            res = dot(act, down(j)).astype(BF16).astype(F32)
+            for s in range(n):
+                mix_s[s, where, lanes] = (cols[s] * res[s * cap : (s + 1) * cap, :]).astype(BF16)
+
+    @pl.when(at == local - 1)
+    def _():
+        for s in range(n):
+            y_s[s] = tdot(pick_s[s], mix_s[s]).astype(BF16)
+
+    for s in range(n - 1):
+
+        @pl.when(at == local + s * 3 * local // (n - 1))
+        def _():
+            chain.step(s)
+
+    @pl.when(phase == 0)
+    def _():
+        for s in range(n):
+            hot = pick_s[s, where, :]
+            x_s[s * cap : (s + 1) * cap, :] = dot(hot, n2_ref[s]).astype(BF16)
+            g_s[s * cap : (s + 1) * cap, :] = dot(hot, cot_ref[s]).astype(BF16)
+        grad_act = jnp.zeros((tall, ff), F32)
+        for j in range(blocks):
+            grad_act = grad_act + dot_t(g_s[:, j * ff : (j + 1) * ff], down(j))
+        act = act_s[e].astype(F32)
+        sums = jnp.sum(act * grad_act, axis=1, keepdims=True)
+        cols = []
+        for s in range(n):
+            pick = pick_s[s, where, :].astype(F32) > 0.5
+            cols.append(gate_column(s, pick))
+            part = sums[s * cap : (s + 1) * cap, :]
+            gg_ref[s, pl.ds(e, 1), :] = jnp.sum(jnp.where(pick, part, 0.0), axis=0, keepdims=True)
+        col = jnp.concatenate(cols, axis=0)
+        grad_act = grad_act * col
+        gact_s[...] = (act * col).astype(BF16)
+        ggp = (grad_act * slope_s[e].astype(F32)).astype(BF16)
         ggp_s[...] = ggp
-        gup_s[...] = (grad_act * silu).astype(BF16)
-        dw_ref[...] = tdot(xe[...], ggp).astype(BF16).reshape(dw_ref.shape)
+        gup_s[...] = (grad_act * silu_s[e].astype(F32)).astype(BF16)
+        dw_ref[...] = tdot(x_s[...], ggp).astype(BF16).reshape(dw_ref.shape)
 
     @pl.when(phase == 1)
     def _():
-        dw_ref[...] = tdot(xe[...], gup_s[...]).astype(BF16).reshape(dw_ref.shape)
-        grows = (dot_t(ggp_s[...], whole(wg_ref)) + dot_t(gup_s[...], whole(wu_ref))).astype(BF16)
-        for s in range(groups):
-            grows_s[s, pl.ds(pl.multiple_of(e * cap, cap), cap), :] = grows[s * cap:(s + 1) * cap, :]
+        dw_ref[...] = tdot(x_s[...], gup_s[...]).astype(BF16).reshape(dw_ref.shape)
+        grows = dot_t(ggp_s[...], whole(wg_ref)) + dot_t(gup_s[...], whole(wu_ref))
+        grows = grows.astype(BF16)
+        for s in range(n):
+            mix_s[s, where, :] = grows[s * cap : (s + 1) * cap, :]
 
     @pl.when(phase == 2)
     def _():
         for j in range(blocks):
-            lanes = slice(j * ff, (j + 1) * ff)
-            dw_ref[:, 0, j * depth:(j + 1) * depth, :] = tdot(act_s[...], gr[:, lanes]).astype(BF16).reshape(shards, depth, ff)
-
-    @pl.when((phase == 2) & (e == pl.num_programs(0) - 1))
+            grad = tdot(gact_s[...], g_s[:, j * ff : (j + 1) * ff]).astype(BF16)
+            dw_ref[:, 0, j * depth : (j + 1) * depth, :] = grad.reshape(shards, depth, ff)
+
+    @pl.when(at == 4 * local - 1)
     def _():
-        for s in range(groups):
-            y_ref[s] = tdot(pick_s[s], gated_s[s]).astype(BF16)
-            gx_ref[s] = tdot(pick_s[s], grows_s[s]).astype(BF16)
-
-
-def experts(member, chosen, small, n2, cot, w):
-    groups, rows, width = n2.shape
+        for s in range(n):
+            gx_ref[s] = tdot(pick_s[s], mix_s[s]).astype(BF16)
+        chain.finish(total)
+        output_ref[...] = (hidden_ref[...] + total[...]).astype(BF16)
+
+
+def experts(n, chosen, small, n2, cot, hidden, w):
+    _, rows, width = n2.shape
     shards, local, depth, ff = w.shape
     local = local // 3
-    cap = rows * TOPK * 5 // (4 * local * groups)
-    tall = groups * cap
-    padded = chosen.shape[1] // groups
+    cap = rows * TOPK * 5 // (4 * local * n)
+    tall = n * cap
+    padded = chosen.shape[1] // n
     once = pl.Buffered(1)
 
     def const(shape):
-        return pl.BlockSpec(shape, lambda e, p: (0,) * len(shape), pipeline_mode=once)
+        return pl.BlockSpec(shape, lambda i: (0,) * len(shape), pipeline_mode=once)
+
+    def place(i):
+        later = jnp.maximum(i - local, 0)
+        return jnp.where(i < local, i, later // 3), later % 3
 
     def weight(k):
-        return pl.BlockSpec((shards, 1, depth, ff), lambda e, p: (0, k * local + e, 0, 0))
+        return pl.BlockSpec((shards, 1, depth, ff), lambda i: (0, k * local + place(i)[0], 0, 0))
+
+    def grads(i):
+        later = jnp.maximum(i - local, 0)
+        return (0, later % 3 * local + later // 3, 0, 0)
 
     sds, vm = jax.ShapeDtypeStruct, pltpu.VMEM
+    saved, half = vm((local, tall, ff), BF16), vm((tall, ff), BF16)
     return pl.pallas_call(
-        expert_kernel,
-        grid=(local, 3),
+        functools.partial(expert_kernel, n),
+        grid=(4 * local,),
         in_specs=[
-            pl.BlockSpec(memory_space=pltpu.SMEM), const(chosen.shape), const(small.shape),
-            const(n2.shape), const(n2.shape), weight(0), weight(1), weight(2),
+            const(chosen.shape), const(small.shape), const(n2.shape), const(n2.shape),
+            const(hidden.shape), weight(0), weight(1), weight(2),
         ],
         out_specs=[
-            pl.BlockSpec((shards, 1, depth, ff), lambda e, p: (0, p * local + e, 0, 0)),
-            const(n2.shape), const(n2.shape), const((groups, padded, rows)),
+            pl.BlockSpec((shards, 1, depth, ff), grads),
+            const(n2.shape), const((n, padded, rows)), const(hidden.shape),
         ],
         out_shape=[
-            sds(w.shape, BF16), sds(n2.shape, BF16), sds(n2.shape, BF16),
-            sds((groups, padded, rows), F32),
+            sds(w.shape, BF16), sds(n2.shape, BF16), sds((n, padded, rows), F32),
+            sds(hidden.shape, BF16),
         ],
         scratch_shapes=[
-            vm((tall, width), BF16), vm((tall, width), BF16), vm((tall, width), BF16),
-            vm((tall, ff), BF16), vm((tall, ff), BF16), vm((tall, ff), BF16),
-            vm((groups, local * cap, rows), BF16), vm((groups, local * cap, width), BF16),
-            vm((groups, local * cap, width), BF16), vm(chosen.shape, F32),
-            vm(chosen.shape, jnp.int32),
-        ],
+            vm((tall, width), BF16), vm((tall, width), BF16), saved, saved, saved, half, half, half,
+            vm((n, local * cap, rows), BF16), vm((n, local * cap, width), BF16), vm(n2.shape, BF16),
+            vm((n + 1, rows, width), BF16), vm(hidden.shape, F32), vm(chosen.shape, F32), vm(chosen.shape, jnp.int32),
+        ]
+        + chain_sems(n),
         compiler_params=pltpu.CompilerParams(
-            vmem_limit_bytes=60 * 1024 * 1024, dimension_semantics=("arbitrary", "arbitrary")
+            collective_id=6, has_side_effects=True, vmem_limit_bytes=60 * 1024 * 1024,
+            dimension_semantics=("arbitrary",),
         ),
         cost_estimate=pl.CostEstimate(
             flops=40 * 10**9, transcendentals=0, bytes_accessed=60 * 10**6
         ),
         name="experts",
-    )(member, chosen, small, n2, cot, w, w, w)
+    )(chosen, small, n2, cot, hidden, w, w, w)
+
+
+def rotary_tables(length):
+    half = HEAD_SIZE // 2
+    freqs = THETA ** (-(np.arange(half, dtype=np.float32) * 2.0 / HEAD_SIZE)).astype(np.float32)
+    angles = np.arange(length, dtype=np.float32)[:, None] * freqs[None, :]
+    cosine, sine = np.cos(angles), np.sin(angles)
+    cosine = np.concatenate([cosine, cosine, cosine, cosine], axis=1)
+    sine = np.concatenate([-sine, sine, -sine, sine], axis=1)
+    return jnp.asarray(cosine, F32), jnp.asarray(sine, F32)
 
 
 def per_device(
@@ -795,36 +970,29 @@
     hot = routes[:, :, None] == jnp.arange(n * local, dtype=jnp.int32)
     chosen = jnp.any(hot, axis=1).astype(F32).T.reshape(n, local, rows)
     chosen = jnp.pad(chosen, ((0, 0), (0, padded - local), (0, 0))).reshape(n * padded, rows)
-    half = HEAD_SIZE // 2
-    freqs = THETA ** (-(jnp.arange(half, dtype=F32) * 2.0 / HEAD_SIZE))
-    angles = jnp.arange(length, dtype=jnp.int32).astype(F32)[:, None] * freqs[None, :]
-    cosine, sine = jnp.cos(angles), jnp.sin(angles)
-    cosine = jnp.concatenate([cosine, cosine, cosine, cosine], axis=1)
-    sine = jnp.concatenate([-sine, sine, -sine, sine], axis=1)
-
-    tokens_all, chosen_all = gather_tokens(n, tokens, chosen)
-    norms, q, k, v, lse, out, att, cots, small = attend(
-        n, kv_local, tokens_all, packed, cosine, sine, starts, cotangent
+    cosine, sine = rotary_tables(length)
+    chips = lax.axis_size("dp") // 2
+
+    tokens_all = gather_tokens(n, tokens)
+    norms, q, k, v, lse, out, att, cots, small, chosen_all = attend(
+        n, kv_local, tokens_all, packed, cosine, sine, starts, cotangent, chosen
     )
     hidden, twos, two = mix(n, tokens, att, packed, small)
-    grad_experts, y, back, gg = experts(
-        member.astype(jnp.int32)[None], chosen_all, small, twos, cots, experts_w
-    )
-    expert_grads = lax.psum_scatter(grad_experts, "dp", scatter_dimension=0).astype(F32)
+    grad_experts, back, gg, output = experts(n, chosen_all, small, twos, cots, hidden, experts_w)
+    expert_grads = lax.psum_scatter(grad_experts, "dp", scatter_dimension=0)
+    grad_hidden, ga, grad_o, extra = give_back(
+        n, back, gg, chosen, small, hidden, two, cotangent, att, packed
+    )
+    input_grad, shares, o_grad = attend_back(
+        n, kv_local, chips, (q, k, v, lse, out), ga, starts, cosine, sine, norms, packed, tokens,
+        small, grad_hidden, extra, grad_o,
+    )
+    expert_grads = expert_grads.astype(F32)
     gate_grad, up_grad = expert_grads[:local], expert_grads[local : 2 * local]
     down_grad = expert_grads[2 * local :].reshape(local, blocks, depth, ff)
     down_grad = down_grad.transpose(0, 2, 1, 3).reshape(local, depth, width)
-    grad_hidden, ga, grad_o, extra = give_back(
-        n, back, gg, chosen, small, hidden, two, cotangent, att, packed
-    )
-    grad_o = lax.psum_scatter(grad_o.reshape(-1, shard, width), "dp", scatter_dimension=0)
-    output, input_grad, grad_w = attend_back(
-        n, kv_local, (q, k, v, lse, out), ga, starts, cosine, sine, norms, packed, tokens, small,
-        grad_hidden, hidden, y, extra,
-    )
-    grad_w = lax.psum_scatter(grad_w.reshape(-1, shard, wide), "dp", scatter_dimension=0)
-    o_grad = lax.psum(grad_o, "expert").astype(F32)
-    shares = lax.all_gather(grad_w, "expert").astype(F32)
+    o_grad = o_grad.astype(F32).transpose(1, 0, 2).reshape(shard, width)
+    shares = shares.astype(F32)
     q_grad = shares[:, :, :q_cols].transpose(1, 0, 2).reshape(shard, -1)
     k_grad = shares[:, :, q_cols : q_cols + k_cols].transpose(1, 0, 2).reshape(shard, -1)
     v_grad = shares[:, :, q_cols + k_cols : used].transpose(1, 0, 2).reshape(shard, -1)

time: 872 us -> 562 us (0.64)
  waiting for transfers between devices: 320 us -> 0.07 us
  Pallas kernels: 484 us -> 493 us
    reduce_scatter x3 -> x1, waiting for transfers between devices: 253 us -> 0.01 us  [per_device(): expert_grads = lax.psum_scatter(grad_experts, 'dp', scatter_dimension=0)]
    psum x1 -> x0, waiting for transfers between devices: 34.7 us -> none  [per_device(): o_grad = lax.psum(grad_o, 'expert').astype(F32)]
    all_gather x1 -> x0, waiting for transfers between devices: 31.1 us -> none  [per_device(): shares = lax.all_gather(grad_w, 'expert').astype(F32)]
    pallas_call x1, Pallas kernels: 71 us -> 93.1 us  [experts(): pl.pallas_call(functools.partial(expert_kernel, n), grid=(4 * local,), in...]
    pallas_call x5, Pallas kernels: 413 us -> 400 us  [call(): pl.pallas_call(kernel, in_specs=[anywhere if j in far else smem if a.dtyp...]
    unnamed x61 -> x65, local copies, waits for them, and re-layouts: 17.9 us -> 19.4 us
  transfers between devices with their start and end apart: 7 -> 3, of which waited for: 5 -> 0; matrix products, arithmetic and copies ran while one was open for 2% -> 2% of each run, Pallas kernels for 21% -> 72%
where the time goes in v2:
time: 562 us; the launch traced here: 553 us
  Pallas kernels  493 us (88%)
  local copies, waits for them, and re-layouts  38.6 us (7%)
  between operations  14.6 us (3%)
  other arithmetic  6.18 us (1%)
    pallas_call x5, Pallas kernels, call(): pl.pallas_call(kernel, in_specs=[anywhere if j in far else smem if a.dtyp...  400 us
    pallas_call x1, Pallas kernels, experts(): pl.pallas_call(functools.partial(expert_kernel, n), grid=(4 * local,), in...  93.1 us
    unnamed x65, local copies, waits for them, and re-layouts  19.4 us
  transfers between devices with their start and end apart: 3, of which 0 were waited for; matrix products, arithmetic and copies ran while one was open for 2% of the time, Pallas kernels for 72%

profile of v2, /device:TPU:0, one launch (start us, length us, event | category | flops | bytes accessed | tf_op | source)
XLA Modules:
  0.0 552.7 jit_solution(14681064999127219544)
XLA Ops:
  9.8 0.8 constant_dynamic-slice_fusion
  10.6 2.0 concatenate.6
  13.8 0.9 copy-done.27
  14.7 2.0 pad_maximum_fusion
  17.8 58.0 %gather_tokens.1.tokens_ref = bf16[4,256,1536]{2,1,0:T(8,128)(2,1)S(1)} custom-call(bf16[256,1536]{1,0:T(8,128)(2,1)S(1)} %copy-done.4), custom_call_target="tpu_custom_call" | custom-call | flops 1000000 | bytes 786432 | tf_op jit(solution)/shard_map/gather_tokens/pallas_call | solution.py:219
  75.8 1.6 copy-done.3
  77.5 1.1 copy-done.12
  78.7 71.1 %attend.1 = (bf16[4,256,1536]{2,1,0:T(8,128)(2,1)S(1)}, bf16[3,1024,128]{2,1,0:T(8,128)(2,1)S(1)}, bf16[1024,128]{1,0:T(8,128)(2,1)S(1)}, bf16[1024,128]{1,0:T(8...) custom-call(bf16[4,256,1536]{2,1,0:T(8,128)(2,1)} %copy-done.3, ...), custom_call_target="tpu_custom_call" | custom-call | flops 5000000000 | bytes 12091400 | tf_op jit(solution)/shard_map/attend/pallas_call | solution.py:219
  149.8 1.6 copy-done.17
  151.5 1.1 copy-done.18
  152.6 0.9 copy-done.19
  156.2 53.3 %mix.1 = (f32[256,1536]{1,0:T(8,128)S(1)}, bf16[4,256,1536]{2,1,0:T(8,128)(2,1)S(1)}, bf16[256,1536]{1,0:T(8,128)(2,1)S(1)}) custom-call(bf16[256,1536]{1,0:T(8,128)(2,1)S(1)} %copy-done.4, bf16[4,256,384]{2,1,0:T(8,128)(2,1)S(1)} %get-tuple-element.38.att_ref, bf16[1536,2304]{1,0:T(8,128)(2,1)S(1)} %copy-done.2, f32[40,1536]{1,0:T(8,128)S(1)} %get-tuple-element.37.small_ref), custom_call_target="tpu_custom_call" | custom-call | flops 2000000000 | bytes 8896512 | tf_op jit(solution)/shard_map/mix/pallas_call | solution.py:219
  209.5 1.6 copy-done.7
  211.1 1.1 copy-done.8
  212.3 93.1 %experts.1 = (bf16[8,15,192,512]{3,2,1,0:T(8,128)(2,1)}, bf16[4,256,1536]{2,1,0:T(8,128)(2,1)}, f32[4,8,256]{2,1,0:T(8,128)}, bf16[256,1536]{1,0:T(8,128)(2,1)}) custom-call(f32[4,32,256]{2,1,0:T(8,128)} %copy-done.22, f32[40,1536]{1,0:T(8,128)} %copy-done.5, bf16[4,256,1536]{2,1,0:T(8,128)(2,1)} %copy-done.7, ...), custom_call_target="tpu_custom_call" | custom-call | flops 40000000000 | bytes 60000000 | tf_op jit(solution)/shard_map/experts/pallas_call | solution.py:888
  305.4 0.9 copy-done.6
  306.3 71.2 %give_back.1 = (f32[256,1536]{1,0:T(8,128)S(1)}, bf16[4,256,384]{2,1,0:T(8,128)(2,1)S(1)}, bf16[1536,1536]{1,0:T(8,128)(2,1)}, f32[40,1536]{1,0:T(8,128)S(1)}) custom-call(bf16[4,256,1536]{2,1,0:T(8,128)(2,1)} %get-tuple-element.48.parts_ref, f32[4,8,256]{2,1,0:T(8,128)S(1)} %copy-done.16, f32[32,256]{1,0:T(8,128)S(1)} %convert_bitcast_fusion.1.chosen_ref, ...), custom_call_target="tpu_custom_call" | custom-call | flops 4000000000 | bytes 14467072 | tf_op jit(solution)/shard_map/give_back/pallas_call | solution.py:219
  377.6 1.1 copy-done.13
  378.7 0.9 copy-done.14
  380.3 146.3 %attend_back.1 = (bf16[256,1536]{1,0:T(8,128)(2,1)}, bf16[4,192,768]{2,1,0:T(8,128)(2,1)}, bf16[4,192,384]{2,1,0:T(8,128)(2,1)}) custom-call(bf16[3,1024,128]{2,1,0:T(8,128)(2,1)} %copy-done.19, bf16[1024,128]{1,0:T(8,128)(2,1)} %copy-done.20, bf16[1024,128]{1,0:T(8,128)(2,1)} %copy-done.21, f32[8,1024]{1,0:T(8,128)} %copy-done.23, ...), custom_call_target="tpu_custom_call" | custom-call | flops 10000000000 | bytes 22544392 | tf_op jit(solution)/shard_map/attend_back/pallas_call | solution.py:219
  526.7 1.2 convert_bitcast_fusion
  527.9 1.2 copy.83
  529.4 1.2 copy.80
  530.6 0.8 copy.88
  532.2 0.8 copy.89
  533.7 1.5 slice.63
  535.2 1.4 copy.87
  536.6 2.4 reshape.101
  539.0 2.6 convert_element_type.21
  541.7 2.3 slice_bitcast_fusion
  544.0 0.9 copy.92
  544.9 0.9 copy.93
  (82 shorter events, 10.2 us)
Async XLA Ops:
  7.2 2.6 copy-start
  7.2 5.5 copy-start.25
  7.2 70.3 %all-gather.5.cloned.1.call-start = ((), (), s32[]{:S(2)}) async-start(), calls=%async_computation.2 | async-start | bytes 7962624 | tf_op jit(solution)/shard_map/all_gather | solution.py:963
  12.6 1.2 copy-start.26
  12.6 199.7 %all-gather.7.cloned.1.call-start = ((), (), s32[]{:S(2)}) async-start(), calls=%async_computation.3 | async-start | bytes 26542080 | tf_op jit(solution)/shard_map/all_gather | solution.py:968
  13.4 1.3 copy-start.27
  16.7 0.7 copy-start.30
  16.7 1.1 copy-start.4
  16.7 60.8 %copy-start.9 = (bf16[256,1536]{1,0:T(8,128)(2,1)S(1)}, bf16[256,1536]{1,0:T(8,128)(2,1)}, u32[]{:S(2)}) copy-start(bf16[256,1536]{1,0:T(8,128)(2,1)} %cot_ref.3) | copy-start | bytes 2359300
  16.7 60.8 %copy-start.10 = (s32[1,2]{1,0:T(1,128)S(1)}, s32[1,2]{1,0:T(1,128)}, u32[]{:S(2)}) copy-start(s32[1,2]{1,0:T(1,128)} %starts_ref.3) | copy-start | bytes 28
  16.7 60.8 %copy-start.11 = (f32[1024,128]{1,0:T(8,128)S(1)}, f32[1024,128]{1,0:T(8,128)}, u32[]{:S(2)}) copy-start(f32[1024,128]{1,0:T(8,128)} %constant.28.clone.sin_ref) | copy-start | bytes 1572868
  16.7 517.0 %reduce-scatter.2.cloned.1.call-start = ((), (), s32[]{:S(2)}) async-start(), calls=%async_computation.1 | async-start | bytes 26542080 | tf_op jit(solution)/shard_map/reduce_scatter | solution.py:982
  75.8 1.6 copy-start.3
  77.5 1.2 copy-start.12
  78.7 77.5 %copy-start.2 = (bf16[1536,2304]{1,0:T(8,128)(2,1)S(1)}, bf16[1536,2304]{1,0:T(8,128)(2,1)}, u32[]{:S(2)}) copy-start(bf16[1536,2304]{1,0:T(8,128)(2,1)} %all-gather.5.cloned.1.call-done.packed_ref) | copy-start | bytes 21233668
  149.8 1.6 copy-start.17
  151.5 1.1 copy-start.18
  152.6 0.9 copy-start.19
  153.5 0.7 copy-start.20
  154.2 0.7 copy-start.21
  156.2 53.3 %copy-start.5 = (f32[40,1536]{1,0:T(8,128)}, f32[40,1536]{1,0:T(8,128)S(1)}, u32[]{:S(2)}) copy-start(f32[40,1536]{1,0:T(8,128)S(1)} %get-tuple-element.37.small_ref) | copy-start | bytes 737284
  209.5 1.6 copy-start.7
  211.1 1.1 copy-start.8
  305.4 0.9 copy-start.6
  305.4 0.9 copy-start.16
  377.6 1.1 copy-start.13
  378.7 0.9 copy-start.14
  379.6 0.7 copy-start.15
  526.7 2.4 copy-start.24
  541.6 2.4 copy-start.28
  541.6 3.2 copy-start.29
  541.7 4.1 copy-start.1
  (2 other events, 1.3 us)
Sparse Core Ops, SparseCore 0:
  12.7 51.5 all-gather.4
  66.2 118.6 all-gather.6
  305.6 185.0 reduce-scatter.1

commit v3 on v2

--- a/solution.py
+++ b/solution.py
@@ -157,33 +157,40 @@
 
 
 class PairReduce:
-    def __init__(self, chips, place, parts, first, sums, second, sems):
+    def __init__(self, chips, place, parts, first, sums, second, near_sems, across_sems):
         self.chips, self.core, self.chip = chips, place % 2, place // 2
         self.partner = place + 1 - 2 * self.core
         self.parts, self.first, self.sums, self.second = parts, first, sums, second
-        self.sems = sems
+        self.near_sems, self.across_sems = near_sems, across_sems
 
     def near(self, c):
-        s, r, _, _ = self.sems
+        s, r = self.near_sems
         source = self.parts.at[2 * c + 1 - self.core]
         return remote(source, self.first.at[c], s.at[c], r.at[c], self.partner, "dp")
 
     def across(self, c, slot):
-        _, _, s, r = self.sems
+        s, r = self.across_sems
         return remote(
             self.sums.at[c], self.second.at[slot], s.at[c], r.at[slot], 2 * c + self.core, "dp"
         )
 
-    def start(self):
+    def pair(self):
         for c in range(self.chips):
             self.near(c).start()
 
-    def middle(self):
+    def add(self):
         for c in range(self.chips):
             self.near(c).wait_recv()
             mine = self.parts[2 * c + self.core].astype(F32)
             self.sums[c] = (mine + self.first[c].astype(F32)).astype(BF16)
 
+    def pair_sent(self):
+        for c in range(self.chips):
+            self.near(c).wait_send()
+
+    def spread(self):
+        for c in range(self.chips):
+
             @pl.when(c != self.chip)
             def _():
                 self.across(c, self.chip).start()
@@ -191,7 +198,6 @@
     def finish(self, total):
         total[...] = self.sums[self.chip].astype(F32)
         for c in range(self.chips):
-            self.near(c).wait_send()
 
             @pl.when(c != self.chip)
             def _():
@@ -200,10 +206,6 @@
                 total[...] += self.second[c].astype(F32)
 
 
-def pair_sems(chips):
-    return [pltpu.SemaphoreType.DMA((chips,)) for _ in range(4)]
-
-
 def chain_sems(n):
     return [pltpu.SemaphoreType.DMA((2, n - 1)), pltpu.SemaphoreType.DMA((2, n - 1))]
 
@@ -212,7 +214,7 @@
     return [pltpu.SemaphoreType.DMA((n,)), pltpu.SemaphoreType.DMA((n,))]
 
 
-def call(kernel, outs, scratch, ident, name, flops, mib, args, far=()):
+def call(kernel, outs, scratch, ident, name, micros, mib, args, far=()):
     vmem = pl.BlockSpec(memory_space=pltpu.VMEM)
     smem, anywhere = pl.BlockSpec(memory_space=pltpu.SMEM), pl.BlockSpec(memory_space=pl.ANY)
     nbytes = sum(a.size * a.dtype.itemsize for a in args)
@@ -228,28 +230,56 @@
         compiler_params=pltpu.CompilerParams(
             collective_id=ident, has_side_effects=True, vmem_limit_bytes=mib * 1024 * 1024
         ),
-        cost_estimate=pl.CostEstimate(flops=flops, transcendentals=0, bytes_accessed=nbytes),
+        cost_estimate=pl.CostEstimate(
+            flops=micros * 10**9, transcendentals=0, bytes_accessed=nbytes
+        ),
         name=name,
     )(*args)
 
 
-def gather_kernel(n, tokens_ref, all_ref, s0, r0):
+def gather_kernel(
+    n, tokens_ref, q_ref, k_ref, v_ref, gate_ref, up_ref, down_ref, all_ref, heads_ref, stack_ref,
+    s0, r0,
+):
     me = lax.axis_index("expert")
     barrier_all(n, me)
     all_ref[me] = tokens_ref[...]
     chain = ChainGather(n, me, all_ref, s0, r0)
-    for s in range(n - 1):
+    chain.step(0)
+    local, depth, _ = down_ref.shape
+    ff = gate_ref.shape[2]
+    stack_ref[:local] = gate_ref[...]
+    stack_ref[local : 2 * local] = up_ref[...]
+    for j in range(down_ref.shape[2] // ff):
+        stack_ref[2 * local :, j * depth : (j + 1) * depth, :] = down_ref[
+            :, :, j * ff : (j + 1) * ff
+        ]
+    cols = heads_ref.shape[1] // n
+    at = 0
+    if cols * n > q_ref.shape[1] + 2 * k_ref.shape[1]:
+        heads_ref[...] = jnp.zeros_like(heads_ref)
+    for ref in (q_ref, k_ref, v_ref):
+        part = ref.shape[1] // n
+        for z in range(n):
+            heads_ref[:, z * cols + at : z * cols + at + part] = ref[:, z * part : (z + 1) * part]
+        at += part
+    for s in range(1, n - 1):
         chain.step(s)
     chain.finish()
 
 
-def gather_tokens(n, tokens):
+def gather_tokens(n, cols, tokens, wq, wk, wv, gate, up, down):
     rows, width = tokens.shape
+    local, shard, ff = gate.shape
+    sds = jax.ShapeDtypeStruct
     return call(
         functools.partial(gather_kernel, n),
-        [jax.ShapeDtypeStruct((n, rows, width), BF16)],
-        chain_sems(n), 1, "gather_tokens", 10**6, 16, (tokens,),
-    )[0]
+        [
+            sds((n, rows, width), BF16), sds((shard, n * cols), BF16),
+            sds((3 * local, shard, ff), BF16),
+        ],
+        chain_sems(n), 1, "gather_tokens", 60, 24, (tokens, wq, wk, wv, gate, up, down),
+    )
 
 
 def turn(x, cosine, sine):
@@ -291,7 +321,7 @@
     weights = pltpu.make_async_copy(packed_ref.at[:, pl.ds(width, wide)], w_s, load)
     weights.start()
     barrier_all(n, me)
-    cots_ref[me] = cot_ref[...]
+    cots_ref[me] = cot_ref[:, : cots_ref.shape[2]]
     chain = ChainGather(n, me, cots_ref, s0, r0)
     chain.step(0)
     swap = Exchange(n, me, send_att, att_ref, s1, r1)
@@ -384,7 +414,7 @@
             sds((lse_rows, length), F32),
             sds((per_key, length, tile), F32),
             sds((n, rows, q_cols), BF16),
-            sds((n, rows, width), BF16),
+            sds((n, rows, width // 2), BF16),
             sds((8 + chosen.shape[0], width), F32),
             sds((n,) + chosen.shape, F32),
         ],
@@ -393,7 +423,7 @@
             pltpu.VMEM((n,) + chosen.shape, F32), DMA,
         ]
         + chain_sems(n) + direct_sems(n) + direct_sems(n),
-        2, "attend", 5 * 10**9, 44,
+        2, "attend", 80, 44,
         (tokens_all, packed, cosine, sine, starts, cot, chosen), (1,),
     )
 
@@ -429,7 +459,7 @@
         functools.partial(mix_kernel, n),
         [sds((rows, width), F32), sds((n, rows, width), BF16), sds((rows, width), BF16)],
         [pltpu.VMEM((width, width), BF16), DMA] + chain_sems(n),
-        3, "mix", 2 * 10**9, 32, (tokens, att, packed, small), (2,),
+        3, "mix", 60, 32, (tokens, att, packed, small), (2,),
     )
 
 
@@ -506,14 +536,16 @@
 def return_kernel(
     n, parts_ref, gg_ref, chosen_ref, small_ref, hidden_ref, norm_ref, cot_ref, att_ref, packed_ref,
     grad_ref, ga_ref, o_ref, extra_ref,
-    w_s, slots, total, gg_s, send_ga, load, s0, r0, s1, r1, s2, r2,
+    w_s, slots, total, gg_s, send_ga, o_parts, o_first, load, s0, r0, s1, r1, s2, r2, *near,
 ):
     me = lax.axis_index("expert")
+    place = lax.axis_index("dp")
+    chips = o_ref.shape[0]
     width = w_s.shape[0]
     q_cols = ga_ref.shape[2]
     weights = pltpu.make_async_copy(packed_ref.at[:, pl.ds(0, width)], w_s, load)
     weights.start()
-    barrier_all(n, me)
+    barrier_plane(n, me, chips, place)
     chain = ChainReduce(n, me, parts_ref, slots, s0, r0)
     chain.step(0)
     gates_swap = Exchange(n, me, gg_ref, gg_s, s1, r1)
@@ -543,55 +575,69 @@
         send_ga[d] = dot_t(proj, w_s[d * q_cols : (d + 1) * q_cols, :]).astype(BF16)
         swap.start(d)
     ga_ref[me] = send_ga[me]
+    shard = o_parts.shape[1]
     for d in range(n):
-        o_ref[d * q_cols : (d + 1) * q_cols, :] = tdot(att_ref[d], proj).astype(BF16)
+        grad_o = tdot(att_ref[d], proj).astype(BF16)
+        o_parts[d * q_cols // shard : (d + 1) * q_cols // shard] = grad_o.reshape(-1, shard, width)
+    o_sum = PairReduce(chips, place, o_parts, o_first, o_ref, None, near, None)
+    o_sum.pair()
+    o_sum.add()
+    o_sum.pair_sent()
     swap.finish()
 
 
-def give_back(n, parts, gg, chosen, small, hidden, norm, cot, att, packed):
+def give_back(n, chips, parts, gg, chosen, small, hidden, norm, cot, att, packed):
     rows, width = cot.shape
     q_cols = att.shape[2]
+    shard = width // (2 * chips)
     sds, vm = jax.ShapeDtypeStruct, pltpu.VMEM
     return call(
         functools.partial(return_kernel, n),
         [
-            sds((rows, width), F32), sds(att.shape, BF16), sds((width, width), BF16),
+            sds((rows, width), F32), sds(att.shape, BF16), sds((chips, shard, width), BF16),
             sds(small.shape, F32),
         ],
         [
             vm((width, width), BF16), vm((n + 1, rows, width), BF16),
-            vm((rows, width), F32), vm(gg.shape, F32), vm((n, rows, q_cols), BF16), DMA,
+            vm((rows, width), F32), vm(gg.shape, F32), vm((n, rows, q_cols), BF16),
+            vm((2 * chips, shard, width), BF16), vm((chips, shard, width), BF16), DMA,
         ]
-        + chain_sems(n) + direct_sems(n) + direct_sems(n),
-        4, "give_back", 4 * 10**9, 48,
+        + chain_sems(n) + direct_sems(n) + direct_sems(n) + direct_sems(chips),
+        4, "give_back", 80, 48,
         (parts, gg, chosen, small, hidden, norm, cot, att, packed), (8,),
     )
 
 
 def attend_back_kernel(
-    n, kv_local, chips, q_ref, k_ref, v_ref, lse_ref, out_ref, ga_ref, starts_ref, cos_ref,
-    sin_ref, norm_ref, packed_ref, tokens_ref, small_ref, grad_ref, extra_ref, o_ref,
+    n, kv_local, q_ref, k_ref, v_ref, lse_ref, out_ref, ga_ref, starts_ref, cos_ref,
+    sin_ref, norm_ref, all_ref, tokens_ref, small_ref, grad_ref, extra_ref, o_ref,
     input_ref, shares_ref, og_ref,
-    w_s, gq_s, gk_s, gv_s, gqkv_s, ga_s, parts_s, b_slots, total, load,
-    o_first, o_sums, o_second, o_total, o_send, o_got, dw_s, w_first, w_sums, w_second, w_total,
-    s1, r1, s2, r2, s3, r3, s4, r4, *sems,
+    w_s, gq_s, gk_s, gv_s, gqkv_s, ga_s, q_send, q_got, kv_send, kv_got, load,
+    o_second, o_total, o_send, o_got, dw_s, w_first, w_sums, w_second, w_total,
+    s0, r0, s1, r1, s2, r2, s3, r3, s4, r4, *sems,
 ):
     me = lax.axis_index("expert")
     place = lax.axis_index("dp")
     per_key, length, tile = q_ref.shape
+    chips, shard, _ = o_ref.shape
     rows = length // n
     q_cols, k_cols = per_key * tile, tile
-    width, wide = w_s.shape
-    used = q_cols + 2 * k_cols
+    width = w_s.shape[0]
+    cols = w_s.shape[1] // n
     scale = HEAD_SIZE ** (-0.5)
     pieces = starts_ref.shape[1]
-    weights = pltpu.make_async_copy(packed_ref.at[:, pl.ds(width, wide)], w_s, load)
+    weights = pltpu.make_async_copy(all_ref, w_s, load)
     weights.start()
     barrier_plane(n, me, chips, place)
-    o_sum = PairReduce(chips, place, o_ref, o_first, o_sums, o_second, sems[:4])
-    o_sum.start()
+    o_sum = PairReduce(chips, place, None, None, o_ref, o_second, None, sems[:2])
+    o_sum.spread()
+    q_swap = Exchange(n, me, q_send, q_got, s0, r0)
+    kv_swap = Exchange(n, me, kv_send, kv_got, s1, r1)
     o_swap = Exchange(n, me, o_send, o_got, s2, r2)
     o_share = ChainGather(n, me, og_ref, s3, r3)
+    w_share = ChainGather(n, me, shares_ref, s4, r4)
+    gq_s[...] = jnp.zeros_like(gq_s)
+    gqkv_s[...] = jnp.zeros_like(gqkv_s)
     gk_s[...] = jnp.zeros_like(gk_s)
     gv_s[...] = jnp.zeros_like(gv_s)
     lane = lax.broadcasted_iota(jnp.int32, (rows, tile), 1)
@@ -628,117 +674,117 @@
                 probs = jnp.exp(scores - lse_ref[h : h + 1, part])
                 grad_probs = dot_t(values, ga_g)
                 grad_raw = (probs * (grad_probs - delta_s[h : h + 1, :])).astype(BF16)
-                gk_s[:reach, :] += dot(grad_raw, q_g)
+                gk_s[:reach, :tile] += dot(grad_raw, q_g)
                 gv_s[:reach, :] += dot(probs.astype(BF16), ga_g)
                 key = jnp.where(k_lane // HEAD_SIZE == g, keys, jnp.zeros_like(keys))
                 grad_q = grad_q + tdot(grad_raw, key)
             for g in range(kv_local):
                 at = (g * per_key + t) * HEAD_SIZE
-                gq_s[part, at : at + HEAD_SIZE] = (
+                gq_s[:, at : at + HEAD_SIZE] = (
                     grad_q[:, g * HEAD_SIZE : (g + 1) * HEAD_SIZE] * scale
                 )
-        if i == 0:
-            o_sum.middle()
-        if i == n // 2:
-            o_sum.finish(o_total)
-            piece = width // n
-            for d in range(n):
-                o_send[d] = o_total[:, d * piece : (d + 1) * piece].astype(BF16)
-                o_swap.start(d)
-        if i == n - 1:
-            o_swap.finish()
-            mine = o_send[me].astype(F32)
-            for d in range(n):
-                mine = mine + jnp.where(d == me, 0.0, o_got[d].astype(F32))
-            og_ref[me] = mine.astype(BF16)
-            o_share.step(0)
-    gq_s[:, q_cols:] = gk_s[...]
-    weights.wait()
-    if used < gqkv_s.shape[1]:
-        gqkv_s[...] = jnp.zeros_like(gqkv_s)
-    gain = small_ref[:1, :]
-    grad_gain = jnp.zeros_like(gain)
+        turned = turn(gq_s[...], cos_ref[part, :], -sin_ref[part, :])[:, :q_cols].astype(BF16)
+        gqkv_s[part, :q_cols] = turned
+        q_send[i] = turned
+        q_swap.start(i)
     for i in range(n):
         part = slice(i * rows, (i + 1) * rows)
-        qk = turn(gq_s[part, :], cos_ref[part, :], -sin_ref[part, :]).astype(BF16)
-        gqkv_s[part, : q_cols + k_cols] = qk
-        gqkv_s[part, q_cols + k_cols : used] = gv_s[part, :].astype(BF16)
-        back = dot_t(gqkv_s[part, :], w_s[:, : wide - 128])
-        parts_s[i] = back.astype(BF16)
-        grad_gain = grad_gain + jnp.sum(back * norm_ref[i].astype(F32), axis=0, keepdims=True)
-    chain = ChainReduce(n, me, parts_s, b_slots, s1, r1)
-    chain.step(0)
+        turned = turn(gk_s[part, :], cos_ref[part, :], -sin_ref[part, :])[:, :k_cols].astype(BF16)
+        kv_send[i, :, :k_cols] = turned
+        kv_send[i, :, k_cols:] = gv_s[part, :].astype(BF16)
+        kv_swap.start(i)
+        gqkv_s[part, q_cols : q_cols + 2 * k_cols] = kv_send[i]
+    weights.wait()
     norms = norm_ref[...].reshape(length, width)
-    dw = tdot(norms, gqkv_s[...]).astype(BF16)
-    dw_s[:, :, : wide - 128] = dw.reshape(2 * chips, -1, wide - 128)
+    dw = tdot(norms, gqkv_s[...])
+    own = w_s[:, pl.ds(pl.multiple_of(me * cols, 128), cols)].astype(F32)
+    grad_gain = jnp.sum(dw * own, axis=1, keepdims=True)
+    dw_s[:, :, :cols] = dw.astype(BF16).reshape(2 * chips, shard, cols)
     extra = extra_ref[...]
-    row = lax.broadcasted_iota(jnp.int32, extra.shape, 0)
-    extra = jnp.where(row == 0, grad_gain / gain, extra)
-    extra = jnp.concatenate([extra, jnp.zeros((128 - extra.shape[0], width), F32)], axis=0)
-    dw_s[:, :, wide - 128 :] = extra.T.astype(BF16).reshape(2 * chips, -1, 128)
-    w_sum = PairReduce(chips, place, dw_s, w_first, w_sums, w_second, sems[4:])
-    w_sum.start()
+    extra = jnp.concatenate([extra, jnp.zeros((128 - extra.shape[0], width), F32)], axis=0).T
+    lane_e = lax.broadcasted_iota(jnp.int32, extra.shape, 1)
+    extra = jnp.where(lane_e == 0, grad_gain, extra)
+    dw_s[:, :, cols:] = extra.astype(BF16).reshape(2 * chips, shard, 128)
+    w_sum = PairReduce(chips, place, dw_s, w_first, w_sums, w_second, sems[2:4], sems[4:])
+    w_sum.pair()
+    o_sum.finish(o_total)
+    piece = width // n
+    for d in range(n):
+        o_send[d] = o_total[:, d * piece : (d + 1) * piece].astype(BF16)
+        o_swap.start(d)
+    w_sum.add()
+    w_sum.spread()
+    q_got[me] = q_send[me]
+    kv_got[me] = kv_send[me]
+    q_swap.finish()
+    kv_swap.finish()
+    grad_norm = jnp.zeros((rows, width), F32)
+    for z in range(n):
+        grad_norm = grad_norm + dot_t(q_got[z], w_s[:, z * cols : z * cols + q_cols])
+        grad_norm = grad_norm + dot_t(
+            kv_got[z], w_s[:, z * cols + q_cols : z * cols + q_cols + 2 * k_cols]
+        )
+    grad, _ = rms_back(grad_norm, tokens_ref[...].astype(F32), small_ref[:1, :])
+    input_ref[...] = (grad_ref[...] + grad).astype(BF16)
+    o_swap.finish()
+    mine = o_send[me].astype(F32)
+    for d in range(n):
+        mine = mine + jnp.where(d == me, 0.0, o_got[d].astype(F32))
+    og_ref[me] = mine.astype(BF16)
+    o_share.step(0)
+    w_sum.pair_sent()
+    w_sum.finish(w_total)
+    shares_ref[me] = w_total[...].astype(BF16)
+    w_share.step(0)
     for s in range(1, n - 1):
         o_share.step(s)
+        w_share.step(s)
     o_share.finish()
-    w_sum.middle()
-    if n > 2:
-        chain.step(1)
-    w_sum.finish(w_total)
-    shares_ref[me] = w_total[...].astype(BF16)
-    w_share = ChainGather(n, me, shares_ref, s4, r4)
-    w_share.step(0)
-    for s in range(2, n - 1):
-        chain.step(s)
-    for s in range(1, n - 1):
-        w_share.step(s)
-    chain.finish(total)
-    grad, _ = rms_back(total[...], tokens_ref[...].astype(F32), gain)
-    input_ref[...] = (grad_ref[...] + grad).astype(BF16)
     w_share.finish()
 
 
 def attend_back(
-    n, kv_local, chips, saved, ga, starts, cosine, sine, norms, packed, tokens, small, grad, extra,
-    grad_o,
+    n, kv_local, saved, ga, starts, cosine, sine, norms, w_all, tokens, small, grad, extra, sums_o
 ):
     q, k, v, lse, out = saved
     rows, width = tokens.shape
     per_key, length, tile = q.shape
-    wide = packed.shape[1] - width
+    chips, shard, _ = sums_o.shape
+    cols = w_all.shape[1] // n
+    wide = cols + 128
     sds, vm = jax.ShapeDtypeStruct, pltpu.VMEM
-    qk = (per_key + 1) * tile
-    shard = width // (2 * chips)
-    across, across_w = vm((chips, shard, width), BF16), vm((chips, shard, wide), BF16)
+    q_cols = per_key * tile
+    across_w = vm((chips, shard, wide), BF16)
     piece = vm((n, shard, width // n), BF16)
+    q_block, kv_block = vm((n, rows, q_cols), BF16), vm((n, rows, 2 * tile), BF16)
     return call(
-        functools.partial(attend_back_kernel, n, kv_local, chips),
+        functools.partial(attend_back_kernel, n, kv_local),
         [
             sds((rows, width), BF16), sds((n, shard, wide), BF16),
             sds((n, shard, width // n), BF16),
         ],
         [
-            vm((width, wide), BF16), vm((length, qk), F32), vm((length, tile), F32),
-            vm((length, tile), F32), vm((length, wide - 128), BF16), vm((per_key, rows, tile), BF16),
-            vm((n, rows, width), BF16), vm((n + 1, rows, width), BF16), vm((rows, width), F32), DMA,
-            across, across, across, vm((shard, width), F32), piece, piece,
+            vm(w_all.shape, BF16), vm((rows, -(-q_cols // 128) * 128), F32), vm((length, 128), F32),
+            vm((length, tile), F32), vm((length, cols), BF16), vm((per_key, rows, tile), BF16),
+            q_block, q_block, kv_block, kv_block, DMA,
+            vm((chips, shard, width), BF16), vm((shard, width), F32), piece, piece,
             vm((2 * chips, shard, wide), BF16), across_w, across_w, across_w,
             vm((shard, wide), F32),
         ]
-        + chain_sems(n) + direct_sems(n) + chain_sems(n) + chain_sems(n)
-        + pair_sems(chips) + pair_sems(chips),
-        5, "attend_back", 10 * 10**9, 58,
-        (q, k, v, lse, out, ga, starts, cosine, sine, norms, packed, tokens, small, grad, extra,
-         grad_o.reshape(2 * chips, shard, width)),
+        + direct_sems(n) + direct_sems(n) + direct_sems(n) + chain_sems(n) + chain_sems(n)
+        + direct_sems(chips) + direct_sems(chips) + direct_sems(chips),
+        5, "attend_back", 90, 56,
+        (q, k, v, lse, out, ga, starts, cosine, sine, norms, w_all, tokens, small, grad, extra,
+         sums_o),
         (10,),
     )
 
 
 def expert_kernel(
-    n, chosen_ref, small_ref, n2_ref, cot_ref, hidden_ref, wg_ref, wu_ref, wd_ref,
+    n, chosen_ref, small_ref, n2_ref, cots_ref, cot_ref, hidden_ref, wg_ref, wu_ref, wd_ref,
     dw_ref, gx_ref, gg_ref, output_ref,
     x_s, g_s, slope_s, silu_s, act_s, gact_s, ggp_s, gup_s, pick_s, mix_s, y_s, y_slots,
-    total, gate_s, rank_s, s0, r0,
+    total, gate_s, rank_s, rest_s, s0, r0, s1, r1,
 ):
     me = lax.axis_index("expert")
     _, rows, width = n2_ref.shape
@@ -754,6 +800,8 @@
     mine = me * gg_ref.shape[1] + e
     where = pl.ds(pl.multiple_of(e * cap, cap), cap)
     chain = ChainReduce(n, me, y_s, y_slots, s0, r0)
+    more = ChainGather(n, me, rest_s, s1, r1)
+    half = cots_ref.shape[2]
 
     def whole(ref):
         return ref[...].reshape(width, ff)
@@ -767,6 +815,8 @@
     @pl.when(at == 0)
     def _():
         barrier_all(n, me)
+        rest_s[me] = cot_ref[:, half:]
+        more.step(0)
         before = lax.broadcasted_iota(jnp.int32, (rows, rows), 0)
         upto = jnp.where(before <= lax.broadcasted_iota(jnp.int32, (rows, rows), 1), 1.0, 0.0)
         router = small_ref[8:, :].astype(BF16)
@@ -776,6 +826,12 @@
             count = dot(chosen.astype(BF16), upto.astype(BF16))
             rank_s[s] = jnp.where(chosen > 0.0, count - 1.0, -1.0).astype(jnp.int32)
         gg_ref[...] = jnp.zeros_like(gg_ref)
+
+    for s in range(1, n - 1):
+
+        @pl.when(at == min((s * local + n - 2) // (n - 1), local - 1))
+        def _():
+            more.step(s)
 
     @pl.when(phase < 0)
     def _():
@@ -813,12 +869,17 @@
         def _():
             chain.step(s)
 
+    @pl.when(at == local)
+    def _():
+        more.finish()
+
     @pl.when(phase == 0)
     def _():
         for s in range(n):
             hot = pick_s[s, where, :]
             x_s[s * cap : (s + 1) * cap, :] = dot(hot, n2_ref[s]).astype(BF16)
-            g_s[s * cap : (s + 1) * cap, :] = dot(hot, cot_ref[s]).astype(BF16)
+            g_s[s * cap : (s + 1) * cap, :half] = dot(hot, cots_ref[s]).astype(BF16)
+            g_s[s * cap : (s + 1) * cap, half:] = dot(hot, rest_s[s]).astype(BF16)
         grad_act = jnp.zeros((tall, ff), F32)
         for j in range(blocks):
             grad_act = grad_act + dot_t(g_s[:, j * ff : (j + 1) * ff], down(j))
@@ -860,7 +921,7 @@
         output_ref[...] = (hidden_ref[...] + total[...]).astype(BF16)
 
 
-def experts(n, chosen, small, n2, cot, hidden, w):
+def experts(n, chosen, small, n2, cots, cot, hidden, w):
     _, rows, width = n2.shape
     shards, local, depth, ff = w.shape
     local = local // 3
@@ -889,8 +950,8 @@
         functools.partial(expert_kernel, n),
         grid=(4 * local,),
         in_specs=[
-            const(chosen.shape), const(small.shape), const(n2.shape), const(n2.shape),
-            const(hidden.shape), weight(0), weight(1), weight(2),
+            const(chosen.shape), const(small.shape), const(n2.shape), const(cots.shape),
+            const(cot.shape), const(hidden.shape), weight(0), weight(1), weight(2),
         ],
         out_specs=[
             pl.BlockSpec((shards, 1, depth, ff), grads),
@@ -904,17 +965,68 @@
             vm((tall, width), BF16), vm((tall, width), BF16), saved, saved, saved, half, half, half,
             vm((n, local * cap, rows), BF16), vm((n, local * cap, width), BF16), vm(n2.shape, BF16),
             vm((n + 1, rows, width), BF16), vm(hidden.shape, F32), vm(chosen.shape, F32), vm(chosen.shape, jnp.int32),
+            vm((n, rows, width - cots.shape[2]), BF16),
         ]
-        + chain_sems(n),
+        + chain_sems(n) + chain_sems(n),
         compiler_params=pltpu.CompilerParams(
             collective_id=6, has_side_effects=True, vmem_limit_bytes=60 * 1024 * 1024,
             dimension_semantics=("arbitrary",),
         ),
         cost_estimate=pl.CostEstimate(
-            flops=40 * 10**9, transcendentals=0, bytes_accessed=60 * 10**6
+            flops=95 * 10**9, transcendentals=0, bytes_accessed=60 * 10**6
         ),
         name="experts",
-    )(chosen, small, n2, cot, hidden, w, w, w)
+    )(chosen, small, n2, cots, cot, hidden, w, w, w)
+
+
+def finish_kernel(
+    n, shares_ref, pieces_ref, sums_ref, y_ref, grad_ref, q_ref, k_ref, v_ref, o_ref, small_ref,
+    gate_ref, up_ref, down_ref, output_ref, input_ref,
+):
+    q_cols, k_cols = q_ref.shape[1] // n, k_ref.shape[1] // n
+    piece = pieces_ref.shape[2]
+    cols = shares_ref.shape[2] - 128
+    small = jnp.zeros(small_ref.shape, F32)
+    for z in range(n):
+        at = 0
+        for ref, part in ((q_ref, q_cols), (k_ref, k_cols), (v_ref, k_cols)):
+            ref[:, z * part : (z + 1) * part] = shares_ref[z, :, at : at + part].astype(F32)
+            at += part
+        small = small + shares_ref[z, :, cols:].astype(F32)
+        o_ref[:, z * piece : (z + 1) * piece] = pieces_ref[z].astype(F32)
+    small_ref[...] = small
+    local, depth, _ = down_ref.shape
+    ff = gate_ref.shape[2]
+    gate_ref[...] = sums_ref[:local].astype(F32)
+    up_ref[...] = sums_ref[local : 2 * local].astype(F32)
+    for j in range(down_ref.shape[2] // ff):
+        down_ref[:, :, j * ff : (j + 1) * ff] = sums_ref[
+            2 * local :, j * depth : (j + 1) * depth, :
+        ].astype(F32)
+    output_ref[...] = y_ref[...]
+    input_ref[...] = grad_ref[...]
+
+
+def finish(n, k_width, depth, shares, pieces, sums, y, grad):
+    _, shard, _ = shares.shape
+    width = y.shape[1]
+    local, ff = sums.shape[0] // 3, sums.shape[2]
+    sds = jax.ShapeDtypeStruct
+    square, narrow, expert = (
+        sds((shard, width), F32), sds((shard, k_width), F32), sds((local, shard, ff), F32)
+    )
+    vmem = pl.BlockSpec(memory_space=pltpu.VMEM)
+    return pl.pallas_call(
+        functools.partial(finish_kernel, n),
+        in_specs=[vmem] * 5,
+        out_specs=[vmem] * 10,
+        out_shape=[
+            square, narrow, narrow, square, sds((shard, 128), F32), expert, expert,
+            sds((local, depth, width), F32), sds(y.shape, BF16), sds(y.shape, BF16),
+        ],
+        compiler_params=pltpu.CompilerParams(vmem_limit_bytes=40 * 1024 * 1024),
+        name="finish",
+    )(shares, pieces, sums, y, grad)
 
 
 def rotary_tables(length):
@@ -938,9 +1050,7 @@
     kv_local = KEY_VALUE_HEADS // n
     q_cols = QUERY_HEADS // n * HEAD_SIZE
     k_cols = kv_local * HEAD_SIZE
-    local, shard, ff = expert_gate.shape
-    depth = expert_down.shape[1]
-    blocks = width // ff
+    local, shard, _ = expert_gate.shape
     padded = -(-local // 8) * 8
 
     wq = lax.dynamic_slice_in_dim(q_weight, member * q_cols, q_cols, 1)
@@ -961,46 +1071,41 @@
         axis=1,
     )
     packed = lax.all_gather(packed, "dp").reshape(width, -1)
-    down_rows = expert_down.reshape(local, depth, blocks, ff).transpose(0, 2, 1, 3)
-    stacked = jnp.concatenate(
-        [expert_gate, expert_up, down_rows.reshape(local, shard, ff)], axis=0
-    )
-    experts_w = lax.all_gather(stacked, "dp")
-
     hot = routes[:, :, None] == jnp.arange(n * local, dtype=jnp.int32)
     chosen = jnp.any(hot, axis=1).astype(F32).T.reshape(n, local, rows)
     chosen = jnp.pad(chosen, ((0, 0), (0, padded - local), (0, 0))).reshape(n * padded, rows)
     cosine, sine = rotary_tables(length)
     chips = lax.axis_size("dp") // 2
 
-    tokens_all = gather_tokens(n, tokens)
+    cols = -(-used // 128) * 128
+    tokens_all, w_all, stacked = gather_tokens(
+        n, cols, tokens, q_weight, key_matrix, value_matrix, expert_gate, expert_up, expert_down
+    )
+    experts_w = lax.all_gather(stacked, "dp")
     norms, q, k, v, lse, out, att, cots, small, chosen_all = attend(
         n, kv_local, tokens_all, packed, cosine, sine, starts, cotangent, chosen
     )
+    w_all, att = lax.optimization_barrier((w_all, att))
+    w_all = lax.all_gather(w_all, "dp").reshape(width, n * cols)
     hidden, twos, two = mix(n, tokens, att, packed, small)
-    grad_experts, back, gg, output = experts(n, chosen_all, small, twos, cots, hidden, experts_w)
+    grad_experts, back, gg, output = experts(
+        n, chosen_all, small, twos, cots, cotangent, hidden, experts_w
+    )
     expert_grads = lax.psum_scatter(grad_experts, "dp", scatter_dimension=0)
-    grad_hidden, ga, grad_o, extra = give_back(
-        n, back, gg, chosen, small, hidden, two, cotangent, att, packed
+    grad_hidden, ga, sums_o, extra = give_back(
+        n, chips, back, gg, chosen, small, hidden, two, cotangent, att, packed
     )
     input_grad, shares, o_grad = attend_back(
-        n, kv_local, chips, (q, k, v, lse, out), ga, starts, cosine, sine, norms, packed, tokens,
-        small, grad_hidden, extra, grad_o,
-    )
-    expert_grads = expert_grads.astype(F32)
-    gate_grad, up_grad = expert_grads[:local], expert_grads[local : 2 * local]
-    down_grad = expert_grads[2 * local :].reshape(local, blocks, depth, ff)
-    down_grad = down_grad.transpose(0, 2, 1, 3).reshape(local, depth, width)
-    o_grad = o_grad.astype(F32).transpose(1, 0, 2).reshape(shard, width)
-    shares = shares.astype(F32)
-    q_grad = shares[:, :, :q_cols].transpose(1, 0, 2).reshape(shard, -1)
-    k_grad = shares[:, :, q_cols : q_cols + k_cols].transpose(1, 0, 2).reshape(shard, -1)
-    v_grad = shares[:, :, q_cols + k_cols : used].transpose(1, 0, 2).reshape(shard, -1)
-    rest = jnp.sum(shares[:, :, wide - 128 :], axis=0)
+        n, kv_local, (q, k, v, lse, out), ga, starts, cosine, sine, norms, w_all, tokens,
+        small, grad_hidden, extra, sums_o,
+    )
+    q_grad, k_grad, v_grad, o_grad, rest, gate_grad, up_grad, down_grad, output, input_grad = finish(
+        n, key_matrix.shape[1], expert_down.shape[1], shares, o_grad, expert_grads, output, input_grad
+    )
     router_grad = rest[:, 8 : 8 + n * padded].reshape(shard, n, padded)[:, :, :local]
     return (
-        output, input_grad, rest[:, 0], q_grad, k_grad, v_grad, o_grad, rest[:, 1],
-        router_grad.reshape(shard, n * local), gate_grad, up_grad, down_grad,
+        output, input_grad, rest[:, 0] / attn_gain.astype(F32), q_grad, k_grad, v_grad, o_grad,
+        rest[:, 1], router_grad.reshape(shard, n * local), gate_grad, up_grad, down_grad,
     )
 
 

time: 562 us -> 505 us (0.90)
  Pallas kernels: 493 us -> 445 us
    pallas_call x5, Pallas kernels: 400 us -> 339 us  [call(): pl.pallas_call(kernel, in_specs=[anywhere if j in far else smem if a.dtyp...]
    pallas_call x1, Pallas kernels: 93.1 us -> 102 us  [experts(): pl.pallas_call(functools.partial(expert_kernel, n), grid=(4 * local,), in...]
    reshape x7 -> x0, local copies, waits for them, and re-layouts: 8.4 us -> none  [the longest x1 2.44 us: per_device(): down_grad = down_grad.transpose(0, 2, 1, 3).reshape(local, depth, width)]
    unnamed x65 -> x76, local copies, waits for them, and re-layouts: 19.4 us -> 27.8 us
  transfers between devices with their start and end apart: 3 -> 4, of which waited for: 0 -> 1; matrix products, arithmetic and copies ran while one was open for 2% -> 0% of each run, Pallas kernels for 72% -> 89%
where the time goes in v3:
time: 505 us; the launch traced here: 496 us
  Pallas kernels  445 us (88%)
  local copies, waits for them, and re-layouts  35.5 us (7%)
  between operations  14.5 us (3%)
    pallas_call x5, Pallas kernels, call(): pl.pallas_call(kernel, in_specs=[anywhere if j in far else smem if a.dtyp...  339 us
    pallas_call x1, Pallas kernels, experts(): pl.pallas_call(functools.partial(expert_kernel, n), grid=(4 * local,), in...  102 us
    unnamed x76, local copies, waits for them, and re-layouts  27.8 us
  transfers between devices with their start and end apart: 4, of which 1 were waited for; matrix products, arithmetic and copies ran while one was open for 0% of the time, Pallas kernels for 89%

profile of v3, /device:TPU:0, one launch (start us, length us, event | category | flops | bytes accessed | tf_op | source)
XLA Modules:
  0.0 496.5 jit_solution(8631903685550238995)
XLA Ops:
  7.3 0.8 stack.10
  8.9 0.7 reshape.52
  9.8 0.9 constant_dynamic-slice_fusion.2
  10.7 0.8 constant_dynamic-slice_fusion
  11.6 2.0 concatenate.3
  13.7 1.2 copy-done.11
  14.9 1.1 copy-done.14
  16.0 60.0 %gather_tokens.1 = (bf16[4,256,1536]{2,1,0:T(8,128)(2,1)S(1)}, bf16[192,2560]{1,0:T(8,128)(2,1)}, bf16[15,192,512]{2,1,0:T(8,128)(2,1)}) custom-call(bf16[256,1536]{1,0:T(8,128)(2,1)S(1)} %copy-done.14, bf16[192,1536]{1,0:T(8,128)(2,1)S(1)} %copy-done.5, bf16[192,512]{1,0:T(8,128)(2,1)S(1)} %copy-done.6, bf16[192,512]{1,0:T(8,128)(2,1)S(1)} %copy-done.7, ...), custom_call_target="tpu_custom_call" | custom-call | flops 60000002048 | bytes 4718592 | tf_op jit(solution)/shard_map/gather_tokens/pallas_call | solution.py:221
  76.0 1.7 copy-done.20
  79.2 46.3 %attend.1 = (bf16[4,256,1536]{2,1,0:T(8,128)(2,1)}, bf16[3,1024,128]{2,1,0:T(8,128)(2,1)S(1)}, bf16[1024,128]{1,0:T(8,128)(2,1)S(1)}, bf16[1024,128]{1,0:T(8,128...) custom-call(bf16[4,256,1536]{2,1,0:T(8,128)(2,1)} %copy-done.20, ...), custom_call_target="tpu_custom_call" | custom-call | flops 80000000000 | bytes 12091400 | tf_op jit(solution)/shard_map/attend/pallas_call | solution.py:221
  125.5 1.1 copy-done.22
  126.6 1.1 copy-done.24
  127.7 0.9 copy-done.26
  129.3 0.7 copy-done.30
  130.0 0.7 copy-done.31
  132.1 3.0 copy-done.8
  135.1 0.9 copy-done.28
  136.0 56.9 %mix.1 = (f32[256,1536]{1,0:T(8,128)S(1)}, bf16[4,256,1536]{2,1,0:T(8,128)(2,1)S(1)}, bf16[256,1536]{1,0:T(8,128)(2,1)S(1)}) custom-call(bf16[256,1536]{1,0:T(8,128)(2,1)S(1)} %copy-done.15, bf16[4,256,384]{2,1,0:T(8,128)(2,1)S(1)} %get-tuple-element.61.att_ref, bf16[1536,2304]{1,0:T(8,128)(2,1)S(1)} %copy-done.8, f32[40,1536]{1,0:T(8,128)S(1)} %copy-done.28), custom_call_target="tpu_custom_call" | custom-call | flops 60000002048 | bytes 8896512 | tf_op jit(solution)/shard_map/mix/pallas_call | solution.py:221
  192.9 1.7 copy-done.19
  194.7 1.1 copy-done.21
  196.4 101.9 %experts.1 = (bf16[8,15,192,512]{3,2,1,0:T(8,128)(2,1)}, bf16[4,256,1536]{2,1,0:T(8,128)(2,1)}, f32[4,8,256]{2,1,0:T(8,128)}, bf16[256,1536]{1,0:T(8,128)(2,1)}) custom-call(f32[4,32,256]{2,1,0:T(8,128)} %copy-done.33, f32[40,1536]{1,0:T(8,128)} %copy-done.27, bf16[4,256,1536]{2,1,0:T(8,128)(2,1)} %copy-done.19, bf16[4,256,768]{2,1,0:T(8,128)(2,1)} %copy-done.22, ...), custom_call_target="tpu_custom_call" | custom-call | flops 95000002560 | bytes 60000000 | tf_op jit(solution)/shard_map/experts/pallas_call | solution.py:949
  298.4 1.1 copy-done.13
  299.5 72.2 %give_back.1 = (f32[256,1536]{1,0:T(8,128)S(1)}, bf16[4,256,384]{2,1,0:T(8,128)(2,1)S(1)}, bf16[4,192,1536]{2,1,0:T(8,128)(2,1)}, f32[40,1536]{1,0:T(8,128)S(1)}) custom-call(bf16[4,256,1536]{2,1,0:T(8,128)(2,1)} %get-tuple-element.66.parts_ref, f32[4,8,256]{2,1,0:T(8,128)S(1)} %copy-done.34, f32[32,256]{1,0:T(8,128)S(1)} %convert_bitcast_fusion.chosen_ref, ...), custom_call_target="tpu_custom_call" | custom-call | flops 80000000000 | bytes 14467072 | tf_op jit(solution)/shard_map/give_back/pallas_call | solution.py:221
  371.8 1.1 copy-done.23
  372.9 0.9 copy-done.25
  374.5 103.3 %attend_back.1 = (bf16[256,1536]{1,0:T(8,128)(2,1)}, bf16[4,192,768]{2,1,0:T(8,128)(2,1)}, bf16[4,192,384]{2,1,0:T(8,128)(2,1)}) custom-call(bf16[3,1024,128]{2,1,0:T(8,128)(2,1)} %copy-done.26, bf16[1024,128]{1,0:T(8,128)(2,1)} %copy-done.30, bf16[1024,128]{1,0:T(8,128)(2,1)} %copy-done.31, f32[8,1024]{1,0:T(8,128)} %copy-done.35, ...), custom_call_target="tpu_custom_call" | custom-call | flops 89999998976 | bytes 20971528 | tf_op jit(solution)/shard_map/attend_back/pallas_call | solution.py:221
  477.9 1.8 copy-done
  479.7 1.3 copy-done.1
  481.0 1.1 copy-done.3
  482.1 1.1 copy-done.4
  483.2 4.3 finish.1
  487.5 0.8 slice_reduce_fusion
  (83 shorter events, 7.3 us)
Async XLA Ops:
  7.2 6.5 %copy-start.5 = (bf16[192,1536]{1,0:T(8,128)(2,1)S(1)}, bf16[192,1536]{1,0:T(8,128)(2,1)}, u32[]{:S(2)}) copy-start(bf16[192,1536]{1,0:T(8,128)(2,1)} %q_ref.1) | copy-start | bytes 1769476
  7.2 6.5 %copy-start.6 = (bf16[192,512]{1,0:T(8,128)(2,1)S(1)}, bf16[192,512]{1,0:T(8,128)(2,1)}, u32[]{:S(2)}) copy-start(bf16[192,512]{1,0:T(8,128)(2,1)} %k_ref.1) | copy-start | bytes 589828
  7.2 6.5 %copy-start.7 = (bf16[192,512]{1,0:T(8,128)(2,1)S(1)}, bf16[192,512]{1,0:T(8,128)(2,1)}, u32[]{:S(2)}) copy-start(bf16[192,512]{1,0:T(8,128)(2,1)} %v_ref.1) | copy-start | bytes 589828
  7.2 6.5 %copy-start.9 = (bf16[5,192,512]{2,1,0:T(8,128)(2,1)S(1)}, bf16[5,192,512]{2,1,0:T(8,128)(2,1)}, u32[]{:S(2)}) copy-start(bf16[5,192,512]{2,1,0:T(8,128)(2,1)} %gate_ref.1) | copy-start | bytes 2949124
  7.2 6.5 %copy-start.10 = (bf16[5,192,512]{2,1,0:T(8,128)(2,1)S(1)}, bf16[5,192,512]{2,1,0:T(8,128)(2,1)}, u32[]{:S(2)}) copy-start(bf16[5,192,512]{2,1,0:T(8,128)(2,1)} %up_ref.1) | copy-start | bytes 2949124
  7.2 71.3 %all-gather.7.cloned.1.call-start = ((), (), s32[]{:S(2)}) async-start(), calls=%async_computation.2 | async-start | bytes 7962624 | tf_op jit(solution)/shard_map/all_gather | solution.py:1073
  13.6 182.8 %all-gather.9.cloned.1.call-start = ((), (), s32[]{:S(2)}) async-start(), calls=%async_computation.3 | async-start | bytes 26542080 | tf_op jit(solution)/shard_map/all_gather | solution.py:1084
  13.7 1.2 copy-start.11
  14.9 1.1 copy-start.14
  76.0 1.7 copy-start.20
  77.7 1.1 copy-start.12
  77.7 1.1 copy-start.16
  77.7 1.3 copy-start.17
  77.7 1.5 copy-start.18
  77.8 296.7 %all-gather.11.cloned.1.call-start = ((), (), s32[]{:S(2)}) async-start(), calls=%async_computation.4 | async-start | bytes 8847360 | tf_op jit(solution)/shard_map/all_gather | solution.py:1089
  79.2 52.9 %copy-start.15 = (bf16[256,1536]{1,0:T(8,128)(2,1)S(1)}, bf16[256,1536]{1,0:T(8,128)(2,1)}, u32[]{:S(2)}) copy-start(bf16[256,1536]{1,0:T(8,128)(2,1)} %tokens_ref.5) | copy-start | bytes 2359300
  125.4 1.1 copy-start.22
  126.6 1.1 copy-start.24
  132.0 345.8 %reduce-scatter.2.cloned.1.call-start = ((), (), s32[]{:S(2)}) async-start(), calls=%async_computation.1 | async-start | bytes 26542080 | tf_op jit(solution)/shard_map/reduce_scatter | solution.py:1094
  132.1 3.0 copy-start.8
  192.9 1.7 copy-start.19
  194.7 1.1 copy-start.21
  298.4 1.1 copy-start.13
  298.4 1.2 copy-start.29
  298.4 1.2 copy-start.34
  371.8 1.1 copy-start.23
  374.5 103.3 %copy-start.2 = (bf16[256,1536]{1,0:T(8,128)(2,1)S(1)}, bf16[256,1536]{1,0:T(8,128)(2,1)}, u32[]{:S(2)}) copy-start(bf16[256,1536]{1,0:T(8,128)(2,1)} %get-tuple-element.78.y_ref) | copy-start | bytes 2359300
  477.9 1.8 copy-start
  479.7 1.3 copy-start.1
  481.0 1.1 copy-start.3
  482.1 1.1 copy-start.4
  483.2 5.8 %copy-start.37 = (bf16[192]{0:T(256)(128)(2,1)S(1)}, bf16[192]{0:T(256)(128)(2,1)}, u32[]{:S(2)}) copy-start(bf16[192]{0:T(256)(128)(2,1)} %param.17) | copy-start | bytes 1156
  (10 other events, 7.5 us)
Sparse Core Ops, SparseCore 0:
  13.7 51.5 all-gather.6
  77.9 118.4 all-gather.8
  198.3 52.1 all-gather.10
  298.5 178.0 reduce-scatter.1

commit v4 on v3

--- a/solution.py
+++ b/solution.py
@@ -34,6 +34,7 @@
 
 DMA = pltpu.SemaphoreType.DMA
 MESH = pl.DeviceIdType.MESH
+LIMIT = 60 * 1024 * 1024
 
 
 def barrier_all(n, me):
@@ -214,21 +215,41 @@
     return [pltpu.SemaphoreType.DMA((n,)), pltpu.SemaphoreType.DMA((n,))]
 
 
-def call(kernel, outs, scratch, ident, name, micros, mib, args, far=()):
-    vmem = pl.BlockSpec(memory_space=pltpu.VMEM)
-    smem, anywhere = pl.BlockSpec(memory_space=pltpu.SMEM), pl.BlockSpec(memory_space=pl.ANY)
+def call(kernel, outs, scratch, ident, name, micros, args, far=(), keep=()):
+    vmem, hbm = pl.BlockSpec(memory_space=pltpu.VMEM), pl.BlockSpec(memory_space=pltpu.HBM)
+    smem = pl.BlockSpec(memory_space=pltpu.SMEM)
     nbytes = sum(a.size * a.dtype.itemsize for a in args)
+    first, count = len(args), len(outs)
+
+    def body(*refs):
+        inside, results, rest = refs[:first], list(refs[first : first + count]), refs[first + count :]
+        stages, rest = rest[: len(keep)], rest[len(keep) :]
+        copies = {}
+        if keep:
+            for j, k in enumerate(keep):
+                copies[k] = pltpu.make_async_copy(stages[j], results[k], rest[0].at[j])
+                results[k] = stages[j]
+            rest = rest[1:]
+
+        def save(*which):
+            for k in which:
+                copies[k].start()
+
+        kernel(*inside, *results, *rest, **(dict(save=save) if keep else {}))
+        for k in keep:
+            copies[k].wait()
+
+    kept = [pltpu.VMEM(outs[k].shape, outs[k].dtype) for k in keep]
     return pl.pallas_call(
-        kernel,
+        body,
         in_specs=[
-            anywhere if j in far else smem if a.dtype == jnp.int32 else vmem
-            for j, a in enumerate(args)
+            hbm if j in far else smem if a.dtype == jnp.int32 else vmem for j, a in enumerate(args)
         ],
-        out_specs=[vmem] * len(outs),
+        out_specs=[hbm if k in keep else vmem for k in range(count)],
         out_shape=outs,
-        scratch_shapes=scratch,
+        scratch_shapes=kept + ([pltpu.SemaphoreType.DMA((len(keep),))] if keep else []) + scratch,
         compiler_params=pltpu.CompilerParams(
-            collective_id=ident, has_side_effects=True, vmem_limit_bytes=mib * 1024 * 1024
+            collective_id=ident, has_side_effects=True, vmem_limit_bytes=LIMIT
         ),
         cost_estimate=pl.CostEstimate(
             flops=micros * 10**9, transcendentals=0, bytes_accessed=nbytes
@@ -237,23 +258,91 @@
     )(*args)
 
 
-def gather_kernel(
-    n, tokens_ref, q_ref, k_ref, v_ref, gate_ref, up_ref, down_ref, all_ref, heads_ref, stack_ref,
-    s0, r0,
-):
-    me = lax.axis_index("expert")
-    barrier_all(n, me)
-    all_ref[me] = tokens_ref[...]
-    chain = ChainGather(n, me, all_ref, s0, r0)
-    chain.step(0)
-    local, depth, _ = down_ref.shape
+def stack_kernel(gate_ref, up_ref, down_ref, stack_ref):
+    local, depth, width = down_ref.shape
     ff = gate_ref.shape[2]
     stack_ref[:local] = gate_ref[...]
     stack_ref[local : 2 * local] = up_ref[...]
-    for j in range(down_ref.shape[2] // ff):
+    for j in range(width // ff):
         stack_ref[2 * local :, j * depth : (j + 1) * depth, :] = down_ref[
             :, :, j * ff : (j + 1) * ff
         ]
+
+
+def stack(gate, up, down):
+    local, shard, ff = gate.shape
+    vmem = pl.BlockSpec(memory_space=pltpu.VMEM)
+    return pl.pallas_call(
+        stack_kernel,
+        in_specs=[vmem] * 3,
+        out_specs=vmem,
+        out_shape=jax.ShapeDtypeStruct((3 * local, shard, ff), BF16),
+        compiler_params=pltpu.CompilerParams(vmem_limit_bytes=LIMIT),
+        cost_estimate=pl.CostEstimate(flops=3 * 10**9, transcendentals=0, bytes_accessed=6 * 10**6),
+        name="stack",
+    )(gate, up, down)
+
+
+class PlaneGather:
+    def __init__(self, chips, place, slots, sems):
+        self.chips, self.core, self.chip, self.place = chips, place % 2, place // 2, place
+        self.partner = place + 1 - 2 * self.core
+        self.slots, self.sems = slots, sems
+
+    def across(self, c, block):
+        s, r, _, _ = self.sems
+        ref = self.slots.at[block]
+        return remote(ref, ref, s.at[c], r.at[block // 2], 2 * c + self.core, "dp")
+
+    def near(self, block):
+        _, _, s, r = self.sems
+        ref = self.slots.at[block]
+        return remote(ref, ref, s.at[block // 2], r.at[block // 2], self.partner, "dp")
+
+    def start(self):
+        self.near(self.place).start()
+        for c in range(self.chips):
+
+            @pl.when(c != self.chip)
+            def _():
+                self.across(c, self.place).start()
+
+    def forward(self):
+        for c in range(self.chips):
+
+            @pl.when(c != self.chip)
+            def _():
+                block = 2 * c + self.core
+                self.across(c, block).wait_recv()
+                self.near(block).start()
+
+    def finish(self):
+        for c in range(self.chips):
+            self.near(2 * c + self.core).wait_send()
+            self.near(2 * c + 1 - self.core).wait_recv()
+
+            @pl.when(c != self.chip)
+            def _():
+                self.across(c, self.place).wait_send()
+
+
+def gather_kernel(
+    n, tokens_ref, q_ref, k_ref, v_ref, o_ref, all_ref, heads_ref, o_all_ref, load, s0, r0, *sems, save
+):
+    me = lax.axis_index("expert")
+    place = lax.axis_index("dp")
+    chips = o_all_ref.shape[0] // 2
+    rows = pltpu.make_async_copy(tokens_ref, all_ref.at[me], load.at[0])
+    own = pltpu.make_async_copy(o_ref, o_all_ref.at[place], load.at[1])
+    rows.start()
+    own.start()
+    barrier_plane(n, me, chips, place)
+    chain = ChainGather(n, me, all_ref, s0, r0)
+    weights = PlaneGather(chips, place, o_all_ref, sems)
+    rows.wait()
+    chain.step(0)
+    own.wait()
+    weights.start()
     cols = heads_ref.shape[1] // n
     at = 0
     if cols * n > q_ref.shape[1] + 2 * k_ref.shape[1]:
@@ -263,22 +352,29 @@
         for z in range(n):
             heads_ref[:, z * cols + at : z * cols + at + part] = ref[:, z * part : (z + 1) * part]
         at += part
+    save(1)
     for s in range(1, n - 1):
         chain.step(s)
+    weights.forward()
+    weights.finish()
+    save(2)
     chain.finish()
-
-
-def gather_tokens(n, cols, tokens, wq, wk, wv, gate, up, down):
+    save(0)
+
+
+def gather_tokens(n, cols, tokens, wq, wk, wv, wo):
     rows, width = tokens.shape
-    local, shard, ff = gate.shape
+    shard = wq.shape[0]
+    chips = width // shard // 2
     sds = jax.ShapeDtypeStruct
     return call(
         functools.partial(gather_kernel, n),
         [
             sds((n, rows, width), BF16), sds((shard, n * cols), BF16),
-            sds((3 * local, shard, ff), BF16),
+            sds((2 * chips, shard, width), BF16),
         ],
-        chain_sems(n), 1, "gather_tokens", 60, 24, (tokens, wq, wk, wv, gate, up, down),
+        [pltpu.SemaphoreType.DMA((2,))] + chain_sems(n) + direct_sems(chips) + direct_sems(chips),
+        1, "gather_tokens", 60, (tokens, wq, wk, wv, wo), (0, 4), (0, 1, 2),
     )
 
 
@@ -311,14 +407,14 @@
 def attend_kernel(
     n, kv_local, tokens_ref, packed_ref, cos_ref, sin_ref, starts_ref, cot_ref,
     chosen_ref, norm_ref, q_ref, k_ref, v_ref, lse_ref, out_ref, att_ref, cots_ref, small_ref,
-    every_ref, w_s, send_att, send_chosen, load, s0, r0, s1, r1, s2, r2,
+    every_ref, w_s, send_att, send_chosen, load, s0, r0, s1, r1, s2, r2, *, save,
 ):
     me = lax.axis_index("expert")
     per_key, length, tile = q_ref.shape
     rows = length // n
     q_cols, k_cols = per_key * tile, tile
     width, wide = w_s.shape
-    weights = pltpu.make_async_copy(packed_ref.at[:, pl.ds(width, wide)], w_s, load)
+    weights = pltpu.make_async_copy(packed_ref, w_s, load)
     weights.start()
     barrier_all(n, me)
     cots_ref[me] = cot_ref[:, : cots_ref.shape[2]]
@@ -334,6 +430,7 @@
     weights.wait()
     small = w_s[:, wide - 128 :].astype(F32).T
     small_ref[...] = small[: small_ref.shape[0], :]
+    save(8)
     gain = small[:1, :]
     lane = lax.broadcasted_iota(jnp.int32, (rows, tile), 1)
     lane_w = lax.broadcasted_iota(jnp.int32, (rows, 128), 1)
@@ -352,6 +449,7 @@
             for g in range(kv_local):
                 at = (g * per_key + t) * HEAD_SIZE
                 q_ref[t, part, g * HEAD_SIZE : (g + 1) * HEAD_SIZE] = q[:, at : at + HEAD_SIZE]
+    save(0, 1, 2, 3)
     if n > 2:
         chain.step(1)
     for i in range(n):
@@ -389,9 +487,11 @@
         swap.start(i)
         if i + 2 < n - 1:
             chain.step(i + 2)
+    save(4, 5)
     att_ref[me] = send_att[me]
     choice.finish()
     chain.finish()
+    save(7, 9)
     swap.finish()
 
 
@@ -401,7 +501,7 @@
     tile = kv_local * HEAD_SIZE
     per_key = QUERY_HEADS // KEY_VALUE_HEADS
     q_cols = per_key * tile
-    wide = packed.shape[1] - width
+    wide = packed.shape[1]
     sds = jax.ShapeDtypeStruct
     lse_rows = -(-per_key * kv_local // 8) * 8
     return call(
@@ -423,18 +523,19 @@
             pltpu.VMEM((n,) + chosen.shape, F32), DMA,
         ]
         + chain_sems(n) + direct_sems(n) + direct_sems(n),
-        2, "attend", 80, 44,
+        2, "attend", 80,
         (tokens_all, packed, cosine, sine, starts, cot, chosen), (1,),
+        (0, 1, 2, 3, 4, 5, 7, 8, 9),
     )
 
 
 def mix_kernel(
-    n, tokens_ref, att_ref, packed_ref, small_ref, hidden_ref, norms_ref, own_ref, w_s, load, s0, r0
+    n, tokens_ref, att_ref, packed_ref, small_ref, hidden_ref, norms_ref, own_ref, w_s, load, s0, r0, *, save
 ):
     me = lax.axis_index("expert")
     q_cols = att_ref.shape[2]
     width = w_s.shape[0]
-    weights = pltpu.make_async_copy(packed_ref.at[:, pl.ds(0, width)], w_s, load)
+    weights = pltpu.make_async_copy(packed_ref, w_s, load)
     weights.start()
     hidden = tokens_ref[...].astype(F32)
     weights.wait()
@@ -447,19 +548,22 @@
     barrier_all(n, me)
     norms_ref[me] = norm
     chain = ChainGather(n, me, norms_ref, s0, r0)
-    for s in range(n - 1):
+    chain.step(0)
+    save(0, 2)
+    for s in range(1, n - 1):
         chain.step(s)
     chain.finish()
-
-
-def mix(n, tokens, att, packed, small):
+    save(1)
+
+
+def mix(n, tokens, att, w_o, small):
     rows, width = tokens.shape
     sds = jax.ShapeDtypeStruct
     return call(
         functools.partial(mix_kernel, n),
         [sds((rows, width), F32), sds((n, rows, width), BF16), sds((rows, width), BF16)],
         [pltpu.VMEM((width, width), BF16), DMA] + chain_sems(n),
-        3, "mix", 60, 32, (tokens, att, packed, small), (2,),
+        3, "mix", 60, (tokens, att, w_o, small), (2,), (0, 1, 2),
     )
 
 
@@ -536,14 +640,14 @@
 def return_kernel(
     n, parts_ref, gg_ref, chosen_ref, small_ref, hidden_ref, norm_ref, cot_ref, att_ref, packed_ref,
     grad_ref, ga_ref, o_ref, extra_ref,
-    w_s, slots, total, gg_s, send_ga, o_parts, o_first, load, s0, r0, s1, r1, s2, r2, *near,
+    w_s, slots, total, gg_s, send_ga, o_parts, o_first, load, s0, r0, s1, r1, s2, r2, *near, save,
 ):
     me = lax.axis_index("expert")
     place = lax.axis_index("dp")
     chips = o_ref.shape[0]
     width = w_s.shape[0]
     q_cols = ga_ref.shape[2]
-    weights = pltpu.make_async_copy(packed_ref.at[:, pl.ds(0, width)], w_s, load)
+    weights = pltpu.make_async_copy(packed_ref, w_s, load)
     weights.start()
     barrier_plane(n, me, chips, place)
     chain = ChainReduce(n, me, parts_ref, slots, s0, r0)
@@ -568,6 +672,7 @@
     extra_ref[:8, :] = jnp.where(row == 1, grad_gain, 0.0)
     grad = cot_ref[...].astype(F32) + grad
     grad_ref[...] = grad
+    save(0, 3)
     proj = grad.astype(BF16)
     weights.wait()
     swap = Exchange(n, me, send_ga, ga_ref, s2, r2)
@@ -582,11 +687,13 @@
     o_sum = PairReduce(chips, place, o_parts, o_first, o_ref, None, near, None)
     o_sum.pair()
     o_sum.add()
+    save(2)
     o_sum.pair_sent()
     swap.finish()
-
-
-def give_back(n, chips, parts, gg, chosen, small, hidden, norm, cot, att, packed):
+    save(1)
+
+
+def give_back(n, chips, parts, gg, chosen, small, hidden, norm, cot, att, w_o):
     rows, width = cot.shape
     q_cols = att.shape[2]
     shard = width // (2 * chips)
@@ -603,8 +710,8 @@
             vm((2 * chips, shard, width), BF16), vm((chips, shard, width), BF16), DMA,
         ]
         + chain_sems(n) + direct_sems(n) + direct_sems(n) + direct_sems(chips),
-        4, "give_back", 80, 48,
-        (parts, gg, chosen, small, hidden, norm, cot, att, packed), (8,),
+        4, "give_back", 80,
+        (parts, gg, chosen, small, hidden, norm, cot, att, w_o), (8,), (0, 1, 2, 3),
     )
 
 
@@ -773,7 +880,7 @@
         ]
         + direct_sems(n) + direct_sems(n) + direct_sems(n) + chain_sems(n) + chain_sems(n)
         + direct_sems(chips) + direct_sems(chips) + direct_sems(chips),
-        5, "attend_back", 90, 56,
+        5, "attend_back", 90,
         (q, k, v, lse, out, ga, starts, cosine, sine, norms, w_all, tokens, small, grad, extra,
          sums_o),
         (10,),
@@ -969,7 +1076,7 @@
         ]
         + chain_sems(n) + chain_sems(n),
         compiler_params=pltpu.CompilerParams(
-            collective_id=6, has_side_effects=True, vmem_limit_bytes=60 * 1024 * 1024,
+            collective_id=6, has_side_effects=True, vmem_limit_bytes=LIMIT,
             dimension_semantics=("arbitrary",),
         ),
         cost_estimate=pl.CostEstimate(
@@ -980,9 +1087,22 @@
 
 
 def finish_kernel(
-    n, shares_ref, pieces_ref, sums_ref, y_ref, grad_ref, q_ref, k_ref, v_ref, o_ref, small_ref,
-    gate_ref, up_ref, down_ref, output_ref, input_ref,
+    n, shares_far, pieces_far, sums_far, y_far, grad_far, q_ref, k_ref, v_ref, o_ref, small_ref,
+    gate_ref, up_ref, down_ref, output_ref, input_ref, shares_ref, pieces_ref, sums_ref, sems,
 ):
+    copies = [
+        pltpu.make_async_copy(source, target, sems.at[j])
+        for j, (source, target) in enumerate(
+            (
+                (shares_far, shares_ref), (pieces_far, pieces_ref), (sums_far, sums_ref),
+                (y_far, output_ref), (grad_far, input_ref),
+            )
+        )
+    ]
+    for copy in copies:
+        copy.start()
+    for copy in copies:
+        copy.wait()
     q_cols, k_cols = q_ref.shape[1] // n, k_ref.shape[1] // n
     piece = pieces_ref.shape[2]
     cols = shares_ref.shape[2] - 128
@@ -1003,8 +1123,6 @@
         down_ref[:, :, j * ff : (j + 1) * ff] = sums_ref[
             2 * local :, j * depth : (j + 1) * depth, :
         ].astype(F32)
-    output_ref[...] = y_ref[...]
-    input_ref[...] = grad_ref[...]
 
 
 def finish(n, k_width, depth, shares, pieces, sums, y, grad):
@@ -1015,16 +1133,19 @@
     square, narrow, expert = (
         sds((shard, width), F32), sds((shard, k_width), F32), sds((local, shard, ff), F32)
     )
-    vmem = pl.BlockSpec(memory_space=pltpu.VMEM)
+    vmem, hbm = pl.BlockSpec(memory_space=pltpu.VMEM), pl.BlockSpec(memory_space=pltpu.HBM)
     return pl.pallas_call(
         functools.partial(finish_kernel, n),
-        in_specs=[vmem] * 5,
+        in_specs=[hbm] * 5,
         out_specs=[vmem] * 10,
+        scratch_shapes=[
+            pltpu.VMEM(a.shape, BF16) for a in (shares, pieces, sums)
+        ] + [pltpu.SemaphoreType.DMA((5,))],
         out_shape=[
             square, narrow, narrow, square, sds((shard, 128), F32), expert, expert,
             sds((local, depth, width), F32), sds(y.shape, BF16), sds(y.shape, BF16),
         ],
-        compiler_params=pltpu.CompilerParams(vmem_limit_bytes=40 * 1024 * 1024),
+        compiler_params=pltpu.CompilerParams(vmem_limit_bytes=LIMIT),
         name="finish",
     )(shares, pieces, sums, y, grad)
 
@@ -1065,7 +1186,7 @@
     gap = jnp.zeros((shard, wide - 128 - used), BF16)
     packed = jnp.concatenate(
         [
-            o_weight, wq, wk, wv, gap, jnp.pad(gains, ((0, 0), (0, 6))), router,
+            wq, wk, wv, gap, jnp.pad(gains, ((0, 0), (0, 6))), router,
             jnp.zeros((shard, 120 - n * padded), BF16),
         ],
         axis=1,
@@ -1078,22 +1199,24 @@
     chips = lax.axis_size("dp") // 2
 
     cols = -(-used // 128) * 128
-    tokens_all, w_all, stacked = gather_tokens(
-        n, cols, tokens, q_weight, key_matrix, value_matrix, expert_gate, expert_up, expert_down
-    )
+    stacked = stack(expert_gate, expert_up, expert_down)
     experts_w = lax.all_gather(stacked, "dp")
+    tokens_all, w_all, w_o = gather_tokens(
+        n, cols, tokens, q_weight, key_matrix, value_matrix, o_weight
+    )
+    w_o = w_o.reshape(width, width)
     norms, q, k, v, lse, out, att, cots, small, chosen_all = attend(
         n, kv_local, tokens_all, packed, cosine, sine, starts, cotangent, chosen
     )
     w_all, att = lax.optimization_barrier((w_all, att))
     w_all = lax.all_gather(w_all, "dp").reshape(width, n * cols)
-    hidden, twos, two = mix(n, tokens, att, packed, small)
+    hidden, twos, two = mix(n, tokens, att, w_o, small)
     grad_experts, back, gg, output = experts(
         n, chosen_all, small, twos, cots, cotangent, hidden, experts_w
     )
     expert_grads = lax.psum_scatter(grad_experts, "dp", scatter_dimension=0)
     grad_hidden, ga, sums_o, extra = give_back(
-        n, chips, back, gg, chosen, small, hidden, two, cotangent, att, packed
+        n, chips, back, gg, chosen, small, hidden, two, cotangent, att, w_o
     )
     input_grad, shares, o_grad = attend_back(
         n, kv_local, (q, k, v, lse, out), ga, starts, cosine, sine, norms, w_all, tokens,

time: 505 us -> 492 us (0.974)
  local copies, waits for them, and re-layouts: 35.5 us -> 9.02 us
  Pallas kernels: 445 us -> 458 us
    unnamed x76 -> x4, local copies, waits for them, and re-layouts: 27.8 us -> 0.63 us
    pallas_call x6 -> x7, Pallas kernels: 343 us -> 365 us  [the longest x5 354 us: call(): pl.pallas_call(body, in_specs=[hbm if j in far else smem if a.dtype == jn...]
    pallas_call x1, Pallas kernels: 102 us -> 93.7 us  [experts(): pl.pallas_call(functools.partial(expert_kernel, n), grid=(4 * local,), in...]
  transfers between devices with their start and end apart: 4 -> 4, of which waited for: 1 -> 0; matrix products, arithmetic and copies ran while one was open for 0% -> 0% of each run, Pallas kernels for 89% -> 93%
where the time goes in v4:
time: 492 us; the launch traced here: 483 us
  Pallas kernels  458 us (93%)
  between operations  14.3 us (3%)
  local copies, waits for them, and re-layouts  9.02 us (2%)
    pallas_call x5, Pallas kernels, call(): pl.pallas_call(body, in_specs=[hbm if j in far else smem if a.dtype == jn...  354 us
    pallas_call x1, Pallas kernels, experts(): pl.pallas_call(functools.partial(expert_kernel, n), grid=(4 * local,), in...  93.7 us
  transfers between devices with their start and end apart: 4, of which 0 were waited for; matrix products, arithmetic and copies ran while one was open for 0% of the time, Pallas kernels for 93%

profile of v4, /device:TPU:0, one launch (start us, length us, event | category | flops | bytes accessed | tf_op | source)
XLA Modules:
  0.0 483.3 jit_solution(14473748259287777809)
XLA Ops:
  7.2 0.0 all-gather.7.cloned.1.call-start
  7.2 0.7 stack.10
  7.9 0.7 stack.11
  8.6 0.1 copy.40
  8.7 0.7 reshape.55
  9.5 0.1 copy.41
  9.6 0.9 constant_dynamic-slice_fusion.2
  10.5 0.8 constant_dynamic-slice_fusion
  11.4 0.8 concatenate.3
  12.2 0.0 all-gather.9.cloned.1.call-start
  12.3 3.6 stack.13
  15.9 0.0 all-gather.11.cloned.1.call-start
  15.9 0.6 copy-done
  16.6 0.1 fusion
  16.6 0.6 convert_bitcast_fusion.refs_6_.refs_2_
  17.3 62.0 %gather_tokens.1 = (bf16[4,256,1536]{2,1,0:T(8,128)(2,1)}, bf16[192,2560]{1,0:T(8,128)(2,1)}, bf16[8,192,1536]{2,1,0:T(8,128)(2,1)}) custom-call(bf16[256,1536]{1,0:T(8,128)(2,1)} %refs_11_.1, bf16[192,1536]{1,0:T(8,128)(2,1)} %refs_1_.1, bf16[192,512]{1,0:T(8,128)(2,1)} %refs_2_.2, bf16[192,512]{1,0:T(8,128)(2,1)} %refs_3_.2, bf16[192,1536]{1,0:T(8,128)(2,1)} %refs_4_.2), custom_call_target="tpu_custom_call" | custom-call | flops 60000002048 | bytes 2359296 | tf_op jit(solution)/shard_map/gather_tokens/pallas_call | solution.py:243
  79.3 0.0 all-gather.7.cloned.1.call-done.refs_1_
  79.3 46.3 %attend.1 = (bf16[4,256,1536]{2,1,0:T(8,128)(2,1)}, bf16[3,1024,128]{2,1,0:T(8,128)(2,1)}, bf16[1024,128]{1,0:T(8,128)(2,1)}, bf16[1024,128]{1,0:T(8,128)(2,1)},...) custom-call(bf16[4,256,1536]{2,1,0:T(8,128)(2,1)} %get-tuple-element, ...), custom_call_target="tpu_custom_call" | custom-call | flops 80000000000 | bytes 7372808 | tf_op jit(solution)/shard_map/attend/pallas_call | solution.py:243
  125.6 0.0 reduce-scatter.2.cloned.1.call-start
  125.7 64.6 %mix.1 = (f32[256,1536]{1,0:T(8,128)}, bf16[4,256,1536]{2,1,0:T(8,128)(2,1)}, bf16[256,1536]{1,0:T(8,128)(2,1)}) custom-call(bf16[256,1536]{1,0:T(8,128)(2,1)} %refs_11_.1, bf16[4,256,384]{2,1,0:T(8,128)(2,1)} %get-tuple-element.61.refs_1_.refs_7_, bf16[1536,1536]{1,0:T(8,128)(2,1)} %bitcast.20, f32[40,1536]{1,0:T(8,128)} %get-tuple-element.58.refs_3_.small_ref.refs_12_), custom_call_target="tpu_custom_call" | custom-call | flops 60000002048 | bytes 6537216 | tf_op jit(solution)/shard_map/mix/pallas_call | solution.py:243
  190.3 0.0 all-gather.9.cloned.1.call-done
  190.3 93.7 %experts.1 = (bf16[8,15,192,512]{3,2,1,0:T(8,128)(2,1)}, bf16[4,256,1536]{2,1,0:T(8,128)(2,1)}, f32[4,8,256]{2,1,0:T(8,128)}, bf16[256,1536]{1,0:T(8,128)(2,1)}) custom-call(f32[4,32,256]{2,1,0:T(8,128)} %get-tuple-element.57.chosen_ref, f32[40,1536]{1,0:T(8,128)} %get-tuple-element.58.refs_3_.small_ref.refs_12_, ...), custom_call_target="tpu_custom_call" | custom-call | flops 95000002560 | bytes 60000000 | tf_op jit(solution)/shard_map/experts/pallas_call | solution.py:1056
  284.0 74.0 %give_back.1 = (f32[256,1536]{1,0:T(8,128)}, bf16[4,256,384]{2,1,0:T(8,128)(2,1)}, bf16[4,192,1536]{2,1,0:T(8,128)(2,1)}, f32[40,1536]{1,0:T(8,128)}) custom-call(bf16[4,256,1536]{2,1,0:T(8,128)(2,1)} %get-tuple-element.66.refs_0_, f32[4,8,256]{2,1,0:T(8,128)} %get-tuple-element.67.refs_1_, f32[32,256]{1,0:T(8,128)} %convert_bitcast_fusion.refs_6_.refs_2_, ...), custom_call_target="tpu_custom_call" | custom-call | flops 80000000000 | bytes 12107776 | tf_op jit(solution)/shard_map/give_back/pallas_call | solution.py:243
  358.0 0.0 all-gather.11.cloned.1.call-done.refs_10_
  358.0 107.3 %attend_back.1 = (bf16[256,1536]{1,0:T(8,128)(2,1)}, bf16[4,192,768]{2,1,0:T(8,128)(2,1)}, bf16[4,192,384]{2,1,0:T(8,128)(2,1)}) custom-call(bf16[3,1024,128]{2,1,0:T(8,128)(2,1)} %get-tuple-element.52.refs_0_, bf16[1024,128]{1,0:T(8,128)(2,1)} %get-tuple-element.53.refs_1_, bf16[1024,128]{1,0:T(8,128)(2,1)} %get-tuple-element.54.refs_2_, ...), custom_call_target="tpu_custom_call" | custom-call | flops 89999998976 | bytes 20971528 | tf_op jit(solution)/shard_map/attend_back/pallas_call | solution.py:243
  465.3 0.0 reduce-scatter.2.cloned.1.call-done
  465.4 7.0 %finish.1 = (f32[192,1536]{1,0:T(8,128)}, f32[192,512]{1,0:T(8,128)}, f32[192,512]{1,0:T(8,128)}, f32[192,1536]{1,0:T(8,128)}, f32[192,128]{1,0:T(8,128)}, /*ind...) custom-call(bf16[4,192,768]{2,1,0:T(8,128)(2,1)} %get-tuple-element., ...), custom_call_target="tpu_custom_call" | custom-call | tf_op jit(solution)/shard_map/finish/pallas_call | solution.py:1137
  472.4 1.0 slice.14
  473.3 1.8 slice_reduce_fusion
  475.1 0.1 copy.42
  475.2 0.6 reshape.64
  475.8 0.6 convert_divide_fusion
  (12 shorter events, 0.1 us)
Async XLA Ops:
  7.2 72.1 %all-gather.7.cloned.1.call-start = ((), (), s32[]{:S(2)}) async-start(), calls=%async_computation.2 | async-start | bytes 2654208 | tf_op jit(solution)/shard_map/all_gather | solution.py:1194
  12.2 178.0 %all-gather.9.cloned.1.call-start = ((), (), s32[]{:S(2)}) async-start(), calls=%async_computation.3 | async-start | bytes 26542080 | tf_op jit(solution)/shard_map/all_gather | solution.py:1203
  15.9 0.7 copy-start
  15.9 342.1 %all-gather.11.cloned.1.call-start = ((), (), s32[]{:S(2)}) async-start(), calls=%async_computation.4 | async-start | bytes 8847360 | tf_op jit(solution)/shard_map/all_gather | solution.py:1212
  125.6 339.7 %reduce-scatter.2.cloned.1.call-start = ((), (), s32[]{:S(2)}) async-start(), calls=%async_computation.1 | async-start | bytes 26542080 | tf_op jit(solution)/shard_map/reduce_scatter | solution.py:1217
  465.3 10.4 %copy-start.1 = (bf16[192]{0:T(256)(128)(2,1)S(1)}, bf16[192]{0:T(256)(128)(2,1)}, u32[]{:S(2)}) copy-start(bf16[192]{0:T(256)(128)(2,1)} %param.17) | copy-start | bytes 1156
Sparse Core Ops, SparseCore 0:
  12.4 50.2 all-gather.6
  64.5 117.2 all-gather.8
  183.7 52.1 all-gather.10
  284.2 179.6 reduce-scatter.1

commit v5 on v4

--- a/solution.py
+++ b/solution.py
@@ -258,7 +258,10 @@
     )(*args)
 
 
-def stack_kernel(gate_ref, up_ref, down_ref, stack_ref):
+def stack_kernel(
+    n, me_ref, gate_ref, up_ref, down_ref, q_ref, k_ref, v_ref, first_ref, second_ref, router_ref,
+    stack_ref, packed_ref,
+):
     local, depth, width = down_ref.shape
     ff = gate_ref.shape[2]
     stack_ref[:local] = gate_ref[...]
@@ -267,20 +270,47 @@
         stack_ref[2 * local :, j * depth : (j + 1) * depth, :] = down_ref[
             :, :, j * ff : (j + 1) * ff
         ]
-
-
-def stack(gate, up, down):
+    shard, wide = packed_ref.shape
+    at = 0
+    for ref in (q_ref, k_ref, v_ref):
+        part = ref.shape[1] // n
+        mine = ref[:, :part]
+        for z in range(1, n):
+            mine = jnp.where(me_ref[0] == z, ref[:, z * part : (z + 1) * part], mine)
+        packed_ref[:, at : at + part] = mine
+        at += part
+    small = wide - 128
+    if at < small:
+        packed_ref[:, at:small] = jnp.zeros((shard, small - at), BF16)
+    tall = -(-shard // 128) * 128
+    gains = jnp.concatenate([first_ref[...], second_ref[...]], axis=0).astype(F32)
+    gains = jnp.concatenate([gains, jnp.zeros((2, tall - shard), F32)], axis=1)
+    gains = jnp.concatenate([gains, jnp.zeros((126, tall), F32)], axis=0)
+    packed_ref[:, small:] = gains.T[:shard, :].astype(BF16)
+    padded = -(-local // 8) * 8
+    for z in range(n):
+        lane = small + 8 + z * padded
+        packed_ref[:, lane : lane + local] = router_ref[:, z * local : (z + 1) * local]
+
+
+def stack(n, member, wide, gate, up, down, wq, wk, wv, first, second, router):
     local, shard, ff = gate.shape
     vmem = pl.BlockSpec(memory_space=pltpu.VMEM)
     return pl.pallas_call(
-        stack_kernel,
-        in_specs=[vmem] * 3,
-        out_specs=vmem,
-        out_shape=jax.ShapeDtypeStruct((3 * local, shard, ff), BF16),
+        functools.partial(stack_kernel, n),
+        in_specs=[pl.BlockSpec(memory_space=pltpu.SMEM)] + [vmem] * 9,
+        out_specs=[vmem] * 2,
+        out_shape=[
+            jax.ShapeDtypeStruct((3 * local, shard, ff), BF16),
+            jax.ShapeDtypeStruct((shard, wide), BF16),
+        ],
         compiler_params=pltpu.CompilerParams(vmem_limit_bytes=LIMIT),
-        cost_estimate=pl.CostEstimate(flops=3 * 10**9, transcendentals=0, bytes_accessed=6 * 10**6),
+        cost_estimate=pl.CostEstimate(flops=4 * 10**9, transcendentals=0, bytes_accessed=8 * 10**6),
         name="stack",
-    )(gate, up, down)
+    )(
+        member.astype(jnp.int32)[None], gate, up, down, wq, wk, wv, first[None], second[None],
+        router,
+    )
 
 
 class PlaneGather:
@@ -607,9 +637,10 @@
                 def _():
                     self.copy(way, s - 1, d, slots).wait_send()
 
-    def finish(self, total):
+    def finish(self, total, onto=False):
         n, me = self.n, self.me
-        total[...] = self.parts[me].astype(F32)
+        mine = self.parts[me].astype(F32)
+        total[...] = total[...] + mine if onto else mine
         for way in (0, 1):
             far = self.far(way)
 
@@ -720,7 +751,7 @@
     sin_ref, norm_ref, all_ref, tokens_ref, small_ref, grad_ref, extra_ref, o_ref,
     input_ref, shares_ref, og_ref,
     w_s, gq_s, gk_s, gv_s, gqkv_s, ga_s, q_send, q_got, kv_send, kv_got, load,
-    o_second, o_total, o_send, o_got, dw_s, w_first, w_sums, w_second, w_total,
+    norm_s, tokens_s, grad_s, extra_s, o_second, o_total, o_send, o_got, dw_s, w_first, w_sums, w_second, w_total,
     s0, r0, s1, r1, s2, r2, s3, r3, s4, r4, *sems,
 ):
     me = lax.axis_index("expert")
@@ -733,8 +764,17 @@
     cols = w_s.shape[1] // n
     scale = HEAD_SIZE ** (-0.5)
     pieces = starts_ref.shape[1]
-    weights = pltpu.make_async_copy(all_ref, w_s, load)
-    weights.start()
+    late = [
+        pltpu.make_async_copy(source, target, load.at[j])
+        for j, (source, target) in enumerate(
+            (
+                (all_ref, w_s), (norm_ref, norm_s), (tokens_ref, tokens_s), (grad_ref, grad_s),
+                (extra_ref, extra_s),
+            )
+        )
+    ]
+    for copy in late:
+        copy.start()
     barrier_plane(n, me, chips, place)
     o_sum = PairReduce(chips, place, None, None, o_ref, o_second, None, sems[:2])
     o_sum.spread()
@@ -801,26 +841,27 @@
         kv_send[i, :, k_cols:] = gv_s[part, :].astype(BF16)
         kv_swap.start(i)
         gqkv_s[part, q_cols : q_cols + 2 * k_cols] = kv_send[i]
-    weights.wait()
-    norms = norm_ref[...].reshape(length, width)
+    for copy in late:
+        copy.wait()
+    norms = norm_s[...].reshape(length, width)
     dw = tdot(norms, gqkv_s[...])
     own = w_s[:, pl.ds(pl.multiple_of(me * cols, 128), cols)].astype(F32)
     grad_gain = jnp.sum(dw * own, axis=1, keepdims=True)
     dw_s[:, :, :cols] = dw.astype(BF16).reshape(2 * chips, shard, cols)
-    extra = extra_ref[...]
+    extra = extra_s[...]
     extra = jnp.concatenate([extra, jnp.zeros((128 - extra.shape[0], width), F32)], axis=0).T
     lane_e = lax.broadcasted_iota(jnp.int32, extra.shape, 1)
     extra = jnp.where(lane_e == 0, grad_gain, extra)
     dw_s[:, :, cols:] = extra.astype(BF16).reshape(2 * chips, shard, 128)
     w_sum = PairReduce(chips, place, dw_s, w_first, w_sums, w_second, sems[2:4], sems[4:])
     w_sum.pair()
+    w_sum.add()
+    w_sum.spread()
     o_sum.finish(o_total)
     piece = width // n
     for d in range(n):
         o_send[d] = o_total[:, d * piece : (d + 1) * piece].astype(BF16)
         o_swap.start(d)
-    w_sum.add()
-    w_sum.spread()
     q_got[me] = q_send[me]
     kv_got[me] = kv_send[me]
     q_swap.finish()
@@ -831,8 +872,8 @@
         grad_norm = grad_norm + dot_t(
             kv_got[z], w_s[:, z * cols + q_cols : z * cols + q_cols + 2 * k_cols]
         )
-    grad, _ = rms_back(grad_norm, tokens_ref[...].astype(F32), small_ref[:1, :])
-    input_ref[...] = (grad_ref[...] + grad).astype(BF16)
+    grad, _ = rms_back(grad_norm, tokens_s[...].astype(F32), small_ref[:1, :])
+    input_ref[...] = (grad_s[...] + grad).astype(BF16)
     o_swap.finish()
     mine = o_send[me].astype(F32)
     for d in range(n):
@@ -873,7 +914,8 @@
         [
             vm(w_all.shape, BF16), vm((rows, -(-q_cols // 128) * 128), F32), vm((length, 128), F32),
             vm((length, tile), F32), vm((length, cols), BF16), vm((per_key, rows, tile), BF16),
-            q_block, q_block, kv_block, kv_block, DMA,
+            q_block, q_block, kv_block, kv_block, pltpu.SemaphoreType.DMA((5,)),
+            vm(norms.shape, BF16), vm(tokens.shape, BF16), vm(grad.shape, F32), vm(extra.shape, F32),
             vm((chips, shard, width), BF16), vm((shard, width), F32), piece, piece,
             vm((2 * chips, shard, wide), BF16), across_w, across_w, across_w,
             vm((shard, wide), F32),
@@ -883,17 +925,19 @@
         5, "attend_back", 90,
         (q, k, v, lse, out, ga, starts, cosine, sine, norms, w_all, tokens, small, grad, extra,
          sums_o),
-        (10,),
+        (9, 10, 11, 13, 14),
     )
 
 
 def expert_kernel(
-    n, chosen_ref, small_ref, n2_ref, cots_ref, cot_ref, hidden_ref, wg_ref, wu_ref, wd_ref,
-    dw_ref, gx_ref, gg_ref, output_ref,
+    n, chips, chosen_ref, small_ref, n2_ref, cots_ref, cot_ref, hidden_ref, wg_ref, wu_ref, wd_ref,
+    dw_ref, gx_ref, gg_ref, output_ref, gate_ref,
     x_s, g_s, slope_s, silu_s, act_s, gact_s, ggp_s, gup_s, pick_s, mix_s, y_s, y_slots,
-    total, gate_s, rank_s, rest_s, s0, r0, s1, r1,
+    total, gate_s, rank_s, rest_s, d_parts, d_first, d_sums, d_second, d_total, d_stage,
+    load, pair_free, across_free, s0, r0, s1, r1, *sems,
 ):
     me = lax.axis_index("expert")
+    place = lax.axis_index("dp")
     _, rows, width = n2_ref.shape
     local, tall, ff = act_s.shape
     cap = tall // n
@@ -909,6 +953,24 @@
     chain = ChainReduce(n, me, y_s, y_slots, s0, r0)
     more = ChainGather(n, me, rest_s, s1, r1)
     half = cots_ref.shape[2]
+    last = local - 1
+    skip = last - gate_ref.shape[0]
+    spread = PairReduce(chips, place, d_parts, d_first, d_sums, d_second, sems[:2], sems[2:])
+    begun = pltpu.make_async_copy(hidden_ref, total, load.at[0])
+    ended = pltpu.make_async_copy(y_s, gx_ref, load.at[1])
+
+    def gate_out(of):
+        return pltpu.make_async_copy(d_stage, gate_ref.at[of - skip], load.at[2])
+
+    def gate_done(of):
+        spread.finish(d_total)
+
+        @pl.when(of > skip)
+        def _():
+            gate_out(of - 1).wait()
+
+        d_stage[...] = d_total[...].astype(BF16)
+        gate_out(of).start()
 
     def whole(ref):
         return ref[...].reshape(width, ff)
@@ -921,7 +983,8 @@
 
     @pl.when(at == 0)
     def _():
-        barrier_all(n, me)
+        barrier_plane(n, me, chips, place)
+        begun.start()
         rest_s[me] = cot_ref[:, half:]
         more.step(0)
         before = lax.broadcasted_iota(jnp.int32, (rows, rows), 0)
@@ -1004,7 +1067,21 @@
         ggp = (grad_act * slope_s[e].astype(F32)).astype(BF16)
         ggp_s[...] = ggp
         gup_s[...] = (grad_act * silu_s[e].astype(F32)).astype(BF16)
-        dw_ref[...] = tdot(x_s[...], ggp).astype(BF16).reshape(dw_ref.shape)
+        grad = tdot(x_s[...], ggp).astype(BF16)
+
+        @pl.when((e < skip) | (e == last))
+        def _():
+            dw_ref[...] = grad.reshape(dw_ref.shape)
+
+        @pl.when((e > skip) & (e < last))
+        def _():
+            pl.semaphore_wait(pair_free, 1)
+            spread.pair_sent()
+
+        @pl.when((e >= skip) & (e < last))
+        def _():
+            d_parts[...] = grad.reshape(d_parts.shape)
+            spread.pair()
 
     @pl.when(phase == 1)
     def _():
@@ -1014,6 +1091,37 @@
         for s in range(n):
             mix_s[s, where, :] = grows[s * cap : (s + 1) * cap, :]
 
+        @pl.when(e > skip)
+        def _():
+            gate_done(e - 1)
+
+        @pl.when((e > skip) & (e < last))
+        def _():
+            for c in range(chips):
+
+                @pl.when(c != spread.chip)
+                def _():
+                    pl.semaphore_signal(
+                        across_free, inc=1, device_id={"dp": 2 * c + spread.core},
+                        device_id_type=MESH,
+                    )
+
+            pl.semaphore_wait(across_free, chips - 1)
+
+        @pl.when((e >= skip) & (e < last))
+        def _():
+            spread.add()
+
+        @pl.when((e >= skip) & (e < last - 1))
+        def _():
+            pl.semaphore_signal(
+                pair_free, inc=1, device_id={"dp": spread.partner}, device_id_type=MESH
+            )
+
+        @pl.when((e >= skip) & (e < last))
+        def _():
+            spread.spread()
+
     @pl.when(phase == 2)
     def _():
         for j in range(blocks):
@@ -1022,19 +1130,25 @@
 
     @pl.when(at == 4 * local - 1)
     def _():
+        begun.wait()
+        chain.finish(total, True)
+        output_ref[...] = total[...].astype(BF16)
         for s in range(n):
-            gx_ref[s] = tdot(pick_s[s], mix_s[s]).astype(BF16)
-        chain.finish(total)
-        output_ref[...] = (hidden_ref[...] + total[...]).astype(BF16)
-
-
-def experts(n, chosen, small, n2, cots, cot, hidden, w):
+            y_s[s] = tdot(pick_s[s], mix_s[s]).astype(BF16)
+        ended.start()
+        spread.pair_sent()
+        gate_out(last - 1).wait()
+        ended.wait()
+
+
+def experts(n, chips, chosen, small, n2, cots, cot, hidden, w):
     _, rows, width = n2.shape
     shards, local, depth, ff = w.shape
     local = local // 3
     cap = rows * TOPK * 5 // (4 * local * n)
     tall = n * cap
     padded = chosen.shape[1] // n
+    skip = min(2, local - 2)
     once = pl.Buffered(1)
 
     def const(shape):
@@ -1049,32 +1163,39 @@
 
     def grads(i):
         later = jnp.maximum(i - local, 0)
-        return (0, later % 3 * local + later // 3, 0, 0)
+        e, phase = later // 3, later % 3
+        before = jnp.where(e < skip, 2 * local + e, local + e - 1)
+        before = jnp.where(e == local - 1, 2 * local + skip, before)
+        return (0, jnp.where(phase == 1, e, jnp.where(phase == 2, local + e, before)), 0, 0)
 
     sds, vm = jax.ShapeDtypeStruct, pltpu.VMEM
+    hbm = pl.BlockSpec(memory_space=pltpu.HBM)
+    across = vm((chips, depth, ff), BF16)
     saved, half = vm((local, tall, ff), BF16), vm((tall, ff), BF16)
     return pl.pallas_call(
-        functools.partial(expert_kernel, n),
+        functools.partial(expert_kernel, n, chips),
         grid=(4 * local,),
         in_specs=[
             const(chosen.shape), const(small.shape), const(n2.shape), const(cots.shape),
-            const(cot.shape), const(hidden.shape), weight(0), weight(1), weight(2),
+            const(cot.shape), hbm, weight(0), weight(1), weight(2),
         ],
         out_specs=[
             pl.BlockSpec((shards, 1, depth, ff), grads),
-            const(n2.shape), const((n, padded, rows)), const(hidden.shape),
+            hbm, const((n, padded, rows)), const(hidden.shape), hbm,
         ],
         out_shape=[
-            sds(w.shape, BF16), sds(n2.shape, BF16), sds((n, padded, rows), F32),
-            sds(hidden.shape, BF16),
+            sds((shards, 2 * local + skip + 1, depth, ff), BF16), sds(n2.shape, BF16),
+            sds((n, padded, rows), F32), sds(hidden.shape, BF16), sds((local - 1 - skip, depth, ff), BF16),
         ],
         scratch_shapes=[
             vm((tall, width), BF16), vm((tall, width), BF16), saved, saved, saved, half, half, half,
             vm((n, local * cap, rows), BF16), vm((n, local * cap, width), BF16), vm(n2.shape, BF16),
             vm((n + 1, rows, width), BF16), vm(hidden.shape, F32), vm(chosen.shape, F32), vm(chosen.shape, jnp.int32),
-            vm((n, rows, width - cots.shape[2]), BF16),
+            vm((n, rows, width - cots.shape[2]), BF16), vm((shards, depth, ff), BF16), across, across,
+            across, vm((depth, ff), F32), vm((depth, ff), BF16), pltpu.SemaphoreType.DMA((3,)),
+            pltpu.SemaphoreType.REGULAR, pltpu.SemaphoreType.REGULAR,
         ]
-        + chain_sems(n) + chain_sems(n),
+        + chain_sems(n) + chain_sems(n) + direct_sems(chips) + direct_sems(chips),
         compiler_params=pltpu.CompilerParams(
             collective_id=6, has_side_effects=True, vmem_limit_bytes=LIMIT,
             dimension_semantics=("arbitrary",),
@@ -1087,14 +1208,14 @@
 
 
 def finish_kernel(
-    n, shares_far, pieces_far, sums_far, y_far, grad_far, q_ref, k_ref, v_ref, o_ref, small_ref,
-    gate_ref, up_ref, down_ref, output_ref, input_ref, shares_ref, pieces_ref, sums_ref, sems,
+    n, shares_far, pieces_far, gates_far, sums_far, y_far, grad_far, q_ref, k_ref, v_ref, o_ref, gains_ref,
+    router_ref, gate_ref, up_ref, down_ref, output_ref, input_ref, shares_ref, pieces_ref, gates_ref, sums_ref, sems,
 ):
     copies = [
         pltpu.make_async_copy(source, target, sems.at[j])
         for j, (source, target) in enumerate(
             (
-                (shares_far, shares_ref), (pieces_far, pieces_ref), (sums_far, sums_ref),
+                (shares_far, shares_ref), (pieces_far, pieces_ref), (gates_far, gates_ref), (sums_far, sums_ref),
                 (y_far, output_ref), (grad_far, input_ref),
             )
         )
@@ -1106,7 +1227,8 @@
     q_cols, k_cols = q_ref.shape[1] // n, k_ref.shape[1] // n
     piece = pieces_ref.shape[2]
     cols = shares_ref.shape[2] - 128
-    small = jnp.zeros(small_ref.shape, F32)
+    shard = q_ref.shape[0]
+    small = jnp.zeros((shard, 128), F32)
     for z in range(n):
         at = 0
         for ref, part in ((q_ref, q_cols), (k_ref, k_cols), (v_ref, k_cols)):
@@ -1114,21 +1236,30 @@
             at += part
         small = small + shares_ref[z, :, cols:].astype(F32)
         o_ref[:, z * piece : (z + 1) * piece] = pieces_ref[z].astype(F32)
-    small_ref[...] = small
     local, depth, _ = down_ref.shape
+    padded = -(-local // 8) * 8
+    for z in range(n):
+        router_ref[:, z * local : (z + 1) * local] = small[
+            :, 8 + z * padded : 8 + z * padded + local
+        ]
+    gap = -(-shard // 128) * 128 - shard
+    gains_ref[...] = jnp.concatenate([small, jnp.zeros((gap, 128), F32)], axis=0).T[:8, :shard]
     ff = gate_ref.shape[2]
-    gate_ref[...] = sums_ref[:local].astype(F32)
-    up_ref[...] = sums_ref[local : 2 * local].astype(F32)
+    skip = local - 1 - gates_ref.shape[0]
+    gate_ref[:skip] = sums_ref[2 * local : 2 * local + skip].astype(F32)
+    gate_ref[skip : local - 1] = gates_ref[...].astype(F32)
+    gate_ref[local - 1] = sums_ref[2 * local + skip].astype(F32)
+    up_ref[...] = sums_ref[:local].astype(F32)
     for j in range(down_ref.shape[2] // ff):
         down_ref[:, :, j * ff : (j + 1) * ff] = sums_ref[
-            2 * local :, j * depth : (j + 1) * depth, :
+            local : 2 * local, j * depth : (j + 1) * depth, :
         ].astype(F32)
 
 
-def finish(n, k_width, depth, shares, pieces, sums, y, grad):
+def finish(n, k_width, depth, shares, pieces, gates, sums, y, grad):
     _, shard, _ = shares.shape
     width = y.shape[1]
-    local, ff = sums.shape[0] // 3, sums.shape[2]
+    local, ff = (sums.shape[0] + gates.shape[0]) // 3, sums.shape[2]
     sds = jax.ShapeDtypeStruct
     square, narrow, expert = (
         sds((shard, width), F32), sds((shard, k_width), F32), sds((local, shard, ff), F32)
@@ -1136,18 +1267,19 @@
     vmem, hbm = pl.BlockSpec(memory_space=pltpu.VMEM), pl.BlockSpec(memory_space=pltpu.HBM)
     return pl.pallas_call(
         functools.partial(finish_kernel, n),
-        in_specs=[hbm] * 5,
-        out_specs=[vmem] * 10,
+        in_specs=[hbm] * 6,
+        out_specs=[vmem] * 11,
         scratch_shapes=[
-            pltpu.VMEM(a.shape, BF16) for a in (shares, pieces, sums)
-        ] + [pltpu.SemaphoreType.DMA((5,))],
+            pltpu.VMEM(a.shape, BF16) for a in (shares, pieces, gates, sums)
+        ] + [pltpu.SemaphoreType.DMA((6,))],
         out_shape=[
-            square, narrow, narrow, square, sds((shard, 128), F32), expert, expert,
+            square, narrow, narrow, square, sds((8, shard), F32), sds((shard, n * local), F32),
+            expert, expert,
             sds((local, depth, width), F32), sds(y.shape, BF16), sds(y.shape, BF16),
         ],
         compiler_params=pltpu.CompilerParams(vmem_limit_bytes=LIMIT),
         name="finish",
-    )(shares, pieces, sums, y, grad)
+    )(shares, pieces, gates, sums, y, grad)
 
 
 def rotary_tables(length):
@@ -1174,24 +1306,15 @@
     local, shard, _ = expert_gate.shape
     padded = -(-local // 8) * 8
 
-    wq = lax.dynamic_slice_in_dim(q_weight, member * q_cols, q_cols, 1)
-    wk = lax.dynamic_slice_in_dim(key_matrix, member * k_cols, k_cols, 1)
-    wv = lax.dynamic_slice_in_dim(value_matrix, member * k_cols, k_cols, 1)
     wide = width // 2
     used = q_cols + 2 * k_cols
-    router = jnp.pad(
-        router_weight.reshape(shard, n, local), ((0, 0), (0, 0), (0, padded - local))
-    ).reshape(shard, n * padded)
-    gains = jnp.stack([attn_gain, ffn_gain], axis=1)
-    gap = jnp.zeros((shard, wide - 128 - used), BF16)
-    packed = jnp.concatenate(
-        [
-            wq, wk, wv, gap, jnp.pad(gains, ((0, 0), (0, 6))), router,
-            jnp.zeros((shard, 120 - n * padded), BF16),
-        ],
-        axis=1,
+    stacked, packed = stack(
+        n, member, wide, expert_gate, expert_up, expert_down, q_weight, key_matrix, value_matrix,
+        attn_gain, ffn_gain, router_weight,
     )
     packed = lax.all_gather(packed, "dp").reshape(width, -1)
+    experts_w = lax.all_gather(stacked, "dp")
+
     hot = routes[:, :, None] == jnp.arange(n * local, dtype=jnp.int32)
     chosen = jnp.any(hot, axis=1).astype(F32).T.reshape(n, local, rows)
     chosen = jnp.pad(chosen, ((0, 0), (0, padded - local), (0, 0))).reshape(n * padded, rows)
@@ -1199,8 +1322,6 @@
     chips = lax.axis_size("dp") // 2
 
     cols = -(-used // 128) * 128
-    stacked = stack(expert_gate, expert_up, expert_down)
-    experts_w = lax.all_gather(stacked, "dp")
     tokens_all, w_all, w_o = gather_tokens(
         n, cols, tokens, q_weight, key_matrix, value_matrix, o_weight
     )
@@ -1211,8 +1332,8 @@
     w_all, att = lax.optimization_barrier((w_all, att))
     w_all = lax.all_gather(w_all, "dp").reshape(width, n * cols)
     hidden, twos, two = mix(n, tokens, att, w_o, small)
-    grad_experts, back, gg, output = experts(
-        n, chosen_all, small, twos, cots, cotangent, hidden, experts_w
+    grad_experts, back, gg, output, gate_sums = experts(
+        n, chips, chosen_all, small, twos, cots, cotangent, hidden, experts_w
     )
     expert_grads = lax.psum_scatter(grad_experts, "dp", scatter_dimension=0)
     grad_hidden, ga, sums_o, extra = give_back(
@@ -1222,13 +1343,16 @@
         n, kv_local, (q, k, v, lse, out), ga, starts, cosine, sine, norms, w_all, tokens,
         small, grad_hidden, extra, sums_o,
     )
-    q_grad, k_grad, v_grad, o_grad, rest, gate_grad, up_grad, down_grad, output, input_grad = finish(
-        n, key_matrix.shape[1], expert_down.shape[1], shares, o_grad, expert_grads, output, input_grad
-    )
-    router_grad = rest[:, 8 : 8 + n * padded].reshape(shard, n, padded)[:, :, :local]
+    (
+        q_grad, k_grad, v_grad, o_grad, gains, router_grad, gate_grad, up_grad, down_grad, output,
+        input_grad,
+    ) = finish(
+        n, key_matrix.shape[1], expert_down.shape[1], shares, o_grad, gate_sums, expert_grads, output,
+        input_grad,
+    )
     return (
-        output, input_grad, rest[:, 0] / attn_gain.astype(F32), q_grad, k_grad, v_grad, o_grad,
-        rest[:, 1], router_grad.reshape(shard, n * local), gate_grad, up_grad, down_grad,
+        output, input_grad, gains[0] / attn_gain.astype(F32), q_grad, k_grad, v_grad, o_grad,
+        gains[1], router_grad, gate_grad, up_grad, down_grad,
     )
 
 

time: 492 us -> 484 us (0.984)
  Pallas kernels: 458 us -> 453 us
    pallas_call x5, Pallas kernels: 354 us -> 340 us  [call(): pl.pallas_call(body, in_specs=[hbm if j in far else smem if a.dtype == jn...]
    pallas_call x3, Pallas kernels: 104 us -> 113 us  [the longest x1 102 us: experts(): pl.pallas_call(functools.partial(expert_kernel, n, chips), grid=(4 * loca...]
where the time goes in v5:
time: 484 us; the launch traced here: 476 us
  Pallas kernels  453 us (94%)
  between operations  14.3 us (3%)
  local copies, waits for them, and re-layouts  6.82 us (1%)
    pallas_call x5, Pallas kernels, call(): pl.pallas_call(body, in_specs=[hbm if j in far else smem if a.dtype == jn...  340 us
    pallas_call x1, Pallas kernels, experts(): pl.pallas_call(functools.partial(expert_kernel, n, chips), grid=(4 * loca...  102 us
  transfers between devices with their start and end apart: 4, of which 0 were waited for; matrix products, arithmetic and copies ran while one was open for 0% of the time, Pallas kernels for 93%

profile of v5, /device:TPU:0, one launch (start us, length us, event | category | flops | bytes accessed | tf_op | source)
XLA Modules:
  0.0 475.9 jit_solution(18433435846095548323)
XLA Ops:
  7.2 0.0 all-gather.7.cloned.1.call-start
  7.2 1.4 copy.37.router_ref
  8.7 1.2 broadcast_in_dim.12.first_ref
  9.9 1.2 broadcast_in_dim.13.second_ref
  11.1 4.1 stack.1
  15.2 0.0 copy-start
  15.2 0.0 all-gather.7.cloned.1.call-update
  15.2 0.0 all-gather.9.cloned.1.call-start
  15.2 0.7 all-gather.9.cloned.1.call-update
  16.0 0.0 all-gather.11.cloned.1.call-start
  16.0 0.0 copy-done
  16.0 0.1 fusion
  16.1 0.6 convert_bitcast_fusion.refs_6_.refs_2_
  16.7 62.1 %gather_tokens.1 = (bf16[4,256,1536]{2,1,0:T(8,128)(2,1)}, bf16[192,2560]{1,0:T(8,128)(2,1)}, bf16[8,192,1536]{2,1,0:T(8,128)(2,1)}) custom-call(bf16[256,1536]{1,0:T(8,128)(2,1)} %refs_11_.1, bf16[192,1536]{1,0:T(8,128)(2,1)} %q_ref.1, bf16[192,512]{1,0:T(8,128)(2,1)} %k_ref.1, bf16[192,512]{1,0:T(8,128)(2,1)} %v_ref.1, bf16[192,1536]{1,0:T(8,128)(2,1)} %refs_4_.2), custom_call_target="tpu_custom_call" | custom-call | flops 60000002048 | bytes 2359296 | tf_op jit(solution)/shard_map/gather_tokens/pallas_call | solution.py:243
  78.8 0.0 all-gather.7.cloned.1.call-done.refs_1_
  78.8 46.3 %attend.1 = (bf16[4,256,1536]{2,1,0:T(8,128)(2,1)}, bf16[3,1024,128]{2,1,0:T(8,128)(2,1)}, bf16[1024,128]{1,0:T(8,128)(2,1)}, bf16[1024,128]{1,0:T(8,128)(2,1)},...) custom-call(bf16[4,256,1536]{2,1,0:T(8,128)(2,1)} %get-tuple-element, ...), custom_call_target="tpu_custom_call" | custom-call | flops 80000000000 | bytes 7372808 | tf_op jit(solution)/shard_map/attend/pallas_call | solution.py:243
  125.2 0.0 all-gather.11.cloned.1.call-update
  125.2 0.0 reduce-scatter.2.cloned.1.call-start
  125.2 64.5 %mix.1 = (f32[256,1536]{1,0:T(8,128)}, bf16[4,256,1536]{2,1,0:T(8,128)(2,1)}, bf16[256,1536]{1,0:T(8,128)(2,1)}) custom-call(bf16[256,1536]{1,0:T(8,128)(2,1)} %refs_11_.1, bf16[4,256,384]{2,1,0:T(8,128)(2,1)} %get-tuple-element.66.refs_1_.refs_7_, bf16[1536,1536]{1,0:T(8,128)(2,1)} %bitcast.16, f32[40,1536]{1,0:T(8,128)} %get-tuple-element.63.refs_3_.small_ref.refs_12_), custom_call_target="tpu_custom_call" | custom-call | flops 60000002048 | bytes 6537216 | tf_op jit(solution)/shard_map/mix/pallas_call | solution.py:243
  189.7 0.0 all-gather.9.cloned.1.call-done
  189.7 101.6 %experts.1 = (bf16[8,13,192,512]{3,2,1,0:T(8,128)(2,1)}, bf16[4,256,1536]{2,1,0:T(8,128)(2,1)}, f32[4,8,256]{2,1,0:T(8,128)}, bf16[256,1536]{1,0:T(8,128)(2,1)}, bf16[2,192,512]{2,1,0:T(8,128)(2,1)}) custom-call(f32[4,32,256]{2,1,0:T(8,128)} %get-tuple-element.62.chosen_ref, f32[40,1536]{1,0:T(8,128)} %get-tuple-element.63.refs_3_.small_ref.refs_12_, ...), custom_call_target="tpu_custom_call" | custom-call | flops 95000002560 | bytes 60000000 | tf_op jit(solution)/shard_map/experts/pallas_call | solution.py:1175
  291.3 0.0 reduce-scatter.2.cloned.1.call-update
  291.4 72.6 %give_back.1 = (f32[256,1536]{1,0:T(8,128)}, bf16[4,256,384]{2,1,0:T(8,128)(2,1)}, bf16[4,192,1536]{2,1,0:T(8,128)(2,1)}, f32[40,1536]{1,0:T(8,128)}) custom-call(bf16[4,256,1536]{2,1,0:T(8,128)(2,1)} %get-tuple-element.72.refs_0_, f32[4,8,256]{2,1,0:T(8,128)} %get-tuple-element.73.refs_1_, f32[32,256]{1,0:T(8,128)} %convert_bitcast_fusion.refs_6_.refs_2_, ...), custom_call_target="tpu_custom_call" | custom-call | flops 80000000000 | bytes 12107776 | tf_op jit(solution)/shard_map/give_back/pallas_call | solution.py:243
  363.9 0.0 all-gather.11.cloned.1.call-done.refs_10_
  364.0 94.6 %attend_back.1 = (bf16[256,1536]{1,0:T(8,128)(2,1)}, bf16[4,192,768]{2,1,0:T(8,128)(2,1)}, bf16[4,192,384]{2,1,0:T(8,128)(2,1)}) custom-call(bf16[3,1024,128]{2,1,0:T(8,128)(2,1)} %get-tuple-element.57.refs_0_, bf16[1024,128]{1,0:T(8,128)(2,1)} %get-tuple-element.58.refs_1_, bf16[1024,128]{1,0:T(8,128)(2,1)} %get-tuple-element.59.refs_2_, ...), custom_call_target="tpu_custom_call" | custom-call | flops 89999998976 | bytes 20971528 | tf_op jit(solution)/shard_map/attend_back/pallas_call | solution.py:243
  458.5 0.0 reduce-scatter.2.cloned.1.call-done
  458.6 0.0 copy-start.1
  458.6 6.9 %finish.1 = (f32[192,1536]{1,0:T(8,128)}, f32[192,512]{1,0:T(8,128)}, f32[192,512]{1,0:T(8,128)}, f32[192,1536]{1,0:T(8,128)}, f32[8,192]{1,0:T(8,128)}, /*index...) custom-call(bf16[4,192,768]{2,1,0:T(8,128)(2,1)} %get-tuple-element., ...), custom_call_target="tpu_custom_call" | custom-call | tf_op jit(solution)/shard_map/finish/pallas_call | solution.py:1268
  465.5 1.6 copy.38
  467.1 1.3 fusion.1
  468.4 0.0 copy-done.1
  468.4 0.6 convert_divide_fusion
  (1 shorter events, 0.0 us)
Async XLA Ops:
  7.2 71.7 %all-gather.7.cloned.1.call-start = ((), (), s32[]{:S(2)}) async-start(), calls=%async_computation.2 | async-start | bytes 2654208 | tf_op jit(solution)/shard_map/all_gather | solution.py:1315
  15.2 0.8 copy-start
  15.2 174.5 %all-gather.9.cloned.1.call-start = ((), (), s32[]{:S(2)}) async-start(), calls=%async_computation.3 | async-start | bytes 26542080 | tf_op jit(solution)/shard_map/all_gather | solution.py:1316
  16.0 348.0 %all-gather.11.cloned.1.call-start = ((), (), s32[]{:S(2)}) async-start(), calls=%async_computation.4 | async-start | bytes 8847360 | tf_op jit(solution)/shard_map/all_gather | solution.py:1333
  125.2 333.4 %reduce-scatter.2.cloned.1.call-start = ((), (), s32[]{:S(2)}) async-start(), calls=%async_computation.1 | async-start | bytes 23003136 | tf_op jit(solution)/shard_map/reduce_scatter | solution.py:1338
  458.6 9.8 %copy-start.1 = (bf16[192]{0:T(256)(128)(2,1)S(1)}, bf16[192]{0:T(256)(128)(2,1)}, u32[]{:S(2)}) copy-start(bf16[192]{0:T(256)(128)(2,1)} %param.17) | copy-start | bytes 1156
Sparse Core Ops, SparseCore 0:
  15.3 46.7 all-gather.6
  64.0 117.2 all-gather.8
  183.2 52.1 all-gather.10
  291.5 162.1 reduce-scatter.1
